TPU v7x, 32 devices: a whole 2x2x4 slice. The times are simulated.
32 devices in a mesh: grp: 4 (over y, x), mem: 8 (over z, core).
Axes of the slice: x: 2, y: 2, z: 4, core: 2. Of those that a mesh axis runs over, the one named last changes fastest.
Arguments:
- factors: bfloat16 [32, 512, 2048], P(('grp', 'mem')), may hold values from -1 to 1
- occ_energy: bfloat16 [32], P(('grp', 'mem')), may hold values from -1.5 to -0.29882812
- vir_energy: bfloat16 [512], replicated, may hold values from 0.3984375 to 3
- pair_code: int32 [4, 8, 3], P('grp'), may hold values from 0 to 2
- pair_count: int32 [4, 8], P('grp'), may hold values from 1 to 3
Outputs:
- aux_density: bfloat16 [32, 512, 2048], P(('grp', 'mem'))
- lagrangian: bfloat16 [32, 512, 2048], P(('grp', 'mem'))
Inputs may be any that keep to these rules, and one draw needn't show every extreme that they name: `pair_code`: only the first pair_count entries of a device's list are read; entries may repeat.
All inputs are finite; a program needn't handle non-finite values.
Results may differ from a plain program's by a relative error of at most 0.0056.
Values may be sent and summed in bfloat16 or wider, within the bound.
No kernel may reach another device: no remote copies, remote signals or barrier semaphores. Data moves between devices by JAX's collectives and lax.ppermute only.
A program may use at most 128 MiB of HBM per device.

v0:
```python
import functools

import jax
import jax.numpy as jnp
from jax import lax
from jax.experimental import pallas as pl
from jax.experimental.pallas import tpu as pltpu
from jax.sharding import PartitionSpec as P


STRIPS = 4
TILE = 128
F32 = jnp.float32
BF16 = jnp.bfloat16

VMEM = pl.BlockSpec(memory_space=pltpu.VMEM)
SMEM = pl.BlockSpec(memory_space=pltpu.SMEM)


def leads(member):
    return (member & 1) == ((member >> 1) & 1)


def first_round(member):
    return jnp.where(leads(member), 2, 1)


def turn(value, back):
    pairs = []
    for member in range(lax.axis_size("mem")):
        target = member ^ (1 if leads(member) else 2)
        pairs.append((target, member) if back else (member, target))
    return lax.ppermute(value, "mem", pairs)


def swap(value, masks):
    groups, members = lax.axis_size("grp"), lax.axis_size("mem")
    pairs = []
    for g in range(groups):
        for m in range(members):
            grp_mask, mem_mask = masks[0] if leads(m) else masks[1]
            pairs.append((g * members + m, (g ^ grp_mask) * members + (m ^ mem_mask)))
    return lax.ppermute(value, ("grp", "mem"), pairs)


def live(codes, counts, member, round_no):
    total = jnp.int32(0)
    for slot in range(codes.shape[0]):
        hit = (slot < counts[0, member]) & (codes[slot, 0, member] == round_no)
        total = total + hit.astype(jnp.int32)
    return total


def weights(codes, counts, round_no):
    me = lax.axis_index("mem")
    other = jnp.where(round_no == 0, me, me ^ round_no)
    own = live(codes, counts, me, round_no)
    far = live(codes, counts, other, round_no)
    return own.astype(F32), far.astype(F32)


def nt(a, b):
    return lax.dot_general(a, b, (((1,), (1,)), ((), ())), preferred_element_type=F32)


def nn(a, b):
    return jnp.dot(a, b, preferred_element_type=F32)


def early_kernel(
    split, b_ref, row_ref, e_ref, first_ref, second_ref, codes, counts,
    one_ref, two_ref, dens_ref, gamma_ref, upper_ref, amp
):
    vir, aux = b_ref.shape
    mask = jnp.where(leads(lax.axis_index("mem")), split[0][0], split[1][0])
    upper_ref[...] = jnp.full(upper_ref.shape, ((lax.axis_index("grp") & mask) != 0).astype(F32))
    row = row_ref[...]
    sums = jnp.broadcast_to(row, (vir, vir)).T + row - e_ref[0]
    one_ref[...] = 1.0 / (sums - first_ref[0])
    two_ref[...] = 1.0 / (sums - second_ref[0])
    own, _ = weights(codes, counts, 0)
    half = vir // 2
    for at in (slice(0, half), slice(half, vir)):
        k = nt(b_ref[...], b_ref[at, :])
        amp[:, at] = (k / (sums[:, at] - e_ref[0])).astype(BF16)
    a = amp[...]
    dens_ref[...] = own * nn(a, a)
    for p in range(STRIPS):
        at = pl.ds(p * (aux // STRIPS), aux // STRIPS)
        gamma_ref[:, at] = (2.0 * own) * nn(a, b_ref[:, at])


def amp_part(at, b_ref, r_ref, over_ref):
    return (nt(b_ref[...], r_ref[...]) * over_ref[:, at]).astype(BF16)


def blocks(size):
    count = size // TILE
    return [(i, j) for i in range(count) for j in range(i, count)]


def density_kernel(b_ref, r_ref, over_ref, codes, counts, dens_in, mt_ref, keep_ref, send_ref, m_ref):
    vir = b_ref.shape[0]
    half = vir // 2
    me = lax.axis_index("mem")
    own, far = weights(codes, counts, first_round(me))
    for at in (slice(0, half), slice(half, vir)):
        mt = amp_part(at, b_ref, r_ref.at[at, :], over_ref)
        mt_ref[:, at] = mt
        m_ref[at, :] = mt.T
    high, low = slice(0, half), slice(half, vir)

    def sums(rows, columns):
        one = nn(mt_ref[rows, :], m_ref[:, columns])
        two = nn(m_ref[rows, :], mt_ref[:, columns])
        return dens_in[rows, columns] + own * one + far * two

    top, rest = sums(high, slice(0, vir)), sums(low, low)
    pieces = []
    for i, j in blocks(vir):
        if i * TILE < half:
            pieces.append(top[i * TILE : (i + 1) * TILE, j * TILE : (j + 1) * TILE])
        else:
            a, b = i * TILE - half, j * TILE - half
            pieces.append(rest[a : a + TILE, b : b + TILE])
    lead = leads(me)
    count = len(pieces) // 2
    for n in range(count):
        at = pl.ds(n * TILE, TILE)
        keep_ref[at, :] = jnp.where(lead, pieces[n], pieces[n + count])
        send_ref[at, :] = jnp.where(lead, pieces[n + count], pieces[n]).astype(BF16)


def first_gamma_kernel(codes, counts, gamma_in, mt_ref, r_ref, gamma_ref):
    own, far = weights(codes, counts, first_round(lax.axis_index("mem")))
    aux = gamma_ref.shape[1]
    for p in range(STRIPS):
        at = pl.ds(p * (aux // STRIPS), aux // STRIPS)
        gamma_ref[:, at] = gamma_in[:, at] + (own + far) * nn(mt_ref[...], r_ref[:, at])


def strips_out(out_ref, held, sems, strips, compute):
    step = held.shape[1] // strips
    copies = []
    for p in range(strips):
        at = pl.ds(p * step, step)
        held[:, at] = compute(at).astype(held.dtype)
        copies.append(pltpu.make_async_copy(held.at[:, at], out_ref.at[:, at], sems.at[p]))
        copies[-1].start()
    for copy in copies:
        copy.wait()


def joined(parts, held):
    start = 0
    for part in parts:
        held[start : start + part.shape[0], :] = part[...]
        start += part.shape[0]


def flat_amp(at, b_ref, r_ref, over_ref, m_ref):
    m_ref[...] = (nt(r_ref[...], b_ref[...]) * over_ref[at, :]).astype(BF16)
    return m_ref[...].T


def second_gamma_kernel(codes, counts, b_ref, over_ref, gamma_in, r_ref, gamma_ref, mt_ref, m_ref):
    own, far = weights(codes, counts, 3 - first_round(lax.axis_index("mem")))
    mt_ref[...] = flat_amp(slice(0, r_ref.shape[0]), b_ref, r_ref, over_ref, m_ref)
    aux = gamma_ref.shape[1]
    for p in range(STRIPS):
        at = pl.ds(p * (aux // STRIPS), aux // STRIPS)
        gamma_ref[:, at] = gamma_in[:, at] + (own + far) * nn(mt_ref[...], r_ref[:, at])


def last_gamma_kernel(codes, counts, b_ref, over_ref, gamma_in, *refs):
    parts, (out_ref, held, sems, r_ref, mt_ref, m_ref) = refs[:-6], refs[-6:]
    own, far = weights(codes, counts, 3 - first_round(lax.axis_index("mem")))
    joined(parts, r_ref)
    vir = b_ref.shape[0]
    mt_ref[...] = flat_amp(slice(vir - r_ref.shape[0], vir), b_ref, r_ref, over_ref, m_ref)
    strips_out(
        out_ref, held, sems, STRIPS, lambda at: gamma_in[:, at] + (own + far) * nn(mt_ref[...], r_ref[:, at])
    )


def apply_kernel(mine_ref, other_ref, b_ref, out_ref, tile, held, sems):
    lead = leads(lax.axis_index("mem"))
    names = blocks(tile.shape[0])
    half = len(names) // 2
    for n, (i, j) in enumerate(names):
        at = pl.ds((n % half) * TILE, TILE)
        low, high = (mine_ref, other_ref) if n < half else (other_ref, mine_ref)
        block = jnp.where(lead, low[at, :].astype(F32), high[at, :].astype(F32)).astype(BF16)
        tile[pl.ds(i * TILE, TILE), pl.ds(j * TILE, TILE)] = block
        if i != j:
            tile[pl.ds(j * TILE, TILE), pl.ds(i * TILE, TILE)] = block.T
    strips_out(out_ref, held, sems, STRIPS, lambda at: nn(tile[...], b_ref[:, at]))


def call(kernel, outs, scratch=(), smem=(), count=0, flops=0, out_spec=VMEM):
    return lambda *args: kernel_call(kernel, outs, scratch, smem, count, flops, out_spec)(*args)


def kernel_call(kernel, outs, scratch, smem, count, flops, out_spec):
    return pl.pallas_call(
        kernel,
        out_shape=outs,
        in_specs=[SMEM if i in smem else VMEM for i in range(count)],
        out_specs=jax.tree.map(lambda _: out_spec, outs),
        scratch_shapes=scratch,
        compiler_params=pltpu.CompilerParams(vmem_limit_bytes=12 << 20),
        cost_estimate=pl.CostEstimate(flops=flops, bytes_accessed=1 << 20, transcendentals=0),
    )


def per_device(factors, occ_energy, vir_energy, pair_code, pair_count):
    return body(factors[0], occ_energy, vir_energy, pair_code, pair_count)


def body(block, occ_energy, vir_energy, pair_code, pair_count):
    vir, aux = block.shape
    members, groups = lax.axis_size("mem"), lax.axis_size("grp")
    shape = jax.ShapeDtypeStruct
    square = shape((vir, vir), F32)
    wide = shape((vir, aux), F32)
    dot = 2 * vir * vir * aux
    out_scratch = [pltpu.VMEM((vir, aux), BF16), pltpu.SemaphoreType.DMA((STRIPS,))]
    any_space = pl.BlockSpec(memory_space=pl.ANY)

    first_energy = turn(occ_energy, False).astype(F32)
    first = turn(block, False)
    second_energy = turn(occ_energy, True).astype(F32)

    pair_code = jnp.transpose(pair_code, (2, 0, 1))
    energy = occ_energy.astype(F32)
    row = vir_energy.astype(F32).reshape(1, vir)
    half = len(blocks(vir)) * TILE // 2
    along = [(0, 3)] + [(0, (1 << k) | 3) for k in range(2, members.bit_length() - 1)]
    across = [(1 << k, 0) for k in range(groups.bit_length() - 1)]
    split, *later = zip(across, across[1:] + across[:1])
    over_first, over_second, dens, gamma, upper = call(
        functools.partial(early_kernel, split),
        (square, square, square, wide, shape((half // 2, TILE), F32)), [pltpu.VMEM((vir, vir), BF16)],
        (2, 3, 4, 5, 6), 7, 2 * dot,
    )(block, row, energy, first_energy, second_energy, pair_code, pair_count)

    mt, keep, send = call(
        density_kernel,
        (shape((vir, vir), BF16), shape((half, TILE), F32), shape((half, TILE), BF16)),
        [pltpu.VMEM((vir, vir), BF16)], (3, 4), 6, dot,
    )(block, first, over_first, pair_code, pair_count, dens)

    total = keep + swap(send, [(0, 1), (0, 1)]).astype(F32)
    upper = upper > 0.5
    below, above = total[: half // 2], total[half // 2 :]
    got = swap(jnp.where(upper, below, above).astype(BF16), split)
    total = jnp.where(upper, above, below) + got.astype(F32)
    for masks in later:
        total = total + swap(total.astype(BF16), masks).astype(F32)
    for mask in along:
        total = total + swap(total.astype(BF16), [mask, mask]).astype(F32)
    mine = (total * (1.0 / (8.0 * groups * members))).astype(BF16)
    got = swap(mine, split)
    mine = jnp.concatenate([jnp.where(upper, got, mine), jnp.where(upper, mine, got)])
    other = swap(mine, [(0, 1), (0, 1)])

    unit = vir // 16
    cuts = (0, 8 * unit, 10 * unit, 13 * unit, vir)
    parts = [block[a:b] for a, b in zip(cuts, cuts[1:])]
    second = [turn(part, True) for part in parts]
    gamma = call(first_gamma_kernel, wide, (), (0, 1), 5, dot)(
        pair_code, pair_count, gamma, mt, first
    )
    bounce = [pltpu.VMEM((vir, vir // 2), BF16), pltpu.VMEM((vir // 2, vir), BF16)]
    gamma = call(second_gamma_kernel, wide, bounce, (0, 1), 6, dot)(
        pair_code, pair_count, block, over_second, gamma, second[0]
    )
    result = call(
        last_gamma_kernel, shape((vir, aux), BF16), [*out_scratch, pltpu.VMEM((vir // 2, aux), BF16), *bounce],
        (0, 1), 8, dot, any_space,
    )(pair_code, pair_count, block, over_second, gamma, *second[1:])
    lagrangian = call(
        apply_kernel, shape((vir, aux), BF16), [pltpu.VMEM((vir, vir), BF16), *out_scratch], (), 3, dot,
        any_space,
    )(mine, other, block)
    return (result[None], lagrangian[None])


def solution(mesh):
    in_specs = (
        P(("grp", "mem"), None, None),
        P(("grp", "mem")),
        P(),
        P("grp", None, None),
        P("grp", None),
    )
    out_specs = (P(("grp", "mem"), None, None), P(("grp", "mem"), None, None))
    return jax.shard_map(
        per_device, mesh=mesh, in_specs=in_specs, out_specs=out_specs, check_vma=False
    )
```

profile of v0, /device:TPU:0, one launch (start us, length us, event | category | flops | bytes accessed | tf_op | source)
XLA Modules:
  0.0 81.0 jit_solution(17184250432520261365)
XLA Ops:
  0.6 0.6 collective-permute-start.2
  1.2 2.1 %collective-permute-start = (bf16[1]{0:T(256)(128)(2,1)}, bf16[1]{0:T(256)(128)(2,1)}, u32[]{:S(2)}, u32[]{:S(2)}) collective-permute-start(bf16[1]{0:T(256)(128)(2,1)} %param.6), channel_id=1, source_target_pairs={{0,1},{1,3},{2,0},{3,2},{4,5},{5,7},{6,4},{7,6},{8,9},{9,11},{10,8... | collective-permute-start | bytes 14 | tf_op jit(solution)/shard_map/ppermute | solution.py:33
  3.3 0.6 collective-permute-start.1
  4.6 0.7 reshape.15
  5.3 22.7 %collective-permute-done = bf16[1]{0:T(256)(128)(2,1)} collective-permute-done((bf16[1]{0:T(256)(128)(2,1)}, bf16[1]{0:T(256)(128)(2,1)}, u32[]{:S(2)}, u32[]{:S(2)}) %collective-permute-start) | collective-permute-done | bytes 34 | tf_op jit(solution)/shard_map/ppermute | solution.py:33
  28.7 0.0 collective-permute-done.1
  29.3 0.0 copy-start
  29.3 1.6 %copy-done = bf16[1,512,2048]{2,1,0:T(8,128)(2,1)S(1)} copy-done((bf16[1,512,2048]{2,1,0:T(8,128)(2,1)S(1)}, bf16[1,512,2048]{2,1,0:T(8,128)(2,1)}, u32[]{:S(2)}) %copy-start) | copy-done | bytes 2097176
  30.9 0.7 copy-done.2
  31.6 0.7 copy-done.4
  32.2 3.4 %shard_map.68 = (f32[512,512]{1,0:T(8,128)S(1)}, f32[512,512]{1,0:T(8,128)S(1)}, f32[512,512]{1,0:T(8,128)S(1)}, f32[512,2048]{1,0:T(8,128)S(1)}, f32[320,128]{1,0:T(8,128)S(1)}) custom-call(bf16[512,2048]{1,0:T(8,128)(2,1)S(1)} %bitcast.14, f32[1,512]{1,0:T(1,128)S(1)} %bitcast.24, f32[1]{0:T(128)S(6)} %convert_element_type.40.e_ref, ...), custom_call_target="tpu_custom_call" | custom-call | flops 2147483648 | bytes 1048576 | tf_op jit(solution)/shard_map/pallas_call | solution.py:201
  35.7 0.0 collective-permute-done.2.r_ref
  35.7 0.0 copy-start.1
  35.7 2.5 %shard_map.69 = (bf16[512,512]{1,0:T(8,128)(2,1)S(1)}, f32[640,128]{1,0:T(8,128)S(1)}, bf16[640,128]{1,0:T(8,128)(2,1)S(1)}) custom-call(bf16[512,2048]{1,0:T(8,128)(2,1)S(1)} %bitcast.15, bf16[512,2048]{1,0:T(8,128)(2,1)S(1)} %collective-permute-done.2.r_ref, f32[512,512]{1,0:T(8,128)S(1)} %get-tuple-element.12.over_ref, s32[3,1,8]{2,1,0:T(1,128)S(1)} %bitcast.20, ...), custom_call_target="tpu_custom_call" | custom-call | flops 1073741824 | bytes 1048576 | tf_op jit(solution)/shard_map/pallas_call | solution.py:201
  38.2 0.1 collective-permute-start.7
  38.2 1.4 %collective-permute-done.7 = bf16[640,128]{1,0:T(8,128)(2,1)S(1)} collective-permute-done((bf16[640,128]{1,0:T(8,128)(2,1)S(1)}, bf16[640,128]{1,0:T(8,128)(2,1)S(1)}, u32[]{:S(2)}, u32[]{:S(2)}) %collective-permute-start.7) | collective-permute-done | bytes 163872 | tf_op jit(solution)/shard_map/ppermute | solution.py:43
  39.7 2.0 %collective-permute-start.8 = (bf16[320,128]{1,0:T(8,128)(2,1)S(1)}, bf16[320,128]{1,0:T(8,128)(2,1)S(1)}, u32[]{:S(2)}, u32[]{:S(2)}) collective-permute-start(bf16[320,128]{1,0:T(8,128)(2,1)S(1)} %get-tuple-element.20), channel_id=1, source_target_pairs={{0,8},{1,17},{2,18},{3,11},{4,12},{5,21},{6,22},{7,15},{8,0},{9,25... | collective-permute-start | bytes 245768 | tf_op jit(solution)/shard_map/ppermute | solution.py:43
  41.7 2.5 %collective-permute-done.8 = bf16[320,128]{1,0:T(8,128)(2,1)S(1)} collective-permute-done((bf16[320,128]{1,0:T(8,128)(2,1)S(1)}, bf16[320,128]{1,0:T(8,128)(2,1)S(1)}, u32[]{:S(2)}, u32[]{:S(2)}) %collective-permute-start.8) | collective-permute-done | bytes 81952 | tf_op jit(solution)/shard_map/ppermute | solution.py:43
  44.3 2.0 %collective-permute-start.9 = (bf16[320,128]{1,0:T(8,128)(2,1)S(1)}, bf16[320,128]{1,0:T(8,128)(2,1)S(1)}, u32[]{:S(2)}, u32[]{:S(2)}) collective-permute-start(bf16[320,128]{1,0:T(8,128)(2,1)S(1)} %get-tuple-element.18), channel_id=1, source_target_pairs={{0,16},{1,9},{2,10},{3,19},{4,20},{5,13},{6,14},{7,23},{8,24},{9,1... | collective-permute-start | bytes 245768 | tf_op jit(solution)/shard_map/ppermute | solution.py:43
  46.3 0.0 copy-done.1
  46.3 0.1 slice_bitcast_fusion
  46.4 0.0 copy-start.3
  46.4 0.0 copy-start.5
  46.4 0.1 collective-permute-start.3
  46.5 2.3 %collective-permute-done.9 = bf16[320,128]{1,0:T(8,128)(2,1)S(1)} collective-permute-done((bf16[320,128]{1,0:T(8,128)(2,1)S(1)}, bf16[320,128]{1,0:T(8,128)(2,1)S(1)}, u32[]{:S(2)}, u32[]{:S(2)}) %collective-permute-start.9) | collective-permute-done | bytes 81952 | tf_op jit(solution)/shard_map/ppermute | solution.py:43
  48.8 0.1 collective-permute-start.10
  48.9 0.5 collective-permute-start.4
  49.4 12.5 %collective-permute-done.10 = bf16[320,128]{1,0:T(8,128)(2,1)S(1)} collective-permute-done((bf16[320,128]{1,0:T(8,128)(2,1)S(1)}, bf16[320,128]{1,0:T(8,128)(2,1)S(1)}, u32[]{:S(2)}, u32[]{:S(2)}) %collective-permute-start.10) | collective-permute-done | bytes 81952 | tf_op jit(solution)/shard_map/ppermute | solution.py:43
  61.9 3.5 %collective-permute-start.11 = (bf16[320,128]{1,0:T(8,128)(2,1)S(1)}, bf16[320,128]{1,0:T(8,128)(2,1)S(1)}, u32[]{:S(2)}, u32[]{:S(2)}) collective-permute-start(bf16[320,128]{1,0:T(8,128)(2,1)S(1)} %fusion.1), channel_id=1, source_target_pairs={{0,7},{1,6},{2,5},{3,4},{4,3},{5,2},{6,1},{7,0},{8,15},{9,14},{10,... | collective-permute-start | bytes 245768 | tf_op jit(solution)/shard_map/ppermute | solution.py:43
  65.4 0.1 slice_bitcast_fusion.1
  65.5 0.1 collective-permute-start.5
  65.6 0.1 collective-permute-start.6
  65.7 2.1 %collective-permute-done.11 = bf16[320,128]{1,0:T(8,128)(2,1)S(1)} collective-permute-done((bf16[320,128]{1,0:T(8,128)(2,1)S(1)}, bf16[320,128]{1,0:T(8,128)(2,1)S(1)}, u32[]{:S(2)}, u32[]{:S(2)}) %collective-permute-start.11) | collective-permute-done | bytes 81952 | tf_op jit(solution)/shard_map/ppermute | solution.py:43
  67.8 0.1 multiply_convert_fusion
  67.8 1.5 %collective-permute-start.12 = (bf16[320,128]{1,0:T(8,128)(2,1)S(1)}, bf16[320,128]{1,0:T(8,128)(2,1)S(1)}, u32[]{:S(2)}, u32[]{:S(2)}) collective-permute-start(bf16[320,128]{1,0:T(8,128)(2,1)S(1)} %multiply_convert_fusion), channel_id=1, source_target_pairs={{0,8},{1,17},{2,18},{3,11},{4,12},{5,21},{6,22},{7,15},{8,0},{9,25... | collective-permute-start | bytes 245768 | tf_op jit(solution)/shard_map/ppermute | solution.py:43
  69.3 0.0 copy-done.3
  69.3 0.0 copy-done.5
  69.3 1.8 %shard_map.70.gamma_in = f32[512,2048]{1,0:T(8,128)S(1)} custom-call(s32[3,1,8]{2,1,0:T(1,128)S(1)} %bitcast.21, s32[1,8]{1,0:T(1,128)S(1)} %copy-done.5, f32[512,2048]{1,0:T(8,128)S(1)} %get-tuple-element.11.gamma_in, bf16[512,512]{1,0:T(8,128)(2,1)S(1)} %get-tuple-element.14.mt_ref, bf16[512,2048]{1,0:T(8,128)(2,1)S(1)} %collective-permute-done.2.r_ref), custom_call_target="tpu_custom_call" | custom-call | flops 1073741824 | bytes 1048576 | tf_op jit(solution)/shard_map/pallas_call | solution.py:201
  71.1 1.2 %collective-permute-done.12 = bf16[320,128]{1,0:T(8,128)(2,1)S(1)} collective-permute-done((bf16[320,128]{1,0:T(8,128)(2,1)S(1)}, bf16[320,128]{1,0:T(8,128)(2,1)S(1)}, u32[]{:S(2)}, u32[]{:S(2)}) %collective-permute-start.12) | collective-permute-done | bytes 81952 | tf_op jit(solution)/shard_map/ppermute | solution.py:43
  72.4 0.1 collective-permute-start.13
  72.5 0.0 collective-permute-done.3.r_ref
  72.5 2.0 %shard_map.71.gamma_in = f32[512,2048]{1,0:T(8,128)S(1)} custom-call(s32[3,1,8]{2,1,0:T(1,128)S(1)} %bitcast.22, s32[1,8]{1,0:T(1,128)S(1)} %copy-done.5, bf16[512,2048]{1,0:T(8,128)(2,1)S(1)} %bitcast.16, f32[512,512]{1,0:T(8,128)S(1)} %get-tuple-element.10.over_ref, f32[512,2048]{1,0:T(8,128)S(1)} %shard_map.70.gamma_in, ...), custom_call_target="tpu_custom_call" | custom-call | flops 1073741824 | bytes 1048576 | tf_op jit(solution)/shard_map/pallas_call | solution.py:201
  74.5 0.0 collective-permute-done.4.refs_0_
  74.5 0.0 collective-permute-done.5.refs_1_
  74.5 1.3 %collective-permute-done.6.refs_2_ = bf16[96,2048]{1,0:T(8,128)(2,1)S(1)} collective-permute-done((bf16[96,2048]{1,0:T(8,128)(2,1)S(1)}, bf16[96,2048]{1,0:T(8,128)(2,1)S(1)}, u32[]{:S(2)}, u32[]{:S(2)}) %collective-permute-start.6) | collective-permute-done | bytes 393248 | tf_op jit(solution)/shard_map/ppermute | solution.py:33
  75.8 3.0 %shard_map.72 = bf16[512,2048]{1,0:T(8,128)(2,1)} custom-call(s32[3,1,8]{2,1,0:T(1,128)S(1)} %bitcast.23, s32[1,8]{1,0:T(1,128)S(1)} %copy-done.5, bf16[512,2048]{1,0:T(8,128)(2,1)S(1)} %bitcast.17, f32[512,512]{1,0:T(8,128)S(1)} %get-tuple-element.10.over_ref, f32[512,2048]{1,0:T(8,128)S(1)} %shard_map.71.gamma_in, ...), custom_call_target="tpu_custom_call" | custom-call | flops 1073741824 | bytes 1048576 | tf_op jit(solution)/shard_map/pallas_call | solution.py:201
  78.8 0.0 collective-permute-done.13.other_ref
  78.8 2.1 %shard_map.73 = bf16[512,2048]{1,0:T(8,128)(2,1)} custom-call(bf16[640,128]{1,0:T(8,128)(2,1)S(1)} %pad_maximum_fusion.mine_ref, bf16[640,128]{1,0:T(8,128)(2,1)S(1)} %collective-permute-done.13.other_ref, bf16[512,2048]{1,0:T(8,128)(2,1)S(1)} %bitcast.18), custom_call_target="tpu_custom_call" | custom-call | flops 1073741824 | bytes 1048576 | tf_op jit(solution)/shard_map/pallas_call | solution.py:201
  (10 shorter events, 0.2 us)
Async XLA Ops:
  0.6 35.0 %collective-permute-start.2 = (bf16[512,2048]{1,0:T(8,128)(2,1)}, bf16[512,2048]{1,0:T(8,128)(2,1)S(1)}, u32[]{:S(2)}, u32[]{:S(2)}) collective-permute-start(bf16[512,2048]{1,0:T(8,128)(2,1)} %bitcast.13), channel_id=1, source_target_pairs={{0,1},{1,3},{2,0},{3,2},{4,5},{5,7},{6,4},{7,6},{8,9},{9,11},{10,8... | collective-permute-start | bytes 6291464 | tf_op jit(solution)/shard_map/ppermute | solution.py:33
  1.2 26.8 %collective-permute-start = (bf16[1]{0:T(256)(128)(2,1)}, bf16[1]{0:T(256)(128)(2,1)}, u32[]{:S(2)}, u32[]{:S(2)}) collective-permute-start(bf16[1]{0:T(256)(128)(2,1)} %param.6), channel_id=1, source_target_pairs={{0,1},{1,3},{2,0},{3,2},{4,5},{5,7},{6,4},{7,6},{8,9},{9,11},{10,8... | collective-permute-start | bytes 14 | tf_op jit(solution)/shard_map/ppermute | solution.py:33
  3.3 25.4 %collective-permute-start.1 = (bf16[1]{0:T(256)(128)(2,1)}, bf16[1]{0:T(256)(128)(2,1)}, u32[]{:S(2)}, u32[]{:S(2)}) collective-permute-start(bf16[1]{0:T(256)(128)(2,1)} %param.6), channel_id=1, source_target_pairs={{1,0},{3,1},{0,2},{2,3},{5,4},{7,5},{4,6},{6,7},{9,8},{11,9},{8,10... | collective-permute-start | bytes 14 | tf_op jit(solution)/shard_map/ppermute | solution.py:33
  29.3 1.6 %copy-start = (bf16[1,512,2048]{2,1,0:T(8,128)(2,1)S(1)}, bf16[1,512,2048]{2,1,0:T(8,128)(2,1)}, u32[]{:S(2)}) copy-start(bf16[1,512,2048]{2,1,0:T(8,128)(2,1)} %param.5) | copy-start | bytes 6291460
  30.9 0.7 copy-start.2
  31.6 0.7 copy-start.4
  35.7 10.6 %copy-start.1 = (bf16[1,512,2048]{2,1,0:T(8,128)(2,1)S(1)}, bf16[1,512,2048]{2,1,0:T(8,128)(2,1)}, u32[]{:S(2)}) copy-start(bf16[1,512,2048]{2,1,0:T(8,128)(2,1)} %param.5) | copy-start | bytes 6291460
  38.2 1.5 %collective-permute-start.7 = (bf16[640,128]{1,0:T(8,128)(2,1)S(1)}, bf16[640,128]{1,0:T(8,128)(2,1)S(1)}, u32[]{:S(2)}, u32[]{:S(2)}) collective-permute-start(bf16[640,128]{1,0:T(8,128)(2,1)S(1)} %get-tuple-element.17), channel_id=1, source_target_pairs={{0,1},{1,0},{2,3},{3,2},{4,5},{5,4},{6,7},{7,6},{8,9},{9,8},{10,11... | collective-permute-start | bytes 491528 | tf_op jit(solution)/shard_map/ppermute | solution.py:43
  39.7 4.5 %collective-permute-start.8 = (bf16[320,128]{1,0:T(8,128)(2,1)S(1)}, bf16[320,128]{1,0:T(8,128)(2,1)S(1)}, u32[]{:S(2)}, u32[]{:S(2)}) collective-permute-start(bf16[320,128]{1,0:T(8,128)(2,1)S(1)} %get-tuple-element.20), channel_id=1, source_target_pairs={{0,8},{1,17},{2,18},{3,11},{4,12},{5,21},{6,22},{7,15},{8,0},{9,25... | collective-permute-start | bytes 245768 | tf_op jit(solution)/shard_map/ppermute | solution.py:43
  44.3 4.5 %collective-permute-start.9 = (bf16[320,128]{1,0:T(8,128)(2,1)S(1)}, bf16[320,128]{1,0:T(8,128)(2,1)S(1)}, u32[]{:S(2)}, u32[]{:S(2)}) collective-permute-start(bf16[320,128]{1,0:T(8,128)(2,1)S(1)} %get-tuple-element.18), channel_id=1, source_target_pairs={{0,16},{1,9},{2,10},{3,19},{4,20},{5,13},{6,14},{7,23},{8,24},{9,1... | collective-permute-start | bytes 245768 | tf_op jit(solution)/shard_map/ppermute | solution.py:43
  46.4 22.9 %copy-start.3 = (s32[1,8,3]{1,0,2:T(1,128)S(1)}, s32[1,8,3]{1,0,2:T(1,128)}, u32[]{:S(2)}) copy-start(s32[1,8,3]{1,0,2:T(1,128)} %param.8) | copy-start | bytes 292
  46.4 22.9 %copy-start.5 = (s32[1,8]{1,0:T(1,128)S(1)}, s32[1,8]{1,0:T(1,128)}, u32[]{:S(2)}) copy-start(s32[1,8]{1,0:T(1,128)} %counts.9) | copy-start | bytes 100
  46.4 26.1 %collective-permute-start.3 = (bf16[256,2048]{1,0:T(8,128)(2,1)S(1)}, bf16[256,2048]{1,0:T(8,128)(2,1)S(1)}, u32[]{:S(2)}, u32[]{:S(2)}) collective-permute-start(bf16[256,2048]{1,0:T(8,128)(2,1)S(1)} %slice_bitcast_fusion), channel_id=1, source_target_pairs={{1,0},{3,1},{0,2},{2,3},{5,4},{7,5},{4,6},{6,7},{9,8},{11,9},{8,10... | collective-permute-start | bytes 3145736 | tf_op jit(solution)/shard_map/ppermute | solution.py:33
  48.8 13.1 %collective-permute-start.10 = (bf16[320,128]{1,0:T(8,128)(2,1)S(1)}, bf16[320,128]{1,0:T(8,128)(2,1)S(1)}, u32[]{:S(2)}, u32[]{:S(2)}) collective-permute-start(bf16[320,128]{1,0:T(8,128)(2,1)S(1)} %fusion), channel_id=1, source_target_pairs={{0,3},{1,2},{2,1},{3,0},{4,7},{5,6},{6,5},{7,4},{8,11},{9,10},{10,... | collective-permute-start | bytes 245768 | tf_op jit(solution)/shard_map/ppermute | solution.py:43
  48.9 25.6 %collective-permute-start.4 = (bf16[64,2048]{1,0:T(8,128)(2,1)S(1)}, bf16[64,2048]{1,0:T(8,128)(2,1)S(1)}, u32[]{:S(2)}, u32[]{:S(2)}) collective-permute-start(bf16[64,2048]{1,0:T(8,128)(2,1)S(1)} %slice_bitcast_fusion.3), channel_id=1, source_target_pairs={{1,0},{3,1},{0,2},{2,3},{5,4},{7,5},{4,6},{6,7},{9,8},{11,9},{8,10... | collective-permute-start | bytes 786440 | tf_op jit(solution)/shard_map/ppermute | solution.py:33
  61.9 5.8 %collective-permute-start.11 = (bf16[320,128]{1,0:T(8,128)(2,1)S(1)}, bf16[320,128]{1,0:T(8,128)(2,1)S(1)}, u32[]{:S(2)}, u32[]{:S(2)}) collective-permute-start(bf16[320,128]{1,0:T(8,128)(2,1)S(1)} %fusion.1), channel_id=1, source_target_pairs={{0,7},{1,6},{2,5},{3,4},{4,3},{5,2},{6,1},{7,0},{8,15},{9,14},{10,... | collective-permute-start | bytes 245768 | tf_op jit(solution)/shard_map/ppermute | solution.py:43
  65.5 9.0 %collective-permute-start.5 = (bf16[96,2048]{1,0:T(8,128)(2,1)S(1)}, bf16[96,2048]{1,0:T(8,128)(2,1)S(1)}, u32[]{:S(2)}, u32[]{:S(2)}) collective-permute-start(bf16[96,2048]{1,0:T(8,128)(2,1)S(1)} %get-tuple-element.23), channel_id=1, source_target_pairs={{1,0},{3,1},{0,2},{2,3},{5,4},{7,5},{4,6},{6,7},{9,8},{11,9},{8,10... | collective-permute-start | bytes 1179656 | tf_op jit(solution)/shard_map/ppermute | solution.py:33
  65.6 10.3 %collective-permute-start.6 = (bf16[96,2048]{1,0:T(8,128)(2,1)S(1)}, bf16[96,2048]{1,0:T(8,128)(2,1)S(1)}, u32[]{:S(2)}, u32[]{:S(2)}) collective-permute-start(bf16[96,2048]{1,0:T(8,128)(2,1)S(1)} %get-tuple-element.22), channel_id=1, source_target_pairs={{1,0},{3,1},{0,2},{2,3},{5,4},{7,5},{4,6},{6,7},{9,8},{11,9},{8,10... | collective-permute-start | bytes 1179656 | tf_op jit(solution)/shard_map/ppermute | solution.py:33
  67.8 4.5 %collective-permute-start.12 = (bf16[320,128]{1,0:T(8,128)(2,1)S(1)}, bf16[320,128]{1,0:T(8,128)(2,1)S(1)}, u32[]{:S(2)}, u32[]{:S(2)}) collective-permute-start(bf16[320,128]{1,0:T(8,128)(2,1)S(1)} %multiply_convert_fusion), channel_id=1, source_target_pairs={{0,8},{1,17},{2,18},{3,11},{4,12},{5,21},{6,22},{7,15},{8,0},{9,25... | collective-permute-start | bytes 245768 | tf_op jit(solution)/shard_map/ppermute | solution.py:43
  72.4 6.4 %collective-permute-start.13 = (bf16[640,128]{1,0:T(8,128)(2,1)S(1)}, bf16[640,128]{1,0:T(8,128)(2,1)S(1)}, u32[]{:S(2)}, u32[]{:S(2)}) collective-permute-start(bf16[640,128]{1,0:T(8,128)(2,1)S(1)} %pad_maximum_fusion.mine_ref), channel_id=1, source_target_pairs={{0,1},{1,0},{2,3},{3,2},{4,5},{5,4},{6,7},{7,6},{8,9},{9,8},{10,11... | collective-permute-start | bytes 491528 | tf_op jit(solution)/shard_map/ppermute | solution.py:43
where the time goes:
time: 81.2 us; the launch traced here: 81 us
  waiting for transfers between devices  46.1 us (57%)
  Pallas kernels  14.8 us (18%)
  starting transfers between devices  13.2 us (16%)
  local copies, waits for them, and re-layouts  3.08 us (4%)
  between operations  2.83 us (3%)
  other arithmetic  0.94 us (1%)
    ppermute x7, waiting for transfers between devices, turn(): return lax.ppermute(value, 'mem', pairs)  24.1 us
    ppermute x7, waiting for transfers between devices, swap(): return lax.ppermute(value, ('grp', 'mem'), pairs)  22.1 us
    pallas_call x6, Pallas kernels, call(): kernel_call(kernel, outs, scratch, smem, count, flops, out_spec)(*args)  14.8 us
    ppermute x7, starting transfers between devices, swap(): return lax.ppermute(value, ('grp', 'mem'), pairs)  9.22 us
    ppermute x7, starting transfers between devices, turn(): return lax.ppermute(value, 'mem', pairs)  3.93 us
    unnamed x12, local copies, waits for them, and re-layouts  2.94 us
  transfers between devices with their start and end apart: 14, of which 8 were waited for; matrix products, arithmetic and copies ran while one was open for 1% of the time, Pallas kernels for 13%

commit v1 on v0

--- a/solution.py
+++ b/solution.py
@@ -163,19 +163,22 @@
     return m_ref[...].T
 
 
-def second_gamma_kernel(codes, counts, b_ref, over_ref, gamma_in, r_ref, gamma_ref, mt_ref, m_ref):
+def next_gamma_kernel(cut, codes, counts, b_ref, over_ref, gamma_in, *refs):
+    parts, (gamma_ref, r_ref, mt_ref, m_ref) = refs[:-4], refs[-4:]
     own, far = weights(codes, counts, 3 - first_round(lax.axis_index("mem")))
-    mt_ref[...] = flat_amp(slice(0, r_ref.shape[0]), b_ref, r_ref, over_ref, m_ref)
+    if len(parts) == 1:
+        r_ref = parts[0]
+    else:
+        joined(parts, r_ref)
+    mt_ref[...] = flat_amp(slice(cut, cut + r_ref.shape[0]), b_ref, r_ref, over_ref, m_ref)
     aux = gamma_ref.shape[1]
     for p in range(STRIPS):
         at = pl.ds(p * (aux // STRIPS), aux // STRIPS)
         gamma_ref[:, at] = gamma_in[:, at] + (own + far) * nn(mt_ref[...], r_ref[:, at])
 
 
-def last_gamma_kernel(codes, counts, b_ref, over_ref, gamma_in, *refs):
-    parts, (out_ref, held, sems, r_ref, mt_ref, m_ref) = refs[:-6], refs[-6:]
+def last_gamma_kernel(codes, counts, b_ref, over_ref, gamma_in, r_ref, out_ref, held, sems, mt_ref, m_ref):
     own, far = weights(codes, counts, 3 - first_round(lax.axis_index("mem")))
-    joined(parts, r_ref)
     vir = b_ref.shape[0]
     mt_ref[...] = flat_amp(slice(vir - r_ref.shape[0], vir), b_ref, r_ref, over_ref, m_ref)
     strips_out(
@@ -264,21 +267,27 @@
     mine = jnp.concatenate([jnp.where(upper, got, mine), jnp.where(upper, mine, got)])
     other = swap(mine, [(0, 1), (0, 1)])
 
-    unit = vir // 16
-    cuts = (0, 8 * unit, 10 * unit, 13 * unit, vir)
+    unit = vir // 32
+    cuts = (0, 16 * unit, 21 * unit, 28 * unit, vir)
     parts = [block[a:b] for a, b in zip(cuts, cuts[1:])]
     second = [turn(part, True) for part in parts]
     gamma = call(first_gamma_kernel, wide, (), (0, 1), 5, dot)(
         pair_code, pair_count, gamma, mt, first
     )
-    bounce = [pltpu.VMEM((vir, vir // 2), BF16), pltpu.VMEM((vir // 2, vir), BF16)]
-    gamma = call(second_gamma_kernel, wide, bounce, (0, 1), 6, dot)(
-        pair_code, pair_count, block, over_second, gamma, second[0]
-    )
+
+    def bounce(rows):
+        return [pltpu.VMEM((vir, rows), BF16), pltpu.VMEM((rows, vir), BF16)]
+
+    for a, b in ((0, 1), (1, 3)):
+        rows = cuts[b] - cuts[a]
+        gamma = call(
+            functools.partial(next_gamma_kernel, cuts[a]), wide, [pltpu.VMEM((rows, aux), BF16), *bounce(rows)],
+            (0, 1), 5 + b - a, dot,
+        )(pair_code, pair_count, block, over_second, gamma, *second[a:b])
     result = call(
-        last_gamma_kernel, shape((vir, aux), BF16), [*out_scratch, pltpu.VMEM((vir // 2, aux), BF16), *bounce],
-        (0, 1), 8, dot, any_space,
-    )(pair_code, pair_count, block, over_second, gamma, *second[1:])
+        last_gamma_kernel, shape((vir, aux), BF16), [*out_scratch, *bounce(vir - cuts[3])],
+        (0, 1), 6, dot, any_space,
+    )(pair_code, pair_count, block, over_second, gamma, second[3])
     lagrangian = call(
         apply_kernel, shape((vir, aux), BF16), [pltpu.VMEM((vir, vir), BF16), *out_scratch], (), 3, dot,
         any_space,

time: 81.2 us -> 82.5 us (1.016)
  Pallas kernels: 14.8 us -> 17.1 us
  waiting for transfers between devices: 46.1 us -> 45 us
    pallas_call x6 -> x7, Pallas kernels: 14.8 us -> 17.1 us  [call(): kernel_call(kernel, outs, scratch, smem, count, flops, out_spec)(*args)]
    ppermute x7, waiting for transfers between devices: 24.1 us -> 22.8 us  [turn(): return lax.ppermute(value, 'mem', pairs)]
  transfers between devices with their start and end apart: 14 -> 14, of which waited for: 8 -> 7; matrix products, arithmetic and copies ran while one was open for 1% -> 1% of each run, Pallas kernels for 13% -> 15%
where the time goes in v1:
time: 82.5 us; the launch traced here: 82.2 us
  waiting for transfers between devices  45 us (55%)
  Pallas kernels  17.1 us (21%)
  starting transfers between devices  13.2 us (16%)
  local copies, waits for them, and re-layouts  3.11 us (4%)
  between operations  2.89 us (4%)
  other arithmetic  0.94 us (1%)
    ppermute x7, waiting for transfers between devices, turn(): return lax.ppermute(value, 'mem', pairs)  22.8 us
    ppermute x7, waiting for transfers between devices, swap(): return lax.ppermute(value, ('grp', 'mem'), pairs)  22.2 us
    pallas_call x7, Pallas kernels, call(): kernel_call(kernel, outs, scratch, smem, count, flops, out_spec)(*args)  17.1 us
    ppermute x7, starting transfers between devices, swap(): return lax.ppermute(value, ('grp', 'mem'), pairs)  8.79 us
    ppermute x7, starting transfers between devices, turn(): return lax.ppermute(value, 'mem', pairs)  4.41 us
    unnamed x12, local copies, waits for them, and re-layouts  2.94 us
  transfers between devices with their start and end apart: 14, of which 7 were waited for; matrix products, arithmetic and copies ran while one was open for 1% of the time, Pallas kernels for 15%

profile of v1, /device:TPU:0, one launch (start us, length us, event | category | flops | bytes accessed | tf_op | source)
XLA Modules:
  0.0 82.2 jit_solution(3792245792320763608)
XLA Ops:
  0.6 0.6 collective-permute-start.2
  1.2 2.1 %collective-permute-start = (bf16[1]{0:T(256)(128)(2,1)}, bf16[1]{0:T(256)(128)(2,1)}, u32[]{:S(2)}, u32[]{:S(2)}) collective-permute-start(bf16[1]{0:T(256)(128)(2,1)} %param.6), channel_id=1, source_target_pairs={{0,1},{1,3},{2,0},{3,2},{4,5},{5,7},{6,4},{7,6},{8,9},{9,11},{10,8... | collective-permute-start | bytes 14 | tf_op jit(solution)/shard_map/ppermute | solution.py:33
  3.3 0.6 collective-permute-start.1
  4.6 0.7 reshape.15
  5.3 22.8 %collective-permute-done = bf16[1]{0:T(256)(128)(2,1)} collective-permute-done((bf16[1]{0:T(256)(128)(2,1)}, bf16[1]{0:T(256)(128)(2,1)}, u32[]{:S(2)}, u32[]{:S(2)}) %collective-permute-start) | collective-permute-done | bytes 34 | tf_op jit(solution)/shard_map/ppermute | solution.py:33
  28.7 0.0 collective-permute-done.1
  29.4 0.0 copy-start
  29.4 1.6 %copy-done = bf16[1,512,2048]{2,1,0:T(8,128)(2,1)S(1)} copy-done((bf16[1,512,2048]{2,1,0:T(8,128)(2,1)S(1)}, bf16[1,512,2048]{2,1,0:T(8,128)(2,1)}, u32[]{:S(2)}) %copy-start) | copy-done | bytes 2097176
  31.0 0.7 copy-done.2
  31.7 0.7 copy-done.4
  32.4 3.4 %shard_map.68 = (f32[512,512]{1,0:T(8,128)S(1)}, f32[512,512]{1,0:T(8,128)S(1)}, f32[512,512]{1,0:T(8,128)S(1)}, f32[512,2048]{1,0:T(8,128)S(1)}, f32[320,128]{1,0:T(8,128)S(1)}) custom-call(bf16[512,2048]{1,0:T(8,128)(2,1)S(1)} %bitcast.14, f32[1,512]{1,0:T(1,128)S(1)} %bitcast.26, f32[1]{0:T(128)S(6)} %convert_element_type.40.e_ref, ...), custom_call_target="tpu_custom_call" | custom-call | flops 2147483648 | bytes 1048576 | tf_op jit(solution)/shard_map/pallas_call | solution.py:204
  35.8 0.0 collective-permute-done.2.r_ref
  35.8 0.0 copy-start.1
  35.8 2.5 %shard_map.69 = (bf16[512,512]{1,0:T(8,128)(2,1)S(1)}, f32[640,128]{1,0:T(8,128)S(1)}, bf16[640,128]{1,0:T(8,128)(2,1)S(1)}) custom-call(bf16[512,2048]{1,0:T(8,128)(2,1)S(1)} %bitcast.15, bf16[512,2048]{1,0:T(8,128)(2,1)S(1)} %collective-permute-done.2.r_ref, f32[512,512]{1,0:T(8,128)S(1)} %get-tuple-element.12.over_ref, s32[3,1,8]{2,1,0:T(1,128)S(1)} %bitcast.21, ...), custom_call_target="tpu_custom_call" | custom-call | flops 1073741824 | bytes 1048576 | tf_op jit(solution)/shard_map/pallas_call | solution.py:204
  38.3 0.1 collective-permute-start.7
  38.4 0.0 copy-done.1
  38.4 0.1 slice_bitcast_fusion
  38.5 0.7 collective-permute-start.3
  39.2 0.6 collective-permute-done.7
  39.8 0.0 copy-start.3
  39.8 0.0 copy-start.5
  39.9 2.0 %collective-permute-start.8 = (bf16[320,128]{1,0:T(8,128)(2,1)S(1)}, bf16[320,128]{1,0:T(8,128)(2,1)S(1)}, u32[]{:S(2)}, u32[]{:S(2)}) collective-permute-start(bf16[320,128]{1,0:T(8,128)(2,1)S(1)} %get-tuple-element.20), channel_id=1, source_target_pairs={{0,8},{1,17},{2,18},{3,11},{4,12},{5,21},{6,22},{7,15},{8,0},{9,25... | collective-permute-start | bytes 245768 | tf_op jit(solution)/shard_map/ppermute | solution.py:43
  41.9 0.1 collective-permute-start.4
  42.0 2.4 %collective-permute-done.8 = bf16[320,128]{1,0:T(8,128)(2,1)S(1)} collective-permute-done((bf16[320,128]{1,0:T(8,128)(2,1)S(1)}, bf16[320,128]{1,0:T(8,128)(2,1)S(1)}, u32[]{:S(2)}, u32[]{:S(2)}) %collective-permute-start.8) | collective-permute-done | bytes 81952 | tf_op jit(solution)/shard_map/ppermute | solution.py:43
  44.4 2.0 %collective-permute-start.9 = (bf16[320,128]{1,0:T(8,128)(2,1)S(1)}, bf16[320,128]{1,0:T(8,128)(2,1)S(1)}, u32[]{:S(2)}, u32[]{:S(2)}) collective-permute-start(bf16[320,128]{1,0:T(8,128)(2,1)S(1)} %get-tuple-element.18), channel_id=1, source_target_pairs={{0,16},{1,9},{2,10},{3,19},{4,20},{5,13},{6,14},{7,23},{8,24},{9,1... | collective-permute-start | bytes 245768 | tf_op jit(solution)/shard_map/ppermute | solution.py:43
  46.5 0.1 collective-permute-start.5
  46.5 2.4 %collective-permute-done.9 = bf16[320,128]{1,0:T(8,128)(2,1)S(1)} collective-permute-done((bf16[320,128]{1,0:T(8,128)(2,1)S(1)}, bf16[320,128]{1,0:T(8,128)(2,1)S(1)}, u32[]{:S(2)}, u32[]{:S(2)}) %collective-permute-start.9) | collective-permute-done | bytes 81952 | tf_op jit(solution)/shard_map/ppermute | solution.py:43
  48.9 0.1 collective-permute-start.10
  49.0 0.3 collective-permute-start.6
  49.4 14.5 %collective-permute-done.10 = bf16[320,128]{1,0:T(8,128)(2,1)S(1)} collective-permute-done((bf16[320,128]{1,0:T(8,128)(2,1)S(1)}, bf16[320,128]{1,0:T(8,128)(2,1)S(1)}, u32[]{:S(2)}, u32[]{:S(2)}) %collective-permute-start.10) | collective-permute-done | bytes 81952 | tf_op jit(solution)/shard_map/ppermute | solution.py:43
  64.0 2.9 %collective-permute-start.11 = (bf16[320,128]{1,0:T(8,128)(2,1)S(1)}, bf16[320,128]{1,0:T(8,128)(2,1)S(1)}, u32[]{:S(2)}, u32[]{:S(2)}) collective-permute-start(bf16[320,128]{1,0:T(8,128)(2,1)S(1)} %fusion.1), channel_id=1, source_target_pairs={{0,7},{1,6},{2,5},{3,4},{4,3},{5,2},{6,1},{7,0},{8,15},{9,14},{10,... | collective-permute-start | bytes 245768 | tf_op jit(solution)/shard_map/ppermute | solution.py:43
  66.9 0.0 copy-done.3
  66.9 0.0 copy-done.5
  66.9 1.8 %shard_map.70.gamma_in = f32[512,2048]{1,0:T(8,128)S(1)} custom-call(s32[3,1,8]{2,1,0:T(1,128)S(1)} %bitcast.22, s32[1,8]{1,0:T(1,128)S(1)} %copy-done.5, f32[512,2048]{1,0:T(8,128)S(1)} %get-tuple-element.11.gamma_in, bf16[512,512]{1,0:T(8,128)(2,1)S(1)} %get-tuple-element.14.mt_ref, bf16[512,2048]{1,0:T(8,128)(2,1)S(1)} %collective-permute-done.2.r_ref), custom_call_target="tpu_custom_call" | custom-call | flops 1073741824 | bytes 1048576 | tf_op jit(solution)/shard_map/pallas_call | solution.py:204
  68.7 1.5 %collective-permute-done.11 = bf16[320,128]{1,0:T(8,128)(2,1)S(1)} collective-permute-done((bf16[320,128]{1,0:T(8,128)(2,1)S(1)}, bf16[320,128]{1,0:T(8,128)(2,1)S(1)}, u32[]{:S(2)}, u32[]{:S(2)}) %collective-permute-start.11) | collective-permute-done | bytes 81952 | tf_op jit(solution)/shard_map/ppermute | solution.py:43
  70.2 0.1 multiply_convert_fusion
  70.2 1.6 %collective-permute-start.12 = (bf16[320,128]{1,0:T(8,128)(2,1)S(1)}, bf16[320,128]{1,0:T(8,128)(2,1)S(1)}, u32[]{:S(2)}, u32[]{:S(2)}) collective-permute-start(bf16[320,128]{1,0:T(8,128)(2,1)S(1)} %multiply_convert_fusion), channel_id=1, source_target_pairs={{0,8},{1,17},{2,18},{3,11},{4,12},{5,21},{6,22},{7,15},{8,0},{9,25... | collective-permute-start | bytes 245768 | tf_op jit(solution)/shard_map/ppermute | solution.py:43
  71.9 0.0 collective-permute-done.3.refs_0_
  71.9 2.0 %shard_map.71.gamma_in = f32[512,2048]{1,0:T(8,128)S(1)} custom-call(s32[3,1,8]{2,1,0:T(1,128)S(1)} %bitcast.23, s32[1,8]{1,0:T(1,128)S(1)} %copy-done.5, bf16[512,2048]{1,0:T(8,128)(2,1)S(1)} %bitcast.16, f32[512,512]{1,0:T(8,128)S(1)} %get-tuple-element.10.over_ref, f32[512,2048]{1,0:T(8,128)S(1)} %shard_map.70.gamma_in, ...), custom_call_target="tpu_custom_call" | custom-call | flops 1073741824 | bytes 1048576 | tf_op jit(solution)/shard_map/pallas_call | solution.py:204
  73.9 0.8 %collective-permute-done.12 = bf16[320,128]{1,0:T(8,128)(2,1)S(1)} collective-permute-done((bf16[320,128]{1,0:T(8,128)(2,1)S(1)}, bf16[320,128]{1,0:T(8,128)(2,1)S(1)}, u32[]{:S(2)}, u32[]{:S(2)}) %collective-permute-start.12) | collective-permute-done | bytes 81952 | tf_op jit(solution)/shard_map/ppermute | solution.py:43
  74.8 0.1 collective-permute-start.13
  74.9 0.0 collective-permute-done.4.refs_0_
  74.9 0.0 collective-permute-done.5.refs_1_
  74.9 2.2 %shard_map.72.gamma_in = f32[512,2048]{1,0:T(8,128)S(1)} custom-call(s32[3,1,8]{2,1,0:T(1,128)S(1)} %bitcast.24, s32[1,8]{1,0:T(1,128)S(1)} %copy-done.5, bf16[512,2048]{1,0:T(8,128)(2,1)S(1)} %bitcast.17, f32[512,512]{1,0:T(8,128)S(1)} %get-tuple-element.10.over_ref, f32[512,2048]{1,0:T(8,128)S(1)} %shard_map.71.gamma_in, ...), custom_call_target="tpu_custom_call" | custom-call | flops 1073741824 | bytes 1048576 | tf_op jit(solution)/shard_map/pallas_call | solution.py:204
  77.1 0.0 collective-permute-done.6.r_ref
  77.1 3.0 %shard_map.73 = bf16[512,2048]{1,0:T(8,128)(2,1)} custom-call(s32[3,1,8]{2,1,0:T(1,128)S(1)} %bitcast.25, s32[1,8]{1,0:T(1,128)S(1)} %copy-done.5, bf16[512,2048]{1,0:T(8,128)(2,1)S(1)} %bitcast.18, f32[512,512]{1,0:T(8,128)S(1)} %get-tuple-element.10.over_ref, f32[512,2048]{1,0:T(8,128)S(1)} %shard_map.72.gamma_in, ...), custom_call_target="tpu_custom_call" | custom-call | flops 1073741824 | bytes 1048576 | tf_op jit(solution)/shard_map/pallas_call | solution.py:204
  80.1 0.0 collective-permute-done.13.other_ref
  80.1 2.1 %shard_map.74 = bf16[512,2048]{1,0:T(8,128)(2,1)} custom-call(bf16[640,128]{1,0:T(8,128)(2,1)S(1)} %pad_maximum_fusion.mine_ref, bf16[640,128]{1,0:T(8,128)(2,1)S(1)} %collective-permute-done.13.other_ref, bf16[512,2048]{1,0:T(8,128)(2,1)S(1)} %bitcast.19), custom_call_target="tpu_custom_call" | custom-call | flops 1073741824 | bytes 1048576 | tf_op jit(solution)/shard_map/pallas_call | solution.py:204
  (12 shorter events, 0.3 us)
Async XLA Ops:
  0.6 35.2 %collective-permute-start.2 = (bf16[512,2048]{1,0:T(8,128)(2,1)}, bf16[512,2048]{1,0:T(8,128)(2,1)S(1)}, u32[]{:S(2)}, u32[]{:S(2)}) collective-permute-start(bf16[512,2048]{1,0:T(8,128)(2,1)} %bitcast.13), channel_id=1, source_target_pairs={{0,1},{1,3},{2,0},{3,2},{4,5},{5,7},{6,4},{7,6},{8,9},{9,11},{10,8... | collective-permute-start | bytes 6291464 | tf_op jit(solution)/shard_map/ppermute | solution.py:33
  1.2 26.9 %collective-permute-start = (bf16[1]{0:T(256)(128)(2,1)}, bf16[1]{0:T(256)(128)(2,1)}, u32[]{:S(2)}, u32[]{:S(2)}) collective-permute-start(bf16[1]{0:T(256)(128)(2,1)} %param.6), channel_id=1, source_target_pairs={{0,1},{1,3},{2,0},{3,2},{4,5},{5,7},{6,4},{7,6},{8,9},{9,11},{10,8... | collective-permute-start | bytes 14 | tf_op jit(solution)/shard_map/ppermute | solution.py:33
  3.3 25.4 %collective-permute-start.1 = (bf16[1]{0:T(256)(128)(2,1)}, bf16[1]{0:T(256)(128)(2,1)}, u32[]{:S(2)}, u32[]{:S(2)}) collective-permute-start(bf16[1]{0:T(256)(128)(2,1)} %param.6), channel_id=1, source_target_pairs={{1,0},{3,1},{0,2},{2,3},{5,4},{7,5},{4,6},{6,7},{9,8},{11,9},{8,10... | collective-permute-start | bytes 14 | tf_op jit(solution)/shard_map/ppermute | solution.py:33
  29.4 1.6 %copy-start = (bf16[1,512,2048]{2,1,0:T(8,128)(2,1)S(1)}, bf16[1,512,2048]{2,1,0:T(8,128)(2,1)}, u32[]{:S(2)}) copy-start(bf16[1,512,2048]{2,1,0:T(8,128)(2,1)} %param.5) | copy-start | bytes 6291460
  31.0 0.7 copy-start.2
  31.7 0.7 copy-start.4
  35.8 2.6 %copy-start.1 = (bf16[1,512,2048]{2,1,0:T(8,128)(2,1)S(1)}, bf16[1,512,2048]{2,1,0:T(8,128)(2,1)}, u32[]{:S(2)}) copy-start(bf16[1,512,2048]{2,1,0:T(8,128)(2,1)} %param.5) | copy-start | bytes 6291460
  38.3 1.5 %collective-permute-start.7 = (bf16[640,128]{1,0:T(8,128)(2,1)S(1)}, bf16[640,128]{1,0:T(8,128)(2,1)S(1)}, u32[]{:S(2)}, u32[]{:S(2)}) collective-permute-start(bf16[640,128]{1,0:T(8,128)(2,1)S(1)} %get-tuple-element.17), channel_id=1, source_target_pairs={{0,1},{1,0},{2,3},{3,2},{4,5},{5,4},{6,7},{7,6},{8,9},{9,8},{10,11... | collective-permute-start | bytes 491528 | tf_op jit(solution)/shard_map/ppermute | solution.py:43
  38.5 33.4 %collective-permute-start.3 = (bf16[256,2048]{1,0:T(8,128)(2,1)S(1)}, bf16[256,2048]{1,0:T(8,128)(2,1)S(1)}, u32[]{:S(2)}, u32[]{:S(2)}) collective-permute-start(bf16[256,2048]{1,0:T(8,128)(2,1)S(1)} %slice_bitcast_fusion), channel_id=1, source_target_pairs={{1,0},{3,1},{0,2},{2,3},{5,4},{7,5},{4,6},{6,7},{9,8},{11,9},{8,10... | collective-permute-start | bytes 3145736 | tf_op jit(solution)/shard_map/ppermute | solution.py:33
  39.8 27.1 %copy-start.3 = (s32[1,8,3]{1,0,2:T(1,128)S(1)}, s32[1,8,3]{1,0,2:T(1,128)}, u32[]{:S(2)}) copy-start(s32[1,8,3]{1,0,2:T(1,128)} %param.8) | copy-start | bytes 292
  39.8 27.1 %copy-start.5 = (s32[1,8]{1,0:T(1,128)S(1)}, s32[1,8]{1,0:T(1,128)}, u32[]{:S(2)}) copy-start(s32[1,8]{1,0:T(1,128)} %counts.11) | copy-start | bytes 100
  39.9 4.5 %collective-permute-start.8 = (bf16[320,128]{1,0:T(8,128)(2,1)S(1)}, bf16[320,128]{1,0:T(8,128)(2,1)S(1)}, u32[]{:S(2)}, u32[]{:S(2)}) collective-permute-start(bf16[320,128]{1,0:T(8,128)(2,1)S(1)} %get-tuple-element.20), channel_id=1, source_target_pairs={{0,8},{1,17},{2,18},{3,11},{4,12},{5,21},{6,22},{7,15},{8,0},{9,25... | collective-permute-start | bytes 245768 | tf_op jit(solution)/shard_map/ppermute | solution.py:43
  41.9 33.0 %collective-permute-start.4 = (bf16[80,2048]{1,0:T(8,128)(2,1)S(1)}, bf16[80,2048]{1,0:T(8,128)(2,1)S(1)}, u32[]{:S(2)}, u32[]{:S(2)}) collective-permute-start(bf16[80,2048]{1,0:T(8,128)(2,1)S(1)} %slice_bitcast_fusion.2), channel_id=1, source_target_pairs={{1,0},{3,1},{0,2},{2,3},{5,4},{7,5},{4,6},{6,7},{9,8},{11,9},{8,10... | collective-permute-start | bytes 983048 | tf_op jit(solution)/shard_map/ppermute | solution.py:33
  44.4 4.5 %collective-permute-start.9 = (bf16[320,128]{1,0:T(8,128)(2,1)S(1)}, bf16[320,128]{1,0:T(8,128)(2,1)S(1)}, u32[]{:S(2)}, u32[]{:S(2)}) collective-permute-start(bf16[320,128]{1,0:T(8,128)(2,1)S(1)} %get-tuple-element.18), channel_id=1, source_target_pairs={{0,16},{1,9},{2,10},{3,19},{4,20},{5,13},{6,14},{7,23},{8,24},{9,1... | collective-permute-start | bytes 245768 | tf_op jit(solution)/shard_map/ppermute | solution.py:43
  46.5 28.4 %collective-permute-start.5 = (bf16[112,2048]{1,0:T(8,128)(2,1)S(1)}, bf16[112,2048]{1,0:T(8,128)(2,1)S(1)}, u32[]{:S(2)}, u32[]{:S(2)}) collective-permute-start(bf16[112,2048]{1,0:T(8,128)(2,1)S(1)} %slice_bitcast_fusion.1), channel_id=1, source_target_pairs={{1,0},{3,1},{0,2},{2,3},{5,4},{7,5},{4,6},{6,7},{9,8},{11,9},{8,10... | collective-permute-start | bytes 1376264 | tf_op jit(solution)/shard_map/ppermute | solution.py:33
  48.9 15.0 %collective-permute-start.10 = (bf16[320,128]{1,0:T(8,128)(2,1)S(1)}, bf16[320,128]{1,0:T(8,128)(2,1)S(1)}, u32[]{:S(2)}, u32[]{:S(2)}) collective-permute-start(bf16[320,128]{1,0:T(8,128)(2,1)S(1)} %fusion), channel_id=1, source_target_pairs={{0,3},{1,2},{2,1},{3,0},{4,7},{5,6},{6,5},{7,4},{8,11},{9,10},{10,... | collective-permute-start | bytes 245768 | tf_op jit(solution)/shard_map/ppermute | solution.py:43
  49.0 28.0 %collective-permute-start.6 = (bf16[64,2048]{1,0:T(8,128)(2,1)S(1)}, bf16[64,2048]{1,0:T(8,128)(2,1)S(1)}, u32[]{:S(2)}, u32[]{:S(2)}) collective-permute-start(bf16[64,2048]{1,0:T(8,128)(2,1)S(1)} %slice_bitcast_fusion.3), channel_id=1, source_target_pairs={{1,0},{3,1},{0,2},{2,3},{5,4},{7,5},{4,6},{6,7},{9,8},{11,9},{8,10... | collective-permute-start | bytes 786440 | tf_op jit(solution)/shard_map/ppermute | solution.py:33
  64.0 6.2 %collective-permute-start.11 = (bf16[320,128]{1,0:T(8,128)(2,1)S(1)}, bf16[320,128]{1,0:T(8,128)(2,1)S(1)}, u32[]{:S(2)}, u32[]{:S(2)}) collective-permute-start(bf16[320,128]{1,0:T(8,128)(2,1)S(1)} %fusion.1), channel_id=1, source_target_pairs={{0,7},{1,6},{2,5},{3,4},{4,3},{5,2},{6,1},{7,0},{8,15},{9,14},{10,... | collective-permute-start | bytes 245768 | tf_op jit(solution)/shard_map/ppermute | solution.py:43
  70.2 4.5 %collective-permute-start.12 = (bf16[320,128]{1,0:T(8,128)(2,1)S(1)}, bf16[320,128]{1,0:T(8,128)(2,1)S(1)}, u32[]{:S(2)}, u32[]{:S(2)}) collective-permute-start(bf16[320,128]{1,0:T(8,128)(2,1)S(1)} %multiply_convert_fusion), channel_id=1, source_target_pairs={{0,8},{1,17},{2,18},{3,11},{4,12},{5,21},{6,22},{7,15},{8,0},{9,25... | collective-permute-start | bytes 245768 | tf_op jit(solution)/shard_map/ppermute | solution.py:43
  74.8 5.3 %collective-permute-start.13 = (bf16[640,128]{1,0:T(8,128)(2,1)S(1)}, bf16[640,128]{1,0:T(8,128)(2,1)S(1)}, u32[]{:S(2)}, u32[]{:S(2)}) collective-permute-start(bf16[640,128]{1,0:T(8,128)(2,1)S(1)} %pad_maximum_fusion.mine_ref), channel_id=1, source_target_pairs={{0,1},{1,0},{2,3},{3,2},{4,5},{5,4},{6,7},{7,6},{8,9},{9,8},{10,11... | collective-permute-start | bytes 491528 | tf_op jit(solution)/shard_map/ppermute | solution.py:43

commit v2 on v0

--- a/solution.py
+++ b/solution.py
@@ -163,8 +163,10 @@
     return m_ref[...].T
 
 
-def second_gamma_kernel(codes, counts, b_ref, over_ref, gamma_in, r_ref, gamma_ref, mt_ref, m_ref):
+def second_gamma_kernel(codes, counts, b_ref, over_ref, gamma_in, *refs):
+    parts, (gamma_ref, r_ref, mt_ref, m_ref) = refs[:-4], refs[-4:]
     own, far = weights(codes, counts, 3 - first_round(lax.axis_index("mem")))
+    joined(parts, r_ref)
     mt_ref[...] = flat_amp(slice(0, r_ref.shape[0]), b_ref, r_ref, over_ref, m_ref)
     aux = gamma_ref.shape[1]
     for p in range(STRIPS):
@@ -255,30 +257,33 @@
     below, above = total[: half // 2], total[half // 2 :]
     got = swap(jnp.where(upper, below, above).astype(BF16), split)
     total = jnp.where(upper, above, below) + got.astype(F32)
+    for mask in along[1:] + along[:1]:
+        total = total + swap(total.astype(BF16), [mask, mask]).astype(F32)
     for masks in later:
         total = total + swap(total.astype(BF16), masks).astype(F32)
-    for mask in along:
-        total = total + swap(total.astype(BF16), [mask, mask]).astype(F32)
     mine = (total * (1.0 / (8.0 * groups * members))).astype(BF16)
     got = swap(mine, split)
     mine = jnp.concatenate([jnp.where(upper, got, mine), jnp.where(upper, mine, got)])
     other = swap(mine, [(0, 1), (0, 1)])
 
-    unit = vir // 16
-    cuts = (0, 8 * unit, 10 * unit, 13 * unit, vir)
+    unit = vir // 32
+    cuts = (0, 14 * unit, 16 * unit, 21 * unit, vir)
     parts = [block[a:b] for a, b in zip(cuts, cuts[1:])]
     second = [turn(part, True) for part in parts]
     gamma = call(first_gamma_kernel, wide, (), (0, 1), 5, dot)(
         pair_code, pair_count, gamma, mt, first
     )
-    bounce = [pltpu.VMEM((vir, vir // 2), BF16), pltpu.VMEM((vir // 2, vir), BF16)]
-    gamma = call(second_gamma_kernel, wide, bounce, (0, 1), 6, dot)(
-        pair_code, pair_count, block, over_second, gamma, second[0]
+    bounce = [
+        pltpu.VMEM((vir // 2, aux), BF16),
+        pltpu.VMEM((vir, vir // 2), BF16),
+        pltpu.VMEM((vir // 2, vir), BF16),
+    ]
+    gamma = call(second_gamma_kernel, wide, bounce, (0, 1), 7, dot)(
+        pair_code, pair_count, block, over_second, gamma, *second[:2]
     )
     result = call(
-        last_gamma_kernel, shape((vir, aux), BF16), [*out_scratch, pltpu.VMEM((vir // 2, aux), BF16), *bounce],
-        (0, 1), 8, dot, any_space,
-    )(pair_code, pair_count, block, over_second, gamma, *second[1:])
+        last_gamma_kernel, shape((vir, aux), BF16), [*out_scratch, *bounce], (0, 1), 7, dot, any_space
+    )(pair_code, pair_count, block, over_second, gamma, *second[2:])
     lagrangian = call(
         apply_kernel, shape((vir, aux), BF16), [pltpu.VMEM((vir, vir), BF16), *out_scratch], (), 3, dot,
         any_space,

time: 81.2 us -> 80.1 us (0.986)
  starting transfers between devices: 13.2 us -> 10.4 us
  waiting for transfers between devices: 46.1 us -> 47.7 us
    ppermute x7, starting transfers between devices: 9.22 us -> 5.85 us  [swap(): return lax.ppermute(value, ('grp', 'mem'), pairs)]
    ppermute x7, waiting for transfers between devices: 22.1 us -> 24.9 us  [swap(): return lax.ppermute(value, ('grp', 'mem'), pairs)]
    ppermute x7, waiting for transfers between devices: 24.1 us -> 22.8 us  [turn(): return lax.ppermute(value, 'mem', pairs)]
  transfers between devices with their start and end apart: 14 -> 14, of which waited for: 8 -> 7; matrix products, arithmetic and copies ran while one was open for 1% -> 1% of each run, Pallas kernels for 13% -> 13%
where the time goes in v2:
time: 80.1 us; the launch traced here: 79.9 us
  waiting for transfers between devices  47.7 us (60%)
  Pallas kernels  14.8 us (18%)
  starting transfers between devices  10.4 us (13%)
  local copies, waits for them, and re-layouts  3.09 us (4%)
  between operations  2.88 us (4%)
  other arithmetic  0.92 us (1%)
    ppermute x7, waiting for transfers between devices, swap(): return lax.ppermute(value, ('grp', 'mem'), pairs)  24.9 us
    ppermute x7, waiting for transfers between devices, turn(): return lax.ppermute(value, 'mem', pairs)  22.8 us
    pallas_call x6, Pallas kernels, call(): kernel_call(kernel, outs, scratch, smem, count, flops, out_spec)(*args)  14.8 us
    ppermute x7, starting transfers between devices, swap(): return lax.ppermute(value, ('grp', 'mem'), pairs)  5.85 us
    ppermute x7, starting transfers between devices, turn(): return lax.ppermute(value, 'mem', pairs)  4.6 us
    unnamed x12, local copies, waits for them, and re-layouts  2.93 us
  transfers between devices with their start and end apart: 14, of which 7 were waited for; matrix products, arithmetic and copies ran while one was open for 1% of the time, Pallas kernels for 13%

profile of v2, /device:TPU:0, one launch (start us, length us, event | category | flops | bytes accessed | tf_op | source)
XLA Modules:
  0.0 79.9 jit_solution(3468236335117454018)
XLA Ops:
  0.6 0.6 collective-permute-start.2
  1.2 2.1 %collective-permute-start = (bf16[1]{0:T(256)(128)(2,1)}, bf16[1]{0:T(256)(128)(2,1)}, u32[]{:S(2)}, u32[]{:S(2)}) collective-permute-start(bf16[1]{0:T(256)(128)(2,1)} %param.6), channel_id=1, source_target_pairs={{0,1},{1,3},{2,0},{3,2},{4,5},{5,7},{6,4},{7,6},{8,9},{9,11},{10,8... | collective-permute-start | bytes 14 | tf_op jit(solution)/shard_map/ppermute | solution.py:33
  3.3 0.6 collective-permute-start.1
  4.6 0.7 reshape.15
  5.3 22.8 %collective-permute-done = bf16[1]{0:T(256)(128)(2,1)} collective-permute-done((bf16[1]{0:T(256)(128)(2,1)}, bf16[1]{0:T(256)(128)(2,1)}, u32[]{:S(2)}, u32[]{:S(2)}) %collective-permute-start) | collective-permute-done | bytes 34 | tf_op jit(solution)/shard_map/ppermute | solution.py:33
  28.7 0.0 collective-permute-done.1
  29.4 0.0 copy-start
  29.4 1.6 %copy-done = bf16[1,512,2048]{2,1,0:T(8,128)(2,1)S(1)} copy-done((bf16[1,512,2048]{2,1,0:T(8,128)(2,1)S(1)}, bf16[1,512,2048]{2,1,0:T(8,128)(2,1)}, u32[]{:S(2)}) %copy-start) | copy-done | bytes 2097176
  31.0 0.0 copy-start.2
  31.0 0.7 copy-done.2
  31.7 0.0 copy-start.4
  31.7 0.7 copy-done.4
  32.4 3.4 %shard_map.68 = (f32[512,512]{1,0:T(8,128)S(1)}, f32[512,512]{1,0:T(8,128)S(1)}, f32[512,512]{1,0:T(8,128)S(1)}, f32[512,2048]{1,0:T(8,128)S(1)}, f32[320,128]{1,0:T(8,128)S(1)}) custom-call(bf16[512,2048]{1,0:T(8,128)(2,1)S(1)} %bitcast.14, f32[1,512]{1,0:T(1,128)S(1)} %bitcast.24, f32[1]{0:T(128)S(6)} %convert_element_type.40.e_ref, ...), custom_call_target="tpu_custom_call" | custom-call | flops 2147483648 | bytes 1048576 | tf_op jit(solution)/shard_map/pallas_call | solution.py:203
  35.8 0.0 collective-permute-done.2.r_ref
  35.8 0.0 copy-start.1
  35.8 2.5 %shard_map.69 = (bf16[512,512]{1,0:T(8,128)(2,1)S(1)}, f32[640,128]{1,0:T(8,128)S(1)}, bf16[640,128]{1,0:T(8,128)(2,1)S(1)}) custom-call(bf16[512,2048]{1,0:T(8,128)(2,1)S(1)} %bitcast.15, bf16[512,2048]{1,0:T(8,128)(2,1)S(1)} %collective-permute-done.2.r_ref, f32[512,512]{1,0:T(8,128)S(1)} %get-tuple-element.12.over_ref, s32[3,1,8]{2,1,0:T(1,128)S(1)} %bitcast.20, ...), custom_call_target="tpu_custom_call" | custom-call | flops 1073741824 | bytes 1048576 | tf_op jit(solution)/shard_map/pallas_call | solution.py:203
  38.3 0.1 collective-permute-start.7
  38.4 1.4 %collective-permute-done.7 = bf16[640,128]{1,0:T(8,128)(2,1)S(1)} collective-permute-done((bf16[640,128]{1,0:T(8,128)(2,1)S(1)}, bf16[640,128]{1,0:T(8,128)(2,1)S(1)}, u32[]{:S(2)}, u32[]{:S(2)}) %collective-permute-start.7) | collective-permute-done | bytes 163872 | tf_op jit(solution)/shard_map/ppermute | solution.py:43
  39.8 2.0 %collective-permute-start.8 = (bf16[320,128]{1,0:T(8,128)(2,1)S(1)}, bf16[320,128]{1,0:T(8,128)(2,1)S(1)}, u32[]{:S(2)}, u32[]{:S(2)}) collective-permute-start(bf16[320,128]{1,0:T(8,128)(2,1)S(1)} %get-tuple-element.20), channel_id=1, source_target_pairs={{0,8},{1,17},{2,18},{3,11},{4,12},{5,21},{6,22},{7,15},{8,0},{9,25... | collective-permute-start | bytes 245768 | tf_op jit(solution)/shard_map/ppermute | solution.py:43
  41.8 0.0 copy-done.1
  41.8 0.1 slice_bitcast_fusion
  41.9 0.1 collective-permute-start.3
  42.0 2.4 %collective-permute-done.8 = bf16[320,128]{1,0:T(8,128)(2,1)S(1)} collective-permute-done((bf16[320,128]{1,0:T(8,128)(2,1)S(1)}, bf16[320,128]{1,0:T(8,128)(2,1)S(1)}, u32[]{:S(2)}, u32[]{:S(2)}) %collective-permute-start.8) | collective-permute-done | bytes 81952 | tf_op jit(solution)/shard_map/ppermute | solution.py:43
  44.4 1.5 %collective-permute-start.9 = (bf16[320,128]{1,0:T(8,128)(2,1)S(1)}, bf16[320,128]{1,0:T(8,128)(2,1)S(1)}, u32[]{:S(2)}, u32[]{:S(2)}) collective-permute-start(bf16[320,128]{1,0:T(8,128)(2,1)S(1)} %get-tuple-element.18), channel_id=1, source_target_pairs={{0,7},{1,6},{2,5},{3,4},{4,3},{5,2},{6,1},{7,0},{8,15},{9,14},{10,... | collective-permute-start | bytes 245768 | tf_op jit(solution)/shard_map/ppermute | solution.py:43
  45.9 1.1 %collective-permute-start.4 = (bf16[32,2048]{1,0:T(8,128)(2,1)S(1)}, bf16[32,2048]{1,0:T(8,128)(2,1)S(1)}, u32[]{:S(2)}, u32[]{:S(2)}) collective-permute-start(bf16[32,2048]{1,0:T(8,128)(2,1)S(1)} %slice_bitcast_fusion.3), channel_id=1, source_target_pairs={{1,0},{3,1},{0,2},{2,3},{5,4},{7,5},{4,6},{6,7},{9,8},{11,9},{8,10... | collective-permute-start | bytes 393224 | tf_op jit(solution)/shard_map/ppermute | solution.py:33
  47.0 11.9 %collective-permute-done.9 = bf16[320,128]{1,0:T(8,128)(2,1)S(1)} collective-permute-done((bf16[320,128]{1,0:T(8,128)(2,1)S(1)}, bf16[320,128]{1,0:T(8,128)(2,1)S(1)}, u32[]{:S(2)}, u32[]{:S(2)}) %collective-permute-start.9) | collective-permute-done | bytes 81952 | tf_op jit(solution)/shard_map/ppermute | solution.py:43
  59.0 0.1 collective-permute-start.10
  59.1 0.1 collective-permute-start.5
  59.1 3.7 %collective-permute-done.10 = bf16[320,128]{1,0:T(8,128)(2,1)S(1)} collective-permute-done((bf16[320,128]{1,0:T(8,128)(2,1)S(1)}, bf16[320,128]{1,0:T(8,128)(2,1)S(1)}, u32[]{:S(2)}, u32[]{:S(2)}) %collective-permute-start.10) | collective-permute-done | bytes 81952 | tf_op jit(solution)/shard_map/ppermute | solution.py:43
  62.9 0.6 collective-permute-start.11
  63.5 0.1 slice_bitcast_fusion.1
  63.6 0.1 collective-permute-start.6
  63.6 4.4 %collective-permute-done.11 = bf16[320,128]{1,0:T(8,128)(2,1)S(1)} collective-permute-done((bf16[320,128]{1,0:T(8,128)(2,1)S(1)}, bf16[320,128]{1,0:T(8,128)(2,1)S(1)}, u32[]{:S(2)}, u32[]{:S(2)}) %collective-permute-start.11) | collective-permute-done | bytes 81952 | tf_op jit(solution)/shard_map/ppermute | solution.py:43
  68.0 0.1 multiply_convert_fusion
  68.1 1.6 %collective-permute-start.12 = (bf16[320,128]{1,0:T(8,128)(2,1)S(1)}, bf16[320,128]{1,0:T(8,128)(2,1)S(1)}, u32[]{:S(2)}, u32[]{:S(2)}) collective-permute-start(bf16[320,128]{1,0:T(8,128)(2,1)S(1)} %multiply_convert_fusion), channel_id=1, source_target_pairs={{0,8},{1,17},{2,18},{3,11},{4,12},{5,21},{6,22},{7,15},{8,0},{9,25... | collective-permute-start | bytes 245768 | tf_op jit(solution)/shard_map/ppermute | solution.py:43
  69.6 0.0 copy-done.3
  69.6 0.0 copy-done.5
  69.6 1.8 %shard_map.70.gamma_in = f32[512,2048]{1,0:T(8,128)S(1)} custom-call(s32[3,1,8]{2,1,0:T(1,128)S(1)} %bitcast.21, s32[1,8]{1,0:T(1,128)S(1)} %copy-done.5, f32[512,2048]{1,0:T(8,128)S(1)} %get-tuple-element.11.gamma_in, bf16[512,512]{1,0:T(8,128)(2,1)S(1)} %get-tuple-element.14.mt_ref, bf16[512,2048]{1,0:T(8,128)(2,1)S(1)} %collective-permute-done.2.r_ref), custom_call_target="tpu_custom_call" | custom-call | flops 1073741824 | bytes 1048576 | tf_op jit(solution)/shard_map/pallas_call | solution.py:203
  71.5 1.1 %collective-permute-done.12 = bf16[320,128]{1,0:T(8,128)(2,1)S(1)} collective-permute-done((bf16[320,128]{1,0:T(8,128)(2,1)S(1)}, bf16[320,128]{1,0:T(8,128)(2,1)S(1)}, u32[]{:S(2)}, u32[]{:S(2)}) %collective-permute-start.12) | collective-permute-done | bytes 81952 | tf_op jit(solution)/shard_map/ppermute | solution.py:43
  72.6 0.1 collective-permute-start.13
  72.7 0.0 collective-permute-done.4.refs_1_
  72.7 0.0 collective-permute-done.3.refs_0_
  72.7 2.0 %shard_map.71.gamma_in = f32[512,2048]{1,0:T(8,128)S(1)} custom-call(s32[3,1,8]{2,1,0:T(1,128)S(1)} %bitcast.22, s32[1,8]{1,0:T(1,128)S(1)} %copy-done.5, bf16[512,2048]{1,0:T(8,128)(2,1)S(1)} %bitcast.16, f32[512,512]{1,0:T(8,128)S(1)} %get-tuple-element.10.over_ref, f32[512,2048]{1,0:T(8,128)S(1)} %shard_map.70.gamma_in, ...), custom_call_target="tpu_custom_call" | custom-call | flops 1073741824 | bytes 1048576 | tf_op jit(solution)/shard_map/pallas_call | solution.py:203
  74.8 0.0 collective-permute-done.5.refs_0_
  74.8 0.0 collective-permute-done.6.refs_1_
  74.8 3.0 %shard_map.72 = bf16[512,2048]{1,0:T(8,128)(2,1)} custom-call(s32[3,1,8]{2,1,0:T(1,128)S(1)} %bitcast.23, s32[1,8]{1,0:T(1,128)S(1)} %copy-done.5, bf16[512,2048]{1,0:T(8,128)(2,1)S(1)} %bitcast.17, f32[512,512]{1,0:T(8,128)S(1)} %get-tuple-element.10.over_ref, f32[512,2048]{1,0:T(8,128)S(1)} %shard_map.71.gamma_in, ...), custom_call_target="tpu_custom_call" | custom-call | flops 1073741824 | bytes 1048576 | tf_op jit(solution)/shard_map/pallas_call | solution.py:203
  77.8 0.0 collective-permute-done.13.other_ref
  77.8 2.1 %shard_map.73 = bf16[512,2048]{1,0:T(8,128)(2,1)} custom-call(bf16[640,128]{1,0:T(8,128)(2,1)S(1)} %pad_maximum_fusion.mine_ref, bf16[640,128]{1,0:T(8,128)(2,1)S(1)} %collective-permute-done.13.other_ref, bf16[512,2048]{1,0:T(8,128)(2,1)S(1)} %bitcast.18), custom_call_target="tpu_custom_call" | custom-call | flops 1073741824 | bytes 1048576 | tf_op jit(solution)/shard_map/pallas_call | solution.py:203
  (11 shorter events, 0.2 us)
Async XLA Ops:
  0.6 35.2 %collective-permute-start.2 = (bf16[512,2048]{1,0:T(8,128)(2,1)}, bf16[512,2048]{1,0:T(8,128)(2,1)S(1)}, u32[]{:S(2)}, u32[]{:S(2)}) collective-permute-start(bf16[512,2048]{1,0:T(8,128)(2,1)} %bitcast.13), channel_id=1, source_target_pairs={{0,1},{1,3},{2,0},{3,2},{4,5},{5,7},{6,4},{7,6},{8,9},{9,11},{10,8... | collective-permute-start | bytes 6291464 | tf_op jit(solution)/shard_map/ppermute | solution.py:33
  1.2 26.9 %collective-permute-start = (bf16[1]{0:T(256)(128)(2,1)}, bf16[1]{0:T(256)(128)(2,1)}, u32[]{:S(2)}, u32[]{:S(2)}) collective-permute-start(bf16[1]{0:T(256)(128)(2,1)} %param.6), channel_id=1, source_target_pairs={{0,1},{1,3},{2,0},{3,2},{4,5},{5,7},{6,4},{7,6},{8,9},{9,11},{10,8... | collective-permute-start | bytes 14 | tf_op jit(solution)/shard_map/ppermute | solution.py:33
  3.3 25.4 %collective-permute-start.1 = (bf16[1]{0:T(256)(128)(2,1)}, bf16[1]{0:T(256)(128)(2,1)}, u32[]{:S(2)}, u32[]{:S(2)}) collective-permute-start(bf16[1]{0:T(256)(128)(2,1)} %param.6), channel_id=1, source_target_pairs={{1,0},{3,1},{0,2},{2,3},{5,4},{7,5},{4,6},{6,7},{9,8},{11,9},{8,10... | collective-permute-start | bytes 14 | tf_op jit(solution)/shard_map/ppermute | solution.py:33
  29.4 1.6 %copy-start = (bf16[1,512,2048]{2,1,0:T(8,128)(2,1)S(1)}, bf16[1,512,2048]{2,1,0:T(8,128)(2,1)}, u32[]{:S(2)}) copy-start(bf16[1,512,2048]{2,1,0:T(8,128)(2,1)} %param.5) | copy-start | bytes 6291460
  31.0 0.7 copy-start.2
  31.7 0.7 copy-start.4
  35.8 6.0 %copy-start.1 = (bf16[1,512,2048]{2,1,0:T(8,128)(2,1)S(1)}, bf16[1,512,2048]{2,1,0:T(8,128)(2,1)}, u32[]{:S(2)}) copy-start(bf16[1,512,2048]{2,1,0:T(8,128)(2,1)} %param.5) | copy-start | bytes 6291460
  38.3 1.5 %collective-permute-start.7 = (bf16[640,128]{1,0:T(8,128)(2,1)S(1)}, bf16[640,128]{1,0:T(8,128)(2,1)S(1)}, u32[]{:S(2)}, u32[]{:S(2)}) collective-permute-start(bf16[640,128]{1,0:T(8,128)(2,1)S(1)} %get-tuple-element.17), channel_id=1, source_target_pairs={{0,1},{1,0},{2,3},{3,2},{4,5},{5,4},{6,7},{7,6},{8,9},{9,8},{10,11... | collective-permute-start | bytes 491528 | tf_op jit(solution)/shard_map/ppermute | solution.py:43
  39.8 4.5 %collective-permute-start.8 = (bf16[320,128]{1,0:T(8,128)(2,1)S(1)}, bf16[320,128]{1,0:T(8,128)(2,1)S(1)}, u32[]{:S(2)}, u32[]{:S(2)}) collective-permute-start(bf16[320,128]{1,0:T(8,128)(2,1)S(1)} %get-tuple-element.20), channel_id=1, source_target_pairs={{0,8},{1,17},{2,18},{3,11},{4,12},{5,21},{6,22},{7,15},{8,0},{9,25... | collective-permute-start | bytes 245768 | tf_op jit(solution)/shard_map/ppermute | solution.py:43
  41.9 30.8 %collective-permute-start.3 = (bf16[224,2048]{1,0:T(8,128)(2,1)S(1)}, bf16[224,2048]{1,0:T(8,128)(2,1)S(1)}, u32[]{:S(2)}, u32[]{:S(2)}) collective-permute-start(bf16[224,2048]{1,0:T(8,128)(2,1)S(1)} %slice_bitcast_fusion), channel_id=1, source_target_pairs={{1,0},{3,1},{0,2},{2,3},{5,4},{7,5},{4,6},{6,7},{9,8},{11,9},{8,10... | collective-permute-start | bytes 2752520 | tf_op jit(solution)/shard_map/ppermute | solution.py:33
  44.3 25.3 %copy-start.3 = (s32[1,8,3]{1,0,2:T(1,128)S(1)}, s32[1,8,3]{1,0,2:T(1,128)}, u32[]{:S(2)}) copy-start(s32[1,8,3]{1,0,2:T(1,128)} %param.8) | copy-start | bytes 292
  44.3 25.3 %copy-start.5 = (s32[1,8]{1,0:T(1,128)S(1)}, s32[1,8]{1,0:T(1,128)}, u32[]{:S(2)}) copy-start(s32[1,8]{1,0:T(1,128)} %counts.9) | copy-start | bytes 100
  44.4 14.6 %collective-permute-start.9 = (bf16[320,128]{1,0:T(8,128)(2,1)S(1)}, bf16[320,128]{1,0:T(8,128)(2,1)S(1)}, u32[]{:S(2)}, u32[]{:S(2)}) collective-permute-start(bf16[320,128]{1,0:T(8,128)(2,1)S(1)} %get-tuple-element.18), channel_id=1, source_target_pairs={{0,7},{1,6},{2,5},{3,4},{4,3},{5,2},{6,1},{7,0},{8,15},{9,14},{10,... | collective-permute-start | bytes 245768 | tf_op jit(solution)/shard_map/ppermute | solution.py:43
  45.9 26.8 %collective-permute-start.4 = (bf16[32,2048]{1,0:T(8,128)(2,1)S(1)}, bf16[32,2048]{1,0:T(8,128)(2,1)S(1)}, u32[]{:S(2)}, u32[]{:S(2)}) collective-permute-start(bf16[32,2048]{1,0:T(8,128)(2,1)S(1)} %slice_bitcast_fusion.3), channel_id=1, source_target_pairs={{1,0},{3,1},{0,2},{2,3},{5,4},{7,5},{4,6},{6,7},{9,8},{11,9},{8,10... | collective-permute-start | bytes 393224 | tf_op jit(solution)/shard_map/ppermute | solution.py:33
  59.0 3.9 %collective-permute-start.10 = (bf16[320,128]{1,0:T(8,128)(2,1)S(1)}, bf16[320,128]{1,0:T(8,128)(2,1)S(1)}, u32[]{:S(2)}, u32[]{:S(2)}) collective-permute-start(bf16[320,128]{1,0:T(8,128)(2,1)S(1)} %fusion), channel_id=1, source_target_pairs={{0,3},{1,2},{2,1},{3,0},{4,7},{5,6},{6,5},{7,4},{8,11},{9,10},{10,... | collective-permute-start | bytes 245768 | tf_op jit(solution)/shard_map/ppermute | solution.py:43
  59.1 15.7 %collective-permute-start.5 = (bf16[80,2048]{1,0:T(8,128)(2,1)S(1)}, bf16[80,2048]{1,0:T(8,128)(2,1)S(1)}, u32[]{:S(2)}, u32[]{:S(2)}) collective-permute-start(bf16[80,2048]{1,0:T(8,128)(2,1)S(1)} %slice_bitcast_fusion.2), channel_id=1, source_target_pairs={{1,0},{3,1},{0,2},{2,3},{5,4},{7,5},{4,6},{6,7},{9,8},{11,9},{8,10... | collective-permute-start | bytes 983048 | tf_op jit(solution)/shard_map/ppermute | solution.py:33
  62.9 5.1 %collective-permute-start.11 = (bf16[320,128]{1,0:T(8,128)(2,1)S(1)}, bf16[320,128]{1,0:T(8,128)(2,1)S(1)}, u32[]{:S(2)}, u32[]{:S(2)}) collective-permute-start(bf16[320,128]{1,0:T(8,128)(2,1)S(1)} %fusion.1), channel_id=1, source_target_pairs={{0,16},{1,9},{2,10},{3,19},{4,20},{5,13},{6,14},{7,23},{8,24},{9,1... | collective-permute-start | bytes 245768 | tf_op jit(solution)/shard_map/ppermute | solution.py:43
  63.6 11.2 %collective-permute-start.6 = (bf16[176,2048]{1,0:T(8,128)(2,1)S(1)}, bf16[176,2048]{1,0:T(8,128)(2,1)S(1)}, u32[]{:S(2)}, u32[]{:S(2)}) collective-permute-start(bf16[176,2048]{1,0:T(8,128)(2,1)S(1)} %slice_bitcast_fusion.1), channel_id=1, source_target_pairs={{1,0},{3,1},{0,2},{2,3},{5,4},{7,5},{4,6},{6,7},{9,8},{11,9},{8,10... | collective-permute-start | bytes 2162696 | tf_op jit(solution)/shard_map/ppermute | solution.py:33
  68.1 4.5 %collective-permute-start.12 = (bf16[320,128]{1,0:T(8,128)(2,1)S(1)}, bf16[320,128]{1,0:T(8,128)(2,1)S(1)}, u32[]{:S(2)}, u32[]{:S(2)}) collective-permute-start(bf16[320,128]{1,0:T(8,128)(2,1)S(1)} %multiply_convert_fusion), channel_id=1, source_target_pairs={{0,8},{1,17},{2,18},{3,11},{4,12},{5,21},{6,22},{7,15},{8,0},{9,25... | collective-permute-start | bytes 245768 | tf_op jit(solution)/shard_map/ppermute | solution.py:43
  72.6 5.2 %collective-permute-start.13 = (bf16[640,128]{1,0:T(8,128)(2,1)S(1)}, bf16[640,128]{1,0:T(8,128)(2,1)S(1)}, u32[]{:S(2)}, u32[]{:S(2)}) collective-permute-start(bf16[640,128]{1,0:T(8,128)(2,1)S(1)} %pad_maximum_fusion.mine_ref), channel_id=1, source_target_pairs={{0,1},{1,0},{2,3},{3,2},{4,5},{5,4},{6,7},{7,6},{8,9},{9,8},{10,11... | collective-permute-start | bytes 491528 | tf_op jit(solution)/shard_map/ppermute | solution.py:43

commit v3 on v0

--- a/solution.py
+++ b/solution.py
@@ -255,17 +255,17 @@
     below, above = total[: half // 2], total[half // 2 :]
     got = swap(jnp.where(upper, below, above).astype(BF16), split)
     total = jnp.where(upper, above, below) + got.astype(F32)
+    for mask in along[1:] + along[:1]:
+        total = total + swap(total.astype(BF16), [mask, mask]).astype(F32)
     for masks in later:
         total = total + swap(total.astype(BF16), masks).astype(F32)
-    for mask in along:
-        total = total + swap(total.astype(BF16), [mask, mask]).astype(F32)
     mine = (total * (1.0 / (8.0 * groups * members))).astype(BF16)
     got = swap(mine, split)
     mine = jnp.concatenate([jnp.where(upper, got, mine), jnp.where(upper, mine, got)])
     other = swap(mine, [(0, 1), (0, 1)])
 
     unit = vir // 16
-    cuts = (0, 8 * unit, 10 * unit, 13 * unit, vir)
+    cuts = (0, 8 * unit, 10 * unit, vir)
     parts = [block[a:b] for a, b in zip(cuts, cuts[1:])]
     second = [turn(part, True) for part in parts]
     gamma = call(first_gamma_kernel, wide, (), (0, 1), 5, dot)(
@@ -277,7 +277,7 @@
     )
     result = call(
         last_gamma_kernel, shape((vir, aux), BF16), [*out_scratch, pltpu.VMEM((vir // 2, aux), BF16), *bounce],
-        (0, 1), 8, dot, any_space,
+        (0, 1), 5 + len(second) - 1, dot, any_space,
     )(pair_code, pair_count, block, over_second, gamma, *second[1:])
     lagrangian = call(
         apply_kernel, shape((vir, aux), BF16), [pltpu.VMEM((vir, vir), BF16), *out_scratch], (), 3, dot,

time: 81.2 us -> 80.5 us (level)
    ppermute x7 -> x6, waiting for transfers between devices: 24.1 us -> 22.9 us  [turn(): return lax.ppermute(value, 'mem', pairs)]
    ppermute x7, starting transfers between devices: 9.22 us -> 8.37 us  [swap(): return lax.ppermute(value, ('grp', 'mem'), pairs)]
    ppermute x7 -> x6, starting transfers between devices: 3.93 us -> 4.66 us  [turn(): return lax.ppermute(value, 'mem', pairs)]
  transfers between devices with their start and end apart: 14 -> 13, of which waited for: 8 -> 8; matrix products, arithmetic and copies ran while one was open for 1% -> 1% of each run, Pallas kernels for 13% -> 13%
where the time goes in v3:
time: 80.5 us; the launch traced here: 80.2 us
  waiting for transfers between devices  45.6 us (57%)
  Pallas kernels  14.8 us (18%)
  starting transfers between devices  13 us (16%)
  local copies, waits for them, and re-layouts  3.09 us (4%)
  between operations  2.78 us (3%)
  other arithmetic  0.94 us (1%)
    ppermute x6, waiting for transfers between devices, turn(): return lax.ppermute(value, 'mem', pairs)  22.9 us
    ppermute x7, waiting for transfers between devices, swap(): return lax.ppermute(value, ('grp', 'mem'), pairs)  22.6 us
    pallas_call x6, Pallas kernels, call(): kernel_call(kernel, outs, scratch, smem, count, flops, out_spec)(*args)  14.8 us
    ppermute x7, starting transfers between devices, swap(): return lax.ppermute(value, ('grp', 'mem'), pairs)  8.37 us
    ppermute x6, starting transfers between devices, turn(): return lax.ppermute(value, 'mem', pairs)  4.66 us
    unnamed x12, local copies, waits for them, and re-layouts  2.94 us
  transfers between devices with their start and end apart: 13, of which 8 were waited for; matrix products, arithmetic and copies ran while one was open for 1% of the time, Pallas kernels for 13%

profile of v3, /device:TPU:0, one launch (start us, length us, event | category | flops | bytes accessed | tf_op | source)
XLA Modules:
  0.0 80.2 jit_solution(12544376760078673064)
XLA Ops:
  0.6 0.6 collective-permute-start.2
  1.2 2.1 %collective-permute-start = (bf16[1]{0:T(256)(128)(2,1)}, bf16[1]{0:T(256)(128)(2,1)}, u32[]{:S(2)}, u32[]{:S(2)}) collective-permute-start(bf16[1]{0:T(256)(128)(2,1)} %param.6), channel_id=1, source_target_pairs={{0,1},{1,3},{2,0},{3,2},{4,5},{5,7},{6,4},{7,6},{8,9},{9,11},{10,8... | collective-permute-start | bytes 14 | tf_op jit(solution)/shard_map/ppermute | solution.py:33
  3.3 0.6 collective-permute-start.1
  4.6 0.7 reshape.14
  5.3 22.7 %collective-permute-done = bf16[1]{0:T(256)(128)(2,1)} collective-permute-done((bf16[1]{0:T(256)(128)(2,1)}, bf16[1]{0:T(256)(128)(2,1)}, u32[]{:S(2)}, u32[]{:S(2)}) %collective-permute-start) | collective-permute-done | bytes 34 | tf_op jit(solution)/shard_map/ppermute | solution.py:33
  28.6 0.0 collective-permute-done.1
  29.3 0.0 copy-start
  29.3 1.6 %copy-done = bf16[1,512,2048]{2,1,0:T(8,128)(2,1)S(1)} copy-done((bf16[1,512,2048]{2,1,0:T(8,128)(2,1)S(1)}, bf16[1,512,2048]{2,1,0:T(8,128)(2,1)}, u32[]{:S(2)}) %copy-start) | copy-done | bytes 2097176
  30.9 0.0 copy-start.2
  30.9 0.7 copy-done.2
  31.6 0.0 copy-start.4
  31.6 0.7 copy-done.4
  32.2 3.4 %shard_map.68 = (f32[512,512]{1,0:T(8,128)S(1)}, f32[512,512]{1,0:T(8,128)S(1)}, f32[512,512]{1,0:T(8,128)S(1)}, f32[512,2048]{1,0:T(8,128)S(1)}, f32[320,128]{1,0:T(8,128)S(1)}) custom-call(bf16[512,2048]{1,0:T(8,128)(2,1)S(1)} %bitcast.12, f32[1,512]{1,0:T(1,128)S(1)} %bitcast.22, f32[1]{0:T(128)S(6)} %convert_element_type.40.e_ref, ...), custom_call_target="tpu_custom_call" | custom-call | flops 2147483648 | bytes 1048576 | tf_op jit(solution)/shard_map/pallas_call | solution.py:201
  35.7 0.0 collective-permute-done.2.r_ref
  35.7 0.0 copy-start.1
  35.7 2.5 %shard_map.69 = (bf16[512,512]{1,0:T(8,128)(2,1)S(1)}, f32[640,128]{1,0:T(8,128)S(1)}, bf16[640,128]{1,0:T(8,128)(2,1)S(1)}) custom-call(bf16[512,2048]{1,0:T(8,128)(2,1)S(1)} %bitcast.13, bf16[512,2048]{1,0:T(8,128)(2,1)S(1)} %collective-permute-done.2.r_ref, f32[512,512]{1,0:T(8,128)S(1)} %get-tuple-element.12.over_ref, s32[3,1,8]{2,1,0:T(1,128)S(1)} %bitcast.18, ...), custom_call_target="tpu_custom_call" | custom-call | flops 1073741824 | bytes 1048576 | tf_op jit(solution)/shard_map/pallas_call | solution.py:201
  38.2 0.1 collective-permute-start.6
  38.2 1.4 %collective-permute-done.6 = bf16[640,128]{1,0:T(8,128)(2,1)S(1)} collective-permute-done((bf16[640,128]{1,0:T(8,128)(2,1)S(1)}, bf16[640,128]{1,0:T(8,128)(2,1)S(1)}, u32[]{:S(2)}, u32[]{:S(2)}) %collective-permute-start.6) | collective-permute-done | bytes 163872 | tf_op jit(solution)/shard_map/ppermute | solution.py:43
  39.7 2.0 %collective-permute-start.7 = (bf16[320,128]{1,0:T(8,128)(2,1)S(1)}, bf16[320,128]{1,0:T(8,128)(2,1)S(1)}, u32[]{:S(2)}, u32[]{:S(2)}) collective-permute-start(bf16[320,128]{1,0:T(8,128)(2,1)S(1)} %get-tuple-element.20), channel_id=1, source_target_pairs={{0,8},{1,17},{2,18},{3,11},{4,12},{5,21},{6,22},{7,15},{8,0},{9,25... | collective-permute-start | bytes 245768 | tf_op jit(solution)/shard_map/ppermute | solution.py:43
  41.7 2.5 %collective-permute-done.7 = bf16[320,128]{1,0:T(8,128)(2,1)S(1)} collective-permute-done((bf16[320,128]{1,0:T(8,128)(2,1)S(1)}, bf16[320,128]{1,0:T(8,128)(2,1)S(1)}, u32[]{:S(2)}, u32[]{:S(2)}) %collective-permute-start.7) | collective-permute-done | bytes 81952 | tf_op jit(solution)/shard_map/ppermute | solution.py:43
  44.2 1.6 %collective-permute-start.8 = (bf16[320,128]{1,0:T(8,128)(2,1)S(1)}, bf16[320,128]{1,0:T(8,128)(2,1)S(1)}, u32[]{:S(2)}, u32[]{:S(2)}) collective-permute-start(bf16[320,128]{1,0:T(8,128)(2,1)S(1)} %get-tuple-element.18), channel_id=1, source_target_pairs={{0,7},{1,6},{2,5},{3,4},{4,3},{5,2},{6,1},{7,0},{8,15},{9,14},{10,... | collective-permute-start | bytes 245768 | tf_op jit(solution)/shard_map/ppermute | solution.py:43
  45.9 0.0 copy-done.1
  45.9 0.1 slice_bitcast_fusion
  45.9 0.0 copy-start.3
  45.9 0.0 copy-start.5
  46.0 1.0 %collective-permute-start.3 = (bf16[256,2048]{1,0:T(8,128)(2,1)S(1)}, bf16[256,2048]{1,0:T(8,128)(2,1)S(1)}, u32[]{:S(2)}, u32[]{:S(2)}) collective-permute-start(bf16[256,2048]{1,0:T(8,128)(2,1)S(1)} %slice_bitcast_fusion), channel_id=1, source_target_pairs={{1,0},{3,1},{0,2},{2,3},{5,4},{7,5},{4,6},{6,7},{9,8},{11,9},{8,10... | collective-permute-start | bytes 3145736 | tf_op jit(solution)/shard_map/ppermute | solution.py:33
  47.0 3.7 %collective-permute-done.8 = bf16[320,128]{1,0:T(8,128)(2,1)S(1)} collective-permute-done((bf16[320,128]{1,0:T(8,128)(2,1)S(1)}, bf16[320,128]{1,0:T(8,128)(2,1)S(1)}, u32[]{:S(2)}, u32[]{:S(2)}) %collective-permute-start.8) | collective-permute-done | bytes 81952 | tf_op jit(solution)/shard_map/ppermute | solution.py:43
  50.7 1.1 %collective-permute-start.9 = (bf16[320,128]{1,0:T(8,128)(2,1)S(1)}, bf16[320,128]{1,0:T(8,128)(2,1)S(1)}, u32[]{:S(2)}, u32[]{:S(2)}) collective-permute-start(bf16[320,128]{1,0:T(8,128)(2,1)S(1)} %fusion), channel_id=1, source_target_pairs={{0,3},{1,2},{2,1},{3,0},{4,7},{5,6},{6,5},{7,4},{8,11},{9,10},{10,... | collective-permute-start | bytes 245768 | tf_op jit(solution)/shard_map/ppermute | solution.py:43
  51.8 0.3 collective-permute-start.4
  52.1 11.5 %collective-permute-done.9 = bf16[320,128]{1,0:T(8,128)(2,1)S(1)} collective-permute-done((bf16[320,128]{1,0:T(8,128)(2,1)S(1)}, bf16[320,128]{1,0:T(8,128)(2,1)S(1)}, u32[]{:S(2)}, u32[]{:S(2)}) %collective-permute-start.9) | collective-permute-done | bytes 81952 | tf_op jit(solution)/shard_map/ppermute | solution.py:43
  63.6 1.8 %collective-permute-start.10 = (bf16[320,128]{1,0:T(8,128)(2,1)S(1)}, bf16[320,128]{1,0:T(8,128)(2,1)S(1)}, u32[]{:S(2)}, u32[]{:S(2)}) collective-permute-start(bf16[320,128]{1,0:T(8,128)(2,1)S(1)} %fusion.1), channel_id=1, source_target_pairs={{0,16},{1,9},{2,10},{3,19},{4,20},{5,13},{6,14},{7,23},{8,24},{9,1... | collective-permute-start | bytes 245768 | tf_op jit(solution)/shard_map/ppermute | solution.py:43
  65.5 0.1 slice_bitcast_fusion.1
  65.5 0.1 collective-permute-start.5
  65.6 2.6 %collective-permute-done.10 = bf16[320,128]{1,0:T(8,128)(2,1)S(1)} collective-permute-done((bf16[320,128]{1,0:T(8,128)(2,1)S(1)}, bf16[320,128]{1,0:T(8,128)(2,1)S(1)}, u32[]{:S(2)}, u32[]{:S(2)}) %collective-permute-start.10) | collective-permute-done | bytes 81952 | tf_op jit(solution)/shard_map/ppermute | solution.py:43
  68.2 0.1 multiply_convert_fusion
  68.3 1.7 %collective-permute-start.11 = (bf16[320,128]{1,0:T(8,128)(2,1)S(1)}, bf16[320,128]{1,0:T(8,128)(2,1)S(1)}, u32[]{:S(2)}, u32[]{:S(2)}) collective-permute-start(bf16[320,128]{1,0:T(8,128)(2,1)S(1)} %multiply_convert_fusion), channel_id=1, source_target_pairs={{0,8},{1,17},{2,18},{3,11},{4,12},{5,21},{6,22},{7,15},{8,0},{9,25... | collective-permute-start | bytes 245768 | tf_op jit(solution)/shard_map/ppermute | solution.py:43
  70.0 0.0 copy-done.3
  70.0 0.0 copy-done.5
  70.0 1.8 %shard_map.70.gamma_in = f32[512,2048]{1,0:T(8,128)S(1)} custom-call(s32[3,1,8]{2,1,0:T(1,128)S(1)} %bitcast.19, s32[1,8]{1,0:T(1,128)S(1)} %copy-done.5, f32[512,2048]{1,0:T(8,128)S(1)} %get-tuple-element.11.gamma_in, bf16[512,512]{1,0:T(8,128)(2,1)S(1)} %get-tuple-element.14.mt_ref, bf16[512,2048]{1,0:T(8,128)(2,1)S(1)} %collective-permute-done.2.r_ref), custom_call_target="tpu_custom_call" | custom-call | flops 1073741824 | bytes 1048576 | tf_op jit(solution)/shard_map/pallas_call | solution.py:201
  71.8 0.9 %collective-permute-done.11 = bf16[320,128]{1,0:T(8,128)(2,1)S(1)} collective-permute-done((bf16[320,128]{1,0:T(8,128)(2,1)S(1)}, bf16[320,128]{1,0:T(8,128)(2,1)S(1)}, u32[]{:S(2)}, u32[]{:S(2)}) %collective-permute-start.11) | collective-permute-done | bytes 81952 | tf_op jit(solution)/shard_map/ppermute | solution.py:43
  72.8 0.1 collective-permute-start.12
  72.9 0.0 collective-permute-done.3.r_ref
  72.9 2.0 %shard_map.71.gamma_in = f32[512,2048]{1,0:T(8,128)S(1)} custom-call(s32[3,1,8]{2,1,0:T(1,128)S(1)} %bitcast.20, s32[1,8]{1,0:T(1,128)S(1)} %copy-done.5, bf16[512,2048]{1,0:T(8,128)(2,1)S(1)} %bitcast.14, f32[512,512]{1,0:T(8,128)S(1)} %get-tuple-element.10.over_ref, f32[512,2048]{1,0:T(8,128)S(1)} %shard_map.70.gamma_in, ...), custom_call_target="tpu_custom_call" | custom-call | flops 1073741824 | bytes 1048576 | tf_op jit(solution)/shard_map/pallas_call | solution.py:201
  75.0 0.0 collective-permute-done.4.refs_0_
  75.0 0.2 collective-permute-done.5.refs_1_
  75.1 3.0 %shard_map.72 = bf16[512,2048]{1,0:T(8,128)(2,1)} custom-call(s32[3,1,8]{2,1,0:T(1,128)S(1)} %bitcast.21, s32[1,8]{1,0:T(1,128)S(1)} %copy-done.5, bf16[512,2048]{1,0:T(8,128)(2,1)S(1)} %bitcast.15, f32[512,512]{1,0:T(8,128)S(1)} %get-tuple-element.10.over_ref, f32[512,2048]{1,0:T(8,128)S(1)} %shard_map.71.gamma_in, ...), custom_call_target="tpu_custom_call" | custom-call | flops 1073741824 | bytes 1048576 | tf_op jit(solution)/shard_map/pallas_call | solution.py:201
  78.1 0.0 collective-permute-done.12.other_ref
  78.1 2.1 %shard_map.73 = bf16[512,2048]{1,0:T(8,128)(2,1)} custom-call(bf16[640,128]{1,0:T(8,128)(2,1)S(1)} %pad_maximum_fusion.mine_ref, bf16[640,128]{1,0:T(8,128)(2,1)S(1)} %collective-permute-done.12.other_ref, bf16[512,2048]{1,0:T(8,128)(2,1)S(1)} %bitcast.16), custom_call_target="tpu_custom_call" | custom-call | flops 1073741824 | bytes 1048576 | tf_op jit(solution)/shard_map/pallas_call | solution.py:201
  (8 shorter events, 0.2 us)
Async XLA Ops:
  0.6 35.0 %collective-permute-start.2 = (bf16[512,2048]{1,0:T(8,128)(2,1)}, bf16[512,2048]{1,0:T(8,128)(2,1)S(1)}, u32[]{:S(2)}, u32[]{:S(2)}) collective-permute-start(bf16[512,2048]{1,0:T(8,128)(2,1)} %bitcast.11), channel_id=1, source_target_pairs={{0,1},{1,3},{2,0},{3,2},{4,5},{5,7},{6,4},{7,6},{8,9},{9,11},{10,8... | collective-permute-start | bytes 6291464 | tf_op jit(solution)/shard_map/ppermute | solution.py:33
  1.2 26.8 %collective-permute-start = (bf16[1]{0:T(256)(128)(2,1)}, bf16[1]{0:T(256)(128)(2,1)}, u32[]{:S(2)}, u32[]{:S(2)}) collective-permute-start(bf16[1]{0:T(256)(128)(2,1)} %param.6), channel_id=1, source_target_pairs={{0,1},{1,3},{2,0},{3,2},{4,5},{5,7},{6,4},{7,6},{8,9},{9,11},{10,8... | collective-permute-start | bytes 14 | tf_op jit(solution)/shard_map/ppermute | solution.py:33
  3.3 25.4 %collective-permute-start.1 = (bf16[1]{0:T(256)(128)(2,1)}, bf16[1]{0:T(256)(128)(2,1)}, u32[]{:S(2)}, u32[]{:S(2)}) collective-permute-start(bf16[1]{0:T(256)(128)(2,1)} %param.6), channel_id=1, source_target_pairs={{1,0},{3,1},{0,2},{2,3},{5,4},{7,5},{4,6},{6,7},{9,8},{11,9},{8,10... | collective-permute-start | bytes 14 | tf_op jit(solution)/shard_map/ppermute | solution.py:33
  29.3 1.6 %copy-start = (bf16[1,512,2048]{2,1,0:T(8,128)(2,1)S(1)}, bf16[1,512,2048]{2,1,0:T(8,128)(2,1)}, u32[]{:S(2)}) copy-start(bf16[1,512,2048]{2,1,0:T(8,128)(2,1)} %param.5) | copy-start | bytes 6291460
  30.9 0.7 copy-start.2
  31.6 0.7 copy-start.4
  35.7 10.2 %copy-start.1 = (bf16[1,512,2048]{2,1,0:T(8,128)(2,1)S(1)}, bf16[1,512,2048]{2,1,0:T(8,128)(2,1)}, u32[]{:S(2)}) copy-start(bf16[1,512,2048]{2,1,0:T(8,128)(2,1)} %param.5) | copy-start | bytes 6291460
  38.2 1.5 %collective-permute-start.6 = (bf16[640,128]{1,0:T(8,128)(2,1)S(1)}, bf16[640,128]{1,0:T(8,128)(2,1)S(1)}, u32[]{:S(2)}, u32[]{:S(2)}) collective-permute-start(bf16[640,128]{1,0:T(8,128)(2,1)S(1)} %get-tuple-element.17), channel_id=1, source_target_pairs={{0,1},{1,0},{2,3},{3,2},{4,5},{5,4},{6,7},{7,6},{8,9},{9,8},{10,11... | collective-permute-start | bytes 491528 | tf_op jit(solution)/shard_map/ppermute | solution.py:43
  39.7 4.5 %collective-permute-start.7 = (bf16[320,128]{1,0:T(8,128)(2,1)S(1)}, bf16[320,128]{1,0:T(8,128)(2,1)S(1)}, u32[]{:S(2)}, u32[]{:S(2)}) collective-permute-start(bf16[320,128]{1,0:T(8,128)(2,1)S(1)} %get-tuple-element.20), channel_id=1, source_target_pairs={{0,8},{1,17},{2,18},{3,11},{4,12},{5,21},{6,22},{7,15},{8,0},{9,25... | collective-permute-start | bytes 245768 | tf_op jit(solution)/shard_map/ppermute | solution.py:43
  44.2 6.5 %collective-permute-start.8 = (bf16[320,128]{1,0:T(8,128)(2,1)S(1)}, bf16[320,128]{1,0:T(8,128)(2,1)S(1)}, u32[]{:S(2)}, u32[]{:S(2)}) collective-permute-start(bf16[320,128]{1,0:T(8,128)(2,1)S(1)} %get-tuple-element.18), channel_id=1, source_target_pairs={{0,7},{1,6},{2,5},{3,4},{4,3},{5,2},{6,1},{7,0},{8,15},{9,14},{10,... | collective-permute-start | bytes 245768 | tf_op jit(solution)/shard_map/ppermute | solution.py:43
  45.9 24.1 %copy-start.3 = (s32[1,8,3]{1,0,2:T(1,128)S(1)}, s32[1,8,3]{1,0,2:T(1,128)}, u32[]{:S(2)}) copy-start(s32[1,8,3]{1,0,2:T(1,128)} %param.8) | copy-start | bytes 292
  45.9 24.1 %copy-start.5 = (s32[1,8]{1,0:T(1,128)S(1)}, s32[1,8]{1,0:T(1,128)}, u32[]{:S(2)}) copy-start(s32[1,8]{1,0:T(1,128)} %counts.9) | copy-start | bytes 100
  46.0 26.9 %collective-permute-start.3 = (bf16[256,2048]{1,0:T(8,128)(2,1)S(1)}, bf16[256,2048]{1,0:T(8,128)(2,1)S(1)}, u32[]{:S(2)}, u32[]{:S(2)}) collective-permute-start(bf16[256,2048]{1,0:T(8,128)(2,1)S(1)} %slice_bitcast_fusion), channel_id=1, source_target_pairs={{1,0},{3,1},{0,2},{2,3},{5,4},{7,5},{4,6},{6,7},{9,8},{11,9},{8,10... | collective-permute-start | bytes 3145736 | tf_op jit(solution)/shard_map/ppermute | solution.py:33
  50.7 12.9 %collective-permute-start.9 = (bf16[320,128]{1,0:T(8,128)(2,1)S(1)}, bf16[320,128]{1,0:T(8,128)(2,1)S(1)}, u32[]{:S(2)}, u32[]{:S(2)}) collective-permute-start(bf16[320,128]{1,0:T(8,128)(2,1)S(1)} %fusion), channel_id=1, source_target_pairs={{0,3},{1,2},{2,1},{3,0},{4,7},{5,6},{6,5},{7,4},{8,11},{9,10},{10,... | collective-permute-start | bytes 245768 | tf_op jit(solution)/shard_map/ppermute | solution.py:43
  51.8 23.1 %collective-permute-start.4 = (bf16[64,2048]{1,0:T(8,128)(2,1)S(1)}, bf16[64,2048]{1,0:T(8,128)(2,1)S(1)}, u32[]{:S(2)}, u32[]{:S(2)}) collective-permute-start(bf16[64,2048]{1,0:T(8,128)(2,1)S(1)} %slice_bitcast_fusion.2), channel_id=1, source_target_pairs={{1,0},{3,1},{0,2},{2,3},{5,4},{7,5},{4,6},{6,7},{9,8},{11,9},{8,10... | collective-permute-start | bytes 786440 | tf_op jit(solution)/shard_map/ppermute | solution.py:33
  63.6 4.6 %collective-permute-start.10 = (bf16[320,128]{1,0:T(8,128)(2,1)S(1)}, bf16[320,128]{1,0:T(8,128)(2,1)S(1)}, u32[]{:S(2)}, u32[]{:S(2)}) collective-permute-start(bf16[320,128]{1,0:T(8,128)(2,1)S(1)} %fusion.1), channel_id=1, source_target_pairs={{0,16},{1,9},{2,10},{3,19},{4,20},{5,13},{6,14},{7,23},{8,24},{9,1... | collective-permute-start | bytes 245768 | tf_op jit(solution)/shard_map/ppermute | solution.py:43
  65.5 9.6 %collective-permute-start.5 = (bf16[192,2048]{1,0:T(8,128)(2,1)S(1)}, bf16[192,2048]{1,0:T(8,128)(2,1)S(1)}, u32[]{:S(2)}, u32[]{:S(2)}) collective-permute-start(bf16[192,2048]{1,0:T(8,128)(2,1)S(1)} %slice_bitcast_fusion.1), channel_id=1, source_target_pairs={{1,0},{3,1},{0,2},{2,3},{5,4},{7,5},{4,6},{6,7},{9,8},{11,9},{8,10... | collective-permute-start | bytes 2359304 | tf_op jit(solution)/shard_map/ppermute | solution.py:33
  68.3 4.5 %collective-permute-start.11 = (bf16[320,128]{1,0:T(8,128)(2,1)S(1)}, bf16[320,128]{1,0:T(8,128)(2,1)S(1)}, u32[]{:S(2)}, u32[]{:S(2)}) collective-permute-start(bf16[320,128]{1,0:T(8,128)(2,1)S(1)} %multiply_convert_fusion), channel_id=1, source_target_pairs={{0,8},{1,17},{2,18},{3,11},{4,12},{5,21},{6,22},{7,15},{8,0},{9,25... | collective-permute-start | bytes 245768 | tf_op jit(solution)/shard_map/ppermute | solution.py:43
  72.8 5.3 %collective-permute-start.12 = (bf16[640,128]{1,0:T(8,128)(2,1)S(1)}, bf16[640,128]{1,0:T(8,128)(2,1)S(1)}, u32[]{:S(2)}, u32[]{:S(2)}) collective-permute-start(bf16[640,128]{1,0:T(8,128)(2,1)S(1)} %pad_maximum_fusion.mine_ref), channel_id=1, source_target_pairs={{0,1},{1,0},{2,3},{3,2},{4,5},{5,4},{6,7},{7,6},{8,9},{9,8},{10,11... | collective-permute-start | bytes 491528 | tf_op jit(solution)/shard_map/ppermute | solution.py:43

commit v4 on v3

--- a/solution.py
+++ b/solution.py
@@ -255,7 +255,13 @@
     below, above = total[: half // 2], total[half // 2 :]
     got = swap(jnp.where(upper, below, above).astype(BF16), split)
     total = jnp.where(upper, above, below) + got.astype(F32)
-    for mask in along[1:] + along[:1]:
+    out = total.astype(BF16)
+    near = [m for _, m in along[:2]]
+    masks = (near + [near[0] ^ near[1]])[::-1] if len(near) > 1 else near
+    masks = sorted(masks, key=lambda m: -(m >> 1))
+    for got in [swap(out, [(0, m), (0, m)]) for m in masks]:
+        total = total + got.astype(F32)
+    for mask in along[2:]:
         total = total + swap(total.astype(BF16), [mask, mask]).astype(F32)
     for masks in later:
         total = total + swap(total.astype(BF16), masks).astype(F32)
@@ -265,7 +271,7 @@
     other = swap(mine, [(0, 1), (0, 1)])
 
     unit = vir // 16
-    cuts = (0, 8 * unit, 10 * unit, vir)
+    cuts = (0, 8 * unit, vir)
     parts = [block[a:b] for a, b in zip(cuts, cuts[1:])]
     second = [turn(part, True) for part in parts]
     gamma = call(first_gamma_kernel, wide, (), (0, 1), 5, dot)(

time: 80.5 us -> 79.9 us (level); the launches traced: 80.2 us -> 78.7 us
  waiting for transfers between devices: 45.6 us -> 43.3 us
    ppermute x7 -> x8, waiting for transfers between devices: 22.6 us -> 13.1 us  [swap(): return lax.ppermute(value, ('grp', 'mem'), pairs)]
    ppermute x6 -> x5, waiting for transfers between devices: 22.9 us -> 30.2 us  [turn(): return lax.ppermute(value, 'mem', pairs)]
    ppermute x7 -> x8, starting transfers between devices: 8.37 us -> 9.56 us  [swap(): return lax.ppermute(value, ('grp', 'mem'), pairs)]
    ppermute x6 -> x5, starting transfers between devices: 4.66 us -> 4 us  [turn(): return lax.ppermute(value, 'mem', pairs)]
where the time goes in v4:
time: 79.9 us; the launch traced here: 78.7 us
  waiting for transfers between devices  43.3 us (54%)
  Pallas kernels  14.8 us (19%)
  starting transfers between devices  13.6 us (17%)
  local copies, waits for them, and re-layouts  3.18 us (4%)
  between operations  2.83 us (4%)
  other arithmetic  0.95 us (1%)
    ppermute x5, waiting for transfers between devices, turn(): return lax.ppermute(value, 'mem', pairs)  30.2 us
    pallas_call x6, Pallas kernels, call(): kernel_call(kernel, outs, scratch, smem, count, flops, out_spec)(*args)  14.8 us
    ppermute x8, waiting for transfers between devices, swap(): return lax.ppermute(value, ('grp', 'mem'), pairs)  13.1 us
    ppermute x8, starting transfers between devices, swap(): return lax.ppermute(value, ('grp', 'mem'), pairs)  9.56 us
    ppermute x5, starting transfers between devices, turn(): return lax.ppermute(value, 'mem', pairs)  4 us
    unnamed x12, local copies, waits for them, and re-layouts  2.94 us
  transfers between devices with their start and end apart: 13, of which 8 were waited for; matrix products, arithmetic and copies ran while one was open for 1% of the time, Pallas kernels for 13%

profile of v4, /device:TPU:0, one launch (start us, length us, event | category | flops | bytes accessed | tf_op | source)
XLA Modules:
  0.0 78.7 jit_solution(13259485442267103150)
XLA Ops:
  0.6 0.6 collective-permute-start.2
  1.2 2.1 %collective-permute-start = (bf16[1]{0:T(256)(128)(2,1)}, bf16[1]{0:T(256)(128)(2,1)}, u32[]{:S(2)}, u32[]{:S(2)}) collective-permute-start(bf16[1]{0:T(256)(128)(2,1)} %param.6), channel_id=1, source_target_pairs={{0,1},{1,3},{2,0},{3,2},{4,5},{5,7},{6,4},{7,6},{8,9},{9,11},{10,8... | collective-permute-start | bytes 14 | tf_op jit(solution)/shard_map/ppermute | solution.py:33
  3.3 0.6 collective-permute-start.1
  4.6 0.7 reshape.13
  5.3 22.8 %collective-permute-done = bf16[1]{0:T(256)(128)(2,1)} collective-permute-done((bf16[1]{0:T(256)(128)(2,1)}, bf16[1]{0:T(256)(128)(2,1)}, u32[]{:S(2)}, u32[]{:S(2)}) %collective-permute-start) | collective-permute-done | bytes 34 | tf_op jit(solution)/shard_map/ppermute | solution.py:33
  28.7 0.0 collective-permute-done.1
  29.4 0.0 copy-start
  29.4 1.6 %copy-done = bf16[1,512,2048]{2,1,0:T(8,128)(2,1)S(1)} copy-done((bf16[1,512,2048]{2,1,0:T(8,128)(2,1)S(1)}, bf16[1,512,2048]{2,1,0:T(8,128)(2,1)}, u32[]{:S(2)}) %copy-start) | copy-done | bytes 2097176
  31.0 0.0 copy-start.2
  31.0 0.7 copy-done.2
  31.7 0.0 copy-start.4
  31.7 0.7 copy-done.4
  32.4 3.4 %shard_map.68 = (f32[512,512]{1,0:T(8,128)S(1)}, f32[512,512]{1,0:T(8,128)S(1)}, f32[512,512]{1,0:T(8,128)S(1)}, f32[512,2048]{1,0:T(8,128)S(1)}, f32[320,128]{1,0:T(8,128)S(1)}) custom-call(bf16[512,2048]{1,0:T(8,128)(2,1)S(1)} %bitcast.10, f32[1,512]{1,0:T(1,128)S(1)} %bitcast.20, f32[1]{0:T(128)S(6)} %convert_element_type.40.e_ref, ...), custom_call_target="tpu_custom_call" | custom-call | flops 2147483648 | bytes 1048576 | tf_op jit(solution)/shard_map/pallas_call | solution.py:201
  35.8 0.0 collective-permute-done.2.r_ref
  35.8 0.0 copy-start.1
  35.8 2.5 %shard_map.69 = (bf16[512,512]{1,0:T(8,128)(2,1)S(1)}, f32[640,128]{1,0:T(8,128)S(1)}, bf16[640,128]{1,0:T(8,128)(2,1)S(1)}) custom-call(bf16[512,2048]{1,0:T(8,128)(2,1)S(1)} %bitcast.11, bf16[512,2048]{1,0:T(8,128)(2,1)S(1)} %collective-permute-done.2.r_ref, f32[512,512]{1,0:T(8,128)S(1)} %get-tuple-element.12.over_ref, s32[3,1,8]{2,1,0:T(1,128)S(1)} %bitcast.16, ...), custom_call_target="tpu_custom_call" | custom-call | flops 1073741824 | bytes 1048576 | tf_op jit(solution)/shard_map/pallas_call | solution.py:201
  38.3 0.1 collective-permute-start.5
  38.4 1.4 %collective-permute-done.5 = bf16[640,128]{1,0:T(8,128)(2,1)S(1)} collective-permute-done((bf16[640,128]{1,0:T(8,128)(2,1)S(1)}, bf16[640,128]{1,0:T(8,128)(2,1)S(1)}, u32[]{:S(2)}, u32[]{:S(2)}) %collective-permute-start.5) | collective-permute-done | bytes 163872 | tf_op jit(solution)/shard_map/ppermute | solution.py:43
  39.8 2.0 %collective-permute-start.6 = (bf16[320,128]{1,0:T(8,128)(2,1)S(1)}, bf16[320,128]{1,0:T(8,128)(2,1)S(1)}, u32[]{:S(2)}, u32[]{:S(2)}) collective-permute-start(bf16[320,128]{1,0:T(8,128)(2,1)S(1)} %get-tuple-element.20), channel_id=1, source_target_pairs={{0,8},{1,17},{2,18},{3,11},{4,12},{5,21},{6,22},{7,15},{8,0},{9,25... | collective-permute-start | bytes 245768 | tf_op jit(solution)/shard_map/ppermute | solution.py:43
  41.8 2.5 %collective-permute-done.6 = bf16[320,128]{1,0:T(8,128)(2,1)S(1)} collective-permute-done((bf16[320,128]{1,0:T(8,128)(2,1)S(1)}, bf16[320,128]{1,0:T(8,128)(2,1)S(1)}, u32[]{:S(2)}, u32[]{:S(2)}) %collective-permute-start.6) | collective-permute-done | bytes 81952 | tf_op jit(solution)/shard_map/ppermute | solution.py:43
  44.4 0.0 copy-start.3
  44.4 0.0 copy-start.5
  44.4 0.1 collective-permute-start.9
  44.5 3.1 %collective-permute-start.8 = (bf16[320,128]{1,0:T(8,128)(2,1)S(1)}, bf16[320,128]{1,0:T(8,128)(2,1)S(1)}, u32[]{:S(2)}, u32[]{:S(2)}) collective-permute-start(bf16[320,128]{1,0:T(8,128)(2,1)S(1)} %get-tuple-element.18), channel_id=1, source_target_pairs={{0,4},{1,5},{2,6},{3,7},{4,0},{5,1},{6,2},{7,3},{8,12},{9,13},{10,... | collective-permute-start | bytes 245768 | tf_op jit(solution)/shard_map/ppermute | solution.py:43
  47.6 1.1 %collective-permute-start.7 = (bf16[320,128]{1,0:T(8,128)(2,1)S(1)}, bf16[320,128]{1,0:T(8,128)(2,1)S(1)}, u32[]{:S(2)}, u32[]{:S(2)}) collective-permute-start(bf16[320,128]{1,0:T(8,128)(2,1)S(1)} %get-tuple-element.18), channel_id=1, source_target_pairs={{0,7},{1,6},{2,5},{3,4},{4,3},{5,2},{6,1},{7,0},{8,15},{9,14},{10,... | collective-permute-start | bytes 245768 | tf_op jit(solution)/shard_map/ppermute | solution.py:43
  48.7 0.0 copy-done.1
  48.7 0.2 slice_bitcast_fusion
  48.9 0.1 collective-permute-start.3
  49.0 0.7 collective-permute-start.4
  49.7 1.0 %collective-permute-done.9 = bf16[320,128]{1,0:T(8,128)(2,1)S(1)} collective-permute-done((bf16[320,128]{1,0:T(8,128)(2,1)S(1)}, bf16[320,128]{1,0:T(8,128)(2,1)S(1)}, u32[]{:S(2)}, u32[]{:S(2)}) %collective-permute-start.9) | collective-permute-done | bytes 81952 | tf_op jit(solution)/shard_map/ppermute | solution.py:43
  50.7 0.0 collective-permute-done.8
  50.7 4.2 %collective-permute-done.7 = bf16[320,128]{1,0:T(8,128)(2,1)S(1)} collective-permute-done((bf16[320,128]{1,0:T(8,128)(2,1)S(1)}, bf16[320,128]{1,0:T(8,128)(2,1)S(1)}, u32[]{:S(2)}, u32[]{:S(2)}) %collective-permute-start.7) | collective-permute-done | bytes 81952 | tf_op jit(solution)/shard_map/ppermute | solution.py:43
  54.9 1.6 %collective-permute-start.10 = (bf16[320,128]{1,0:T(8,128)(2,1)S(1)}, bf16[320,128]{1,0:T(8,128)(2,1)S(1)}, u32[]{:S(2)}, u32[]{:S(2)}) collective-permute-start(bf16[320,128]{1,0:T(8,128)(2,1)S(1)} %fusion), channel_id=1, source_target_pairs={{0,16},{1,9},{2,10},{3,19},{4,20},{5,13},{6,14},{7,23},{8,24},{9,1... | collective-permute-start | bytes 245768 | tf_op jit(solution)/shard_map/ppermute | solution.py:43
  56.5 2.9 %collective-permute-done.10 = bf16[320,128]{1,0:T(8,128)(2,1)S(1)} collective-permute-done((bf16[320,128]{1,0:T(8,128)(2,1)S(1)}, bf16[320,128]{1,0:T(8,128)(2,1)S(1)}, u32[]{:S(2)}, u32[]{:S(2)}) %collective-permute-start.10) | collective-permute-done | bytes 81952 | tf_op jit(solution)/shard_map/ppermute | solution.py:43
  59.4 0.1 multiply_convert_fusion
  59.5 1.6 %collective-permute-start.11 = (bf16[320,128]{1,0:T(8,128)(2,1)S(1)}, bf16[320,128]{1,0:T(8,128)(2,1)S(1)}, u32[]{:S(2)}, u32[]{:S(2)}) collective-permute-start(bf16[320,128]{1,0:T(8,128)(2,1)S(1)} %multiply_convert_fusion), channel_id=1, source_target_pairs={{0,8},{1,17},{2,18},{3,11},{4,12},{5,21},{6,22},{7,15},{8,0},{9,25... | collective-permute-start | bytes 245768 | tf_op jit(solution)/shard_map/ppermute | solution.py:43
  61.0 0.0 copy-done.3
  61.1 0.0 copy-done.5
  61.1 1.8 %shard_map.70.gamma_in = f32[512,2048]{1,0:T(8,128)S(1)} custom-call(s32[3,1,8]{2,1,0:T(1,128)S(1)} %bitcast.17, s32[1,8]{1,0:T(1,128)S(1)} %copy-done.5, f32[512,2048]{1,0:T(8,128)S(1)} %get-tuple-element.11.gamma_in, bf16[512,512]{1,0:T(8,128)(2,1)S(1)} %get-tuple-element.14.mt_ref, bf16[512,2048]{1,0:T(8,128)(2,1)S(1)} %collective-permute-done.2.r_ref), custom_call_target="tpu_custom_call" | custom-call | flops 1073741824 | bytes 1048576 | tf_op jit(solution)/shard_map/pallas_call | solution.py:201
  62.9 1.1 %collective-permute-done.11 = bf16[320,128]{1,0:T(8,128)(2,1)S(1)} collective-permute-done((bf16[320,128]{1,0:T(8,128)(2,1)S(1)}, bf16[320,128]{1,0:T(8,128)(2,1)S(1)}, u32[]{:S(2)}, u32[]{:S(2)}) %collective-permute-start.11) | collective-permute-done | bytes 81952 | tf_op jit(solution)/shard_map/ppermute | solution.py:43
  64.0 0.1 collective-permute-start.12
  64.1 0.0 collective-permute-done.3.r_ref
  64.1 2.0 %shard_map.71.gamma_in = f32[512,2048]{1,0:T(8,128)S(1)} custom-call(s32[3,1,8]{2,1,0:T(1,128)S(1)} %bitcast.18, s32[1,8]{1,0:T(1,128)S(1)} %copy-done.5, bf16[512,2048]{1,0:T(8,128)(2,1)S(1)} %bitcast.12, f32[512,512]{1,0:T(8,128)S(1)} %get-tuple-element.10.over_ref, f32[512,2048]{1,0:T(8,128)S(1)} %shard_map.70.gamma_in, ...), custom_call_target="tpu_custom_call" | custom-call | flops 1073741824 | bytes 1048576 | tf_op jit(solution)/shard_map/pallas_call | solution.py:201
  66.2 7.4 %collective-permute-done.4.refs_0_ = bf16[256,2048]{1,0:T(8,128)(2,1)S(1)} collective-permute-done((bf16[256,2048]{1,0:T(8,128)(2,1)S(1)}, bf16[256,2048]{1,0:T(8,128)(2,1)S(1)}, u32[]{:S(2)}, u32[]{:S(2)}) %collective-permute-start.4) | collective-permute-done | bytes 1048608 | tf_op jit(solution)/shard_map/ppermute | solution.py:33
  73.6 3.0 %shard_map.72 = bf16[512,2048]{1,0:T(8,128)(2,1)} custom-call(s32[3,1,8]{2,1,0:T(1,128)S(1)} %bitcast.19, s32[1,8]{1,0:T(1,128)S(1)} %copy-done.5, bf16[512,2048]{1,0:T(8,128)(2,1)S(1)} %bitcast.13, f32[512,512]{1,0:T(8,128)S(1)} %get-tuple-element.10.over_ref, f32[512,2048]{1,0:T(8,128)S(1)} %shard_map.71.gamma_in, ...), custom_call_target="tpu_custom_call" | custom-call | flops 1073741824 | bytes 1048576 | tf_op jit(solution)/shard_map/pallas_call | solution.py:201
  76.6 0.0 collective-permute-done.12.other_ref
  76.6 2.1 %shard_map.73 = bf16[512,2048]{1,0:T(8,128)(2,1)} custom-call(bf16[640,128]{1,0:T(8,128)(2,1)S(1)} %pad_maximum_fusion.mine_ref, bf16[640,128]{1,0:T(8,128)(2,1)S(1)} %collective-permute-done.12.other_ref, bf16[512,2048]{1,0:T(8,128)(2,1)S(1)} %bitcast.14), custom_call_target="tpu_custom_call" | custom-call | flops 1073741824 | bytes 1048576 | tf_op jit(solution)/shard_map/pallas_call | solution.py:201
  (6 shorter events, 0.2 us)
Async XLA Ops:
  0.6 35.2 %collective-permute-start.2 = (bf16[512,2048]{1,0:T(8,128)(2,1)}, bf16[512,2048]{1,0:T(8,128)(2,1)S(1)}, u32[]{:S(2)}, u32[]{:S(2)}) collective-permute-start(bf16[512,2048]{1,0:T(8,128)(2,1)} %bitcast.9), channel_id=1, source_target_pairs={{0,1},{1,3},{2,0},{3,2},{4,5},{5,7},{6,4},{7,6},{8,9},{9,11},{10,8... | collective-permute-start | bytes 6291464 | tf_op jit(solution)/shard_map/ppermute | solution.py:33
  1.2 26.9 %collective-permute-start = (bf16[1]{0:T(256)(128)(2,1)}, bf16[1]{0:T(256)(128)(2,1)}, u32[]{:S(2)}, u32[]{:S(2)}) collective-permute-start(bf16[1]{0:T(256)(128)(2,1)} %param.6), channel_id=1, source_target_pairs={{0,1},{1,3},{2,0},{3,2},{4,5},{5,7},{6,4},{7,6},{8,9},{9,11},{10,8... | collective-permute-start | bytes 14 | tf_op jit(solution)/shard_map/ppermute | solution.py:33
  3.3 25.4 %collective-permute-start.1 = (bf16[1]{0:T(256)(128)(2,1)}, bf16[1]{0:T(256)(128)(2,1)}, u32[]{:S(2)}, u32[]{:S(2)}) collective-permute-start(bf16[1]{0:T(256)(128)(2,1)} %param.6), channel_id=1, source_target_pairs={{1,0},{3,1},{0,2},{2,3},{5,4},{7,5},{4,6},{6,7},{9,8},{11,9},{8,10... | collective-permute-start | bytes 14 | tf_op jit(solution)/shard_map/ppermute | solution.py:33
  29.4 1.6 %copy-start = (bf16[1,512,2048]{2,1,0:T(8,128)(2,1)S(1)}, bf16[1,512,2048]{2,1,0:T(8,128)(2,1)}, u32[]{:S(2)}) copy-start(bf16[1,512,2048]{2,1,0:T(8,128)(2,1)} %param.5) | copy-start | bytes 6291460
  31.0 0.7 copy-start.2
  31.7 0.7 copy-start.4
  35.8 12.9 %copy-start.1 = (bf16[1,512,2048]{2,1,0:T(8,128)(2,1)S(1)}, bf16[1,512,2048]{2,1,0:T(8,128)(2,1)}, u32[]{:S(2)}) copy-start(bf16[1,512,2048]{2,1,0:T(8,128)(2,1)} %param.5) | copy-start | bytes 6291460
  38.3 1.5 %collective-permute-start.5 = (bf16[640,128]{1,0:T(8,128)(2,1)S(1)}, bf16[640,128]{1,0:T(8,128)(2,1)S(1)}, u32[]{:S(2)}, u32[]{:S(2)}) collective-permute-start(bf16[640,128]{1,0:T(8,128)(2,1)S(1)} %get-tuple-element.17), channel_id=1, source_target_pairs={{0,1},{1,0},{2,3},{3,2},{4,5},{5,4},{6,7},{7,6},{8,9},{9,8},{10,11... | collective-permute-start | bytes 491528 | tf_op jit(solution)/shard_map/ppermute | solution.py:43
  39.8 4.5 %collective-permute-start.6 = (bf16[320,128]{1,0:T(8,128)(2,1)S(1)}, bf16[320,128]{1,0:T(8,128)(2,1)S(1)}, u32[]{:S(2)}, u32[]{:S(2)}) collective-permute-start(bf16[320,128]{1,0:T(8,128)(2,1)S(1)} %get-tuple-element.20), channel_id=1, source_target_pairs={{0,8},{1,17},{2,18},{3,11},{4,12},{5,21},{6,22},{7,15},{8,0},{9,25... | collective-permute-start | bytes 245768 | tf_op jit(solution)/shard_map/ppermute | solution.py:43
  44.4 16.7 %copy-start.3 = (s32[1,8,3]{1,0,2:T(1,128)S(1)}, s32[1,8,3]{1,0,2:T(1,128)}, u32[]{:S(2)}) copy-start(s32[1,8,3]{1,0,2:T(1,128)} %param.8) | copy-start | bytes 292
  44.4 16.7 %copy-start.5 = (s32[1,8]{1,0:T(1,128)S(1)}, s32[1,8]{1,0:T(1,128)}, u32[]{:S(2)}) copy-start(s32[1,8]{1,0:T(1,128)} %counts.9) | copy-start | bytes 100
  44.4 6.3 %collective-permute-start.9 = (bf16[320,128]{1,0:T(8,128)(2,1)S(1)}, bf16[320,128]{1,0:T(8,128)(2,1)S(1)}, u32[]{:S(2)}, u32[]{:S(2)}) collective-permute-start(bf16[320,128]{1,0:T(8,128)(2,1)S(1)} %get-tuple-element.18), channel_id=1, source_target_pairs={{0,3},{1,2},{2,1},{3,0},{4,7},{5,6},{6,5},{7,4},{8,11},{9,10},{10,... | collective-permute-start | bytes 245768 | tf_op jit(solution)/shard_map/ppermute | solution.py:43
  44.5 6.2 %collective-permute-start.8 = (bf16[320,128]{1,0:T(8,128)(2,1)S(1)}, bf16[320,128]{1,0:T(8,128)(2,1)S(1)}, u32[]{:S(2)}, u32[]{:S(2)}) collective-permute-start(bf16[320,128]{1,0:T(8,128)(2,1)S(1)} %get-tuple-element.18), channel_id=1, source_target_pairs={{0,4},{1,5},{2,6},{3,7},{4,0},{5,1},{6,2},{7,3},{8,12},{9,13},{10,... | collective-permute-start | bytes 245768 | tf_op jit(solution)/shard_map/ppermute | solution.py:43
  47.6 7.3 %collective-permute-start.7 = (bf16[320,128]{1,0:T(8,128)(2,1)S(1)}, bf16[320,128]{1,0:T(8,128)(2,1)S(1)}, u32[]{:S(2)}, u32[]{:S(2)}) collective-permute-start(bf16[320,128]{1,0:T(8,128)(2,1)S(1)} %get-tuple-element.18), channel_id=1, source_target_pairs={{0,7},{1,6},{2,5},{3,4},{4,3},{5,2},{6,1},{7,0},{8,15},{9,14},{10,... | collective-permute-start | bytes 245768 | tf_op jit(solution)/shard_map/ppermute | solution.py:43
  48.9 15.2 %collective-permute-start.3 = (bf16[256,2048]{1,0:T(8,128)(2,1)S(1)}, bf16[256,2048]{1,0:T(8,128)(2,1)S(1)}, u32[]{:S(2)}, u32[]{:S(2)}) collective-permute-start(bf16[256,2048]{1,0:T(8,128)(2,1)S(1)} %get-tuple-element.23), channel_id=1, source_target_pairs={{1,0},{3,1},{0,2},{2,3},{5,4},{7,5},{4,6},{6,7},{9,8},{11,9},{8,10... | collective-permute-start | bytes 3145736 | tf_op jit(solution)/shard_map/ppermute | solution.py:33
  49.0 24.6 %collective-permute-start.4 = (bf16[256,2048]{1,0:T(8,128)(2,1)S(1)}, bf16[256,2048]{1,0:T(8,128)(2,1)S(1)}, u32[]{:S(2)}, u32[]{:S(2)}) collective-permute-start(bf16[256,2048]{1,0:T(8,128)(2,1)S(1)} %get-tuple-element.22), channel_id=1, source_target_pairs={{1,0},{3,1},{0,2},{2,3},{5,4},{7,5},{4,6},{6,7},{9,8},{11,9},{8,10... | collective-permute-start | bytes 3145736 | tf_op jit(solution)/shard_map/ppermute | solution.py:33
  54.9 4.5 %collective-permute-start.10 = (bf16[320,128]{1,0:T(8,128)(2,1)S(1)}, bf16[320,128]{1,0:T(8,128)(2,1)S(1)}, u32[]{:S(2)}, u32[]{:S(2)}) collective-permute-start(bf16[320,128]{1,0:T(8,128)(2,1)S(1)} %fusion), channel_id=1, source_target_pairs={{0,16},{1,9},{2,10},{3,19},{4,20},{5,13},{6,14},{7,23},{8,24},{9,1... | collective-permute-start | bytes 245768 | tf_op jit(solution)/shard_map/ppermute | solution.py:43
  59.5 4.5 %collective-permute-start.11 = (bf16[320,128]{1,0:T(8,128)(2,1)S(1)}, bf16[320,128]{1,0:T(8,128)(2,1)S(1)}, u32[]{:S(2)}, u32[]{:S(2)}) collective-permute-start(bf16[320,128]{1,0:T(8,128)(2,1)S(1)} %multiply_convert_fusion), channel_id=1, source_target_pairs={{0,8},{1,17},{2,18},{3,11},{4,12},{5,21},{6,22},{7,15},{8,0},{9,25... | collective-permute-start | bytes 245768 | tf_op jit(solution)/shard_map/ppermute | solution.py:43
  64.0 12.5 %collective-permute-start.12 = (bf16[640,128]{1,0:T(8,128)(2,1)S(1)}, bf16[640,128]{1,0:T(8,128)(2,1)S(1)}, u32[]{:S(2)}, u32[]{:S(2)}) collective-permute-start(bf16[640,128]{1,0:T(8,128)(2,1)S(1)} %pad_maximum_fusion.mine_ref), channel_id=1, source_target_pairs={{0,1},{1,0},{2,3},{3,2},{4,5},{5,4},{6,7},{7,6},{8,9},{9,8},{10,11... | collective-permute-start | bytes 491528 | tf_op jit(solution)/shard_map/ppermute | solution.py:43

commit v5 on v1

--- a/solution.py
+++ b/solution.py
@@ -68,12 +68,13 @@
 
 
 def early_kernel(
-    split, b_ref, row_ref, e_ref, first_ref, second_ref, codes, counts,
-    one_ref, two_ref, dens_ref, gamma_ref, upper_ref, amp
+    splits, b_ref, row_ref, e_ref, first_ref, second_ref, codes, counts,
+    one_ref, two_ref, dens_ref, gamma_ref, upper_ref, upper2_ref, amp
 ):
     vir, aux = b_ref.shape
-    mask = jnp.where(leads(lax.axis_index("mem")), split[0][0], split[1][0])
-    upper_ref[...] = jnp.full(upper_ref.shape, ((lax.axis_index("grp") & mask) != 0).astype(F32))
+    for split, ref in zip(splits, (upper_ref, upper2_ref)):
+        mask = jnp.where(leads(lax.axis_index("mem")), split[0][0], split[1][0])
+        ref[...] = jnp.full(ref.shape, ((lax.axis_index("grp") & mask) != 0).astype(F32))
     row = row_ref[...]
     sums = jnp.broadcast_to(row, (vir, vir)).T + row - e_ref[0]
     one_ref[...] = 1.0 / (sums - first_ref[0])
@@ -240,10 +241,12 @@
     half = len(blocks(vir)) * TILE // 2
     along = [(0, 3)] + [(0, (1 << k) | 3) for k in range(2, members.bit_length() - 1)]
     across = [(1 << k, 0) for k in range(groups.bit_length() - 1)]
-    split, *later = zip(across, across[1:] + across[:1])
-    over_first, over_second, dens, gamma, upper = call(
-        functools.partial(early_kernel, split),
-        (square, square, square, wide, shape((half // 2, TILE), F32)), [pltpu.VMEM((vir, vir), BF16)],
+    splits = list(zip(across, across[1:] + across[:1]))
+    splits, later = splits[:2], splits[2:]
+    over_first, over_second, dens, gamma, *uppers = call(
+        functools.partial(early_kernel, splits),
+        (square, square, square, wide, shape((half // 2, TILE), F32), shape((half // 4, TILE), F32)),
+        [pltpu.VMEM((vir, vir), BF16)],
         (2, 3, 4, 5, 6), 7, 2 * dot,
     )(block, row, energy, first_energy, second_energy, pair_code, pair_count)
 
@@ -254,21 +257,29 @@
     )(block, first, over_first, pair_code, pair_count, dens)
 
     total = keep + swap(send, [(0, 1), (0, 1)]).astype(F32)
-    upper = upper > 0.5
-    below, above = total[: half // 2], total[half // 2 :]
-    got = swap(jnp.where(upper, below, above).astype(BF16), split)
-    total = jnp.where(upper, above, below) + got.astype(F32)
+    uppers = [upper > 0.5 for upper in uppers]
+    for k, (split, upper) in enumerate(zip(splits, uppers)):
+        below, above = total[: half // 2 >> k], total[half // 2 >> k :]
+        got = swap(jnp.where(upper, below, above).astype(BF16), split)
+        total = jnp.where(upper, above, below) + got.astype(F32)
     for masks in later:
         total = total + swap(total.astype(BF16), masks).astype(F32)
-    for mask in along:
+    out = total.astype(BF16)
+    near = [m for _, m in along[:2]]
+    masks = (near + [near[0] ^ near[1]])[::-1] if len(near) > 1 else near
+    masks = sorted(masks, key=lambda m: -(m >> 1))
+    for got in [swap(out, [(0, m), (0, m)]) for m in masks]:
+        total = total + got.astype(F32)
+    for mask in along[2:]:
         total = total + swap(total.astype(BF16), [mask, mask]).astype(F32)
     mine = (total * (1.0 / (8.0 * groups * members))).astype(BF16)
-    got = swap(mine, split)
-    mine = jnp.concatenate([jnp.where(upper, got, mine), jnp.where(upper, mine, got)])
+    for k, (split, upper) in reversed(list(enumerate(zip(splits, uppers)))):
+        got = swap(mine, split)
+        mine = jnp.concatenate([jnp.where(upper, got, mine), jnp.where(upper, mine, got)])
     other = swap(mine, [(0, 1), (0, 1)])
 
     unit = vir // 32
-    cuts = (0, 16 * unit, 21 * unit, 28 * unit, vir)
+    cuts = (0, 16 * unit, 20 * unit, 28 * unit, vir)
     parts = [block[a:b] for a, b in zip(cuts, cuts[1:])]
     second = [turn(part, True) for part in parts]
     gamma = call(first_gamma_kernel, wide, (), (0, 1), 5, dot)(

time: 82.5 us -> 80 us (0.970)
  waiting for transfers between devices: 45 us -> 41.2 us
  starting transfers between devices: 13.2 us -> 14.4 us
    ppermute x7 -> x9, waiting for transfers between devices: 22.2 us -> 18.5 us  [swap(): return lax.ppermute(value, ('grp', 'mem'), pairs)]
    ppermute x7 -> x9, starting transfers between devices: 8.79 us -> 10.6 us  [swap(): return lax.ppermute(value, ('grp', 'mem'), pairs)]
  transfers between devices with their start and end apart: 14 -> 16, of which waited for: 7 -> 8; matrix products, arithmetic and copies ran while one was open for 1% -> 1% of each run, Pallas kernels for 15% -> 16%
where the time goes in v5:
time: 80 us; the launch traced here: 79.7 us
  waiting for transfers between devices  41.2 us (52%)
  Pallas kernels  17.1 us (21%)
  starting transfers between devices  14.4 us (18%)
  local copies, waits for them, and re-layouts  3.11 us (4%)
  between operations  2.9 us (4%)
  other arithmetic  0.96 us (1%)
    ppermute x7, waiting for transfers between devices, turn(): return lax.ppermute(value, 'mem', pairs)  22.8 us
    ppermute x9, waiting for transfers between devices, swap(): return lax.ppermute(value, ('grp', 'mem'), pairs)  18.5 us
    pallas_call x7, Pallas kernels, call(): kernel_call(kernel, outs, scratch, smem, count, flops, out_spec)(*args)  17.1 us
    ppermute x9, starting transfers between devices, swap(): return lax.ppermute(value, ('grp', 'mem'), pairs)  10.6 us
    ppermute x7, starting transfers between devices, turn(): return lax.ppermute(value, 'mem', pairs)  3.86 us
    unnamed x12, local copies, waits for them, and re-layouts  2.94 us
  transfers between devices with their start and end apart: 16, of which 8 were waited for; matrix products, arithmetic and copies ran while one was open for 1% of the time, Pallas kernels for 16%

profile of v5, /device:TPU:0, one launch (start us, length us, event | category | flops | bytes accessed | tf_op | source)
XLA Modules:
  0.0 79.7 jit_solution(11507377845661388346)
XLA Ops:
  0.6 0.6 collective-permute-start.2
  1.2 2.1 %collective-permute-start = (bf16[1]{0:T(256)(128)(2,1)}, bf16[1]{0:T(256)(128)(2,1)}, u32[]{:S(2)}, u32[]{:S(2)}) collective-permute-start(bf16[1]{0:T(256)(128)(2,1)} %param.6), channel_id=1, source_target_pairs={{0,1},{1,3},{2,0},{3,2},{4,5},{5,7},{6,4},{7,6},{8,9},{9,11},{10,8... | collective-permute-start | bytes 14 | tf_op jit(solution)/shard_map/ppermute | solution.py:33
  3.3 0.6 collective-permute-start.1
  4.6 0.7 reshape.15
  5.3 22.7 %collective-permute-done = bf16[1]{0:T(256)(128)(2,1)} collective-permute-done((bf16[1]{0:T(256)(128)(2,1)}, bf16[1]{0:T(256)(128)(2,1)}, u32[]{:S(2)}, u32[]{:S(2)}) %collective-permute-start) | collective-permute-done | bytes 34 | tf_op jit(solution)/shard_map/ppermute | solution.py:33
  28.7 0.0 collective-permute-done.1
  29.4 0.0 copy-start
  29.4 1.6 %copy-done = bf16[1,512,2048]{2,1,0:T(8,128)(2,1)S(1)} copy-done((bf16[1,512,2048]{2,1,0:T(8,128)(2,1)S(1)}, bf16[1,512,2048]{2,1,0:T(8,128)(2,1)}, u32[]{:S(2)}) %copy-start) | copy-done | bytes 2097176
  31.0 0.7 copy-done.2
  31.6 0.7 copy-done.4
  32.3 3.4 %shard_map.68 = (f32[512,512]{1,0:T(8,128)S(1)}, f32[512,512]{1,0:T(8,128)S(1)}, f32[512,512]{1,0:T(8,128)S(1)}, f32[512,2048]{1,0:T(8,128)S(1)}, f32[320,128]{1,0:T(8,128)S(1)}, /*index=5*/f32[160,128]{1,0:T(8,128)S(1)}) custom-call(bf16[512,2048]{1,0:T(8,128)(2,1)S(1)} %bitcast.14, f32[1,512]{1,0:T(1,128)S(1)} %bitcast.26, ...), custom_call_target="tpu_custom_call" | custom-call | flops 2147483648 | bytes 1048576 | tf_op jit(solution)/shard_map/pallas_call | solution.py:205
  35.7 0.0 collective-permute-done.2.r_ref
  35.7 0.0 copy-start.1
  35.8 2.5 %shard_map.69 = (bf16[512,512]{1,0:T(8,128)(2,1)S(1)}, f32[640,128]{1,0:T(8,128)S(1)}, bf16[640,128]{1,0:T(8,128)(2,1)S(1)}) custom-call(bf16[512,2048]{1,0:T(8,128)(2,1)S(1)} %bitcast.15, bf16[512,2048]{1,0:T(8,128)(2,1)S(1)} %collective-permute-done.2.r_ref, f32[512,512]{1,0:T(8,128)S(1)} %get-tuple-element.13.over_ref, s32[3,1,8]{2,1,0:T(1,128)S(1)} %bitcast.21, ...), custom_call_target="tpu_custom_call" | custom-call | flops 1073741824 | bytes 1048576 | tf_op jit(solution)/shard_map/pallas_call | solution.py:205
  38.2 0.1 collective-permute-start.7
  38.3 1.4 %collective-permute-done.7 = bf16[640,128]{1,0:T(8,128)(2,1)S(1)} collective-permute-done((bf16[640,128]{1,0:T(8,128)(2,1)S(1)}, bf16[640,128]{1,0:T(8,128)(2,1)S(1)}, u32[]{:S(2)}, u32[]{:S(2)}) %collective-permute-start.7) | collective-permute-done | bytes 163872 | tf_op jit(solution)/shard_map/ppermute | solution.py:43
  39.8 2.0 %collective-permute-start.8 = (bf16[320,128]{1,0:T(8,128)(2,1)S(1)}, bf16[320,128]{1,0:T(8,128)(2,1)S(1)}, u32[]{:S(2)}, u32[]{:S(2)}) collective-permute-start(bf16[320,128]{1,0:T(8,128)(2,1)S(1)} %get-tuple-element.22), channel_id=1, source_target_pairs={{0,8},{1,17},{2,18},{3,11},{4,12},{5,21},{6,22},{7,15},{8,0},{9,25... | collective-permute-start | bytes 245768 | tf_op jit(solution)/shard_map/ppermute | solution.py:43
  41.8 0.1 slice_bitcast_fusion
  41.9 0.0 copy-start.3
  41.9 0.0 copy-start.5
  41.9 0.1 collective-permute-start.3
  42.0 2.3 %collective-permute-done.8 = bf16[320,128]{1,0:T(8,128)(2,1)S(1)} collective-permute-done((bf16[320,128]{1,0:T(8,128)(2,1)S(1)}, bf16[320,128]{1,0:T(8,128)(2,1)S(1)}, u32[]{:S(2)}, u32[]{:S(2)}) %collective-permute-start.8) | collective-permute-done | bytes 81952 | tf_op jit(solution)/shard_map/ppermute | solution.py:43
  44.3 2.0 %collective-permute-start.9 = (bf16[160,128]{1,0:T(8,128)(2,1)S(1)}, bf16[160,128]{1,0:T(8,128)(2,1)S(1)}, u32[]{:S(2)}, u32[]{:S(2)}) collective-permute-start(bf16[160,128]{1,0:T(8,128)(2,1)S(1)} %get-tuple-element.20), channel_id=1, source_target_pairs={{0,16},{1,9},{2,10},{3,19},{4,20},{5,13},{6,14},{7,23},{8,24},{9,1... | collective-permute-start | bytes 122888 | tf_op jit(solution)/shard_map/ppermute | solution.py:43
  46.4 0.1 collective-permute-start.4
  46.5 1.9 %collective-permute-done.9 = bf16[160,128]{1,0:T(8,128)(2,1)S(1)} collective-permute-done((bf16[160,128]{1,0:T(8,128)(2,1)S(1)}, bf16[160,128]{1,0:T(8,128)(2,1)S(1)}, u32[]{:S(2)}, u32[]{:S(2)}) %collective-permute-start.9) | collective-permute-done | bytes 40992 | tf_op jit(solution)/shard_map/ppermute | solution.py:43
  48.4 0.1 collective-permute-start.12
  48.5 3.1 %collective-permute-start.11 = (bf16[160,128]{1,0:T(8,128)(2,1)S(1)}, bf16[160,128]{1,0:T(8,128)(2,1)S(1)}, u32[]{:S(2)}, u32[]{:S(2)}) collective-permute-start(bf16[160,128]{1,0:T(8,128)(2,1)S(1)} %fusion), channel_id=1, source_target_pairs={{0,4},{1,5},{2,6},{3,7},{4,0},{5,1},{6,2},{7,3},{8,12},{9,13},{10,... | collective-permute-start | bytes 122888 | tf_op jit(solution)/shard_map/ppermute | solution.py:43
  51.6 1.1 %collective-permute-start.10 = (bf16[160,128]{1,0:T(8,128)(2,1)S(1)}, bf16[160,128]{1,0:T(8,128)(2,1)S(1)}, u32[]{:S(2)}, u32[]{:S(2)}) collective-permute-start(bf16[160,128]{1,0:T(8,128)(2,1)S(1)} %fusion), channel_id=1, source_target_pairs={{0,7},{1,6},{2,5},{3,4},{4,3},{5,2},{6,1},{7,0},{8,15},{9,14},{10,... | collective-permute-start | bytes 122888 | tf_op jit(solution)/shard_map/ppermute | solution.py:43
  52.8 7.9 %collective-permute-done.12 = bf16[160,128]{1,0:T(8,128)(2,1)S(1)} collective-permute-done((bf16[160,128]{1,0:T(8,128)(2,1)S(1)}, bf16[160,128]{1,0:T(8,128)(2,1)S(1)}, u32[]{:S(2)}, u32[]{:S(2)}) %collective-permute-start.12) | collective-permute-done | bytes 40992 | tf_op jit(solution)/shard_map/ppermute | solution.py:43
  60.7 0.0 collective-permute-start.5
  60.7 0.0 collective-permute-done.11
  60.7 0.5 collective-permute-start.6
  61.1 2.1 %collective-permute-done.10 = bf16[160,128]{1,0:T(8,128)(2,1)S(1)} collective-permute-done((bf16[160,128]{1,0:T(8,128)(2,1)S(1)}, bf16[160,128]{1,0:T(8,128)(2,1)S(1)}, u32[]{:S(2)}, u32[]{:S(2)}) %collective-permute-start.10) | collective-permute-done | bytes 40992 | tf_op jit(solution)/shard_map/ppermute | solution.py:43
  63.3 0.5 collective-permute-start.13
  63.8 1.8 %shard_map.70.gamma_in = f32[512,2048]{1,0:T(8,128)S(1)} custom-call(s32[3,1,8]{2,1,0:T(1,128)S(1)} %bitcast.22, s32[1,8]{1,0:T(1,128)S(1)} %copy-done.5, f32[512,2048]{1,0:T(8,128)S(1)} %get-tuple-element.12.gamma_in, bf16[512,512]{1,0:T(8,128)(2,1)S(1)} %get-tuple-element.15.mt_ref, bf16[512,2048]{1,0:T(8,128)(2,1)S(1)} %collective-permute-done.2.r_ref), custom_call_target="tpu_custom_call" | custom-call | flops 1073741824 | bytes 1048576 | tf_op jit(solution)/shard_map/pallas_call | solution.py:205
  65.6 2.1 %collective-permute-done.13 = bf16[160,128]{1,0:T(8,128)(2,1)S(1)} collective-permute-done((bf16[160,128]{1,0:T(8,128)(2,1)S(1)}, bf16[160,128]{1,0:T(8,128)(2,1)S(1)}, u32[]{:S(2)}, u32[]{:S(2)}) %collective-permute-start.13) | collective-permute-done | bytes 40992 | tf_op jit(solution)/shard_map/ppermute | solution.py:43
  67.7 1.7 %collective-permute-start.14 = (bf16[320,128]{1,0:T(8,128)(2,1)S(1)}, bf16[320,128]{1,0:T(8,128)(2,1)S(1)}, u32[]{:S(2)}, u32[]{:S(2)}) collective-permute-start(bf16[320,128]{1,0:T(8,128)(2,1)S(1)} %pad_maximum_fusion.1), channel_id=1, source_target_pairs={{0,8},{1,17},{2,18},{3,11},{4,12},{5,21},{6,22},{7,15},{8,0},{9,25... | collective-permute-start | bytes 245768 | tf_op jit(solution)/shard_map/ppermute | solution.py:43
  69.4 0.0 collective-permute-done.3.refs_0_
  69.4 2.0 %shard_map.71.gamma_in = f32[512,2048]{1,0:T(8,128)S(1)} custom-call(s32[3,1,8]{2,1,0:T(1,128)S(1)} %bitcast.23, s32[1,8]{1,0:T(1,128)S(1)} %copy-done.5, bf16[512,2048]{1,0:T(8,128)(2,1)S(1)} %bitcast.16, f32[512,512]{1,0:T(8,128)S(1)} %get-tuple-element.11.over_ref, f32[512,2048]{1,0:T(8,128)S(1)} %shard_map.70.gamma_in, ...), custom_call_target="tpu_custom_call" | custom-call | flops 1073741824 | bytes 1048576 | tf_op jit(solution)/shard_map/pallas_call | solution.py:205
  71.4 0.8 collective-permute-done.14
  72.3 0.1 collective-permute-start.15
  72.4 0.0 collective-permute-done.4.refs_0_
  72.4 0.0 collective-permute-done.5.refs_1_
  72.4 2.2 %shard_map.72.gamma_in = f32[512,2048]{1,0:T(8,128)S(1)} custom-call(s32[3,1,8]{2,1,0:T(1,128)S(1)} %bitcast.24, s32[1,8]{1,0:T(1,128)S(1)} %copy-done.5, bf16[512,2048]{1,0:T(8,128)(2,1)S(1)} %bitcast.17, f32[512,512]{1,0:T(8,128)S(1)} %get-tuple-element.11.over_ref, f32[512,2048]{1,0:T(8,128)S(1)} %shard_map.71.gamma_in, ...), custom_call_target="tpu_custom_call" | custom-call | flops 1073741824 | bytes 1048576 | tf_op jit(solution)/shard_map/pallas_call | solution.py:205
  74.6 0.0 collective-permute-done.6.r_ref
  74.6 3.0 %shard_map.73 = bf16[512,2048]{1,0:T(8,128)(2,1)} custom-call(s32[3,1,8]{2,1,0:T(1,128)S(1)} %bitcast.25, s32[1,8]{1,0:T(1,128)S(1)} %copy-done.5, bf16[512,2048]{1,0:T(8,128)(2,1)S(1)} %bitcast.18, f32[512,512]{1,0:T(8,128)S(1)} %get-tuple-element.11.over_ref, f32[512,2048]{1,0:T(8,128)S(1)} %shard_map.72.gamma_in, ...), custom_call_target="tpu_custom_call" | custom-call | flops 1073741824 | bytes 1048576 | tf_op jit(solution)/shard_map/pallas_call | solution.py:205
  77.6 0.0 collective-permute-done.15.other_ref
  77.6 2.1 %shard_map.74 = bf16[512,2048]{1,0:T(8,128)(2,1)} custom-call(bf16[640,128]{1,0:T(8,128)(2,1)S(1)} %pad_maximum_fusion.mine_ref, bf16[640,128]{1,0:T(8,128)(2,1)S(1)} %collective-permute-done.15.other_ref, bf16[512,2048]{1,0:T(8,128)(2,1)S(1)} %bitcast.19), custom_call_target="tpu_custom_call" | custom-call | flops 1073741824 | bytes 1048576 | tf_op jit(solution)/shard_map/pallas_call | solution.py:205
  (17 shorter events, 0.4 us)
Async XLA Ops:
  0.6 35.1 %collective-permute-start.2 = (bf16[512,2048]{1,0:T(8,128)(2,1)}, bf16[512,2048]{1,0:T(8,128)(2,1)S(1)}, u32[]{:S(2)}, u32[]{:S(2)}) collective-permute-start(bf16[512,2048]{1,0:T(8,128)(2,1)} %bitcast.13), channel_id=1, source_target_pairs={{0,1},{1,3},{2,0},{3,2},{4,5},{5,7},{6,4},{7,6},{8,9},{9,11},{10,8... | collective-permute-start | bytes 6291464 | tf_op jit(solution)/shard_map/ppermute | solution.py:33
  1.2 26.8 %collective-permute-start = (bf16[1]{0:T(256)(128)(2,1)}, bf16[1]{0:T(256)(128)(2,1)}, u32[]{:S(2)}, u32[]{:S(2)}) collective-permute-start(bf16[1]{0:T(256)(128)(2,1)} %param.6), channel_id=1, source_target_pairs={{0,1},{1,3},{2,0},{3,2},{4,5},{5,7},{6,4},{7,6},{8,9},{9,11},{10,8... | collective-permute-start | bytes 14 | tf_op jit(solution)/shard_map/ppermute | solution.py:33
  3.3 25.4 %collective-permute-start.1 = (bf16[1]{0:T(256)(128)(2,1)}, bf16[1]{0:T(256)(128)(2,1)}, u32[]{:S(2)}, u32[]{:S(2)}) collective-permute-start(bf16[1]{0:T(256)(128)(2,1)} %param.6), channel_id=1, source_target_pairs={{1,0},{3,1},{0,2},{2,3},{5,4},{7,5},{4,6},{6,7},{9,8},{11,9},{8,10... | collective-permute-start | bytes 14 | tf_op jit(solution)/shard_map/ppermute | solution.py:33
  29.4 1.6 %copy-start = (bf16[1,512,2048]{2,1,0:T(8,128)(2,1)S(1)}, bf16[1,512,2048]{2,1,0:T(8,128)(2,1)}, u32[]{:S(2)}) copy-start(bf16[1,512,2048]{2,1,0:T(8,128)(2,1)} %param.5) | copy-start | bytes 6291460
  31.0 0.7 copy-start.2
  31.6 0.7 copy-start.4
  35.7 6.0 %copy-start.1 = (bf16[1,512,2048]{2,1,0:T(8,128)(2,1)S(1)}, bf16[1,512,2048]{2,1,0:T(8,128)(2,1)}, u32[]{:S(2)}) copy-start(bf16[1,512,2048]{2,1,0:T(8,128)(2,1)} %param.5) | copy-start | bytes 6291460
  38.2 1.5 %collective-permute-start.7 = (bf16[640,128]{1,0:T(8,128)(2,1)S(1)}, bf16[640,128]{1,0:T(8,128)(2,1)S(1)}, u32[]{:S(2)}, u32[]{:S(2)}) collective-permute-start(bf16[640,128]{1,0:T(8,128)(2,1)S(1)} %get-tuple-element.19), channel_id=1, source_target_pairs={{0,1},{1,0},{2,3},{3,2},{4,5},{5,4},{6,7},{7,6},{8,9},{9,8},{10,11... | collective-permute-start | bytes 491528 | tf_op jit(solution)/shard_map/ppermute | solution.py:43
  39.8 4.5 %collective-permute-start.8 = (bf16[320,128]{1,0:T(8,128)(2,1)S(1)}, bf16[320,128]{1,0:T(8,128)(2,1)S(1)}, u32[]{:S(2)}, u32[]{:S(2)}) collective-permute-start(bf16[320,128]{1,0:T(8,128)(2,1)S(1)} %get-tuple-element.22), channel_id=1, source_target_pairs={{0,8},{1,17},{2,18},{3,11},{4,12},{5,21},{6,22},{7,15},{8,0},{9,25... | collective-permute-start | bytes 245768 | tf_op jit(solution)/shard_map/ppermute | solution.py:43
  41.9 21.9 %copy-start.3 = (s32[1,8,3]{1,0,2:T(1,128)S(1)}, s32[1,8,3]{1,0,2:T(1,128)}, u32[]{:S(2)}) copy-start(s32[1,8,3]{1,0,2:T(1,128)} %param.8) | copy-start | bytes 292
  41.9 21.9 %copy-start.5 = (s32[1,8]{1,0:T(1,128)S(1)}, s32[1,8]{1,0:T(1,128)}, u32[]{:S(2)}) copy-start(s32[1,8]{1,0:T(1,128)} %counts.11) | copy-start | bytes 100
  41.9 27.5 %collective-permute-start.3 = (bf16[256,2048]{1,0:T(8,128)(2,1)S(1)}, bf16[256,2048]{1,0:T(8,128)(2,1)S(1)}, u32[]{:S(2)}, u32[]{:S(2)}) collective-permute-start(bf16[256,2048]{1,0:T(8,128)(2,1)S(1)} %slice_bitcast_fusion), channel_id=1, source_target_pairs={{1,0},{3,1},{0,2},{2,3},{5,4},{7,5},{4,6},{6,7},{9,8},{11,9},{8,10... | collective-permute-start | bytes 3145736 | tf_op jit(solution)/shard_map/ppermute | solution.py:33
  44.3 4.1 %collective-permute-start.9 = (bf16[160,128]{1,0:T(8,128)(2,1)S(1)}, bf16[160,128]{1,0:T(8,128)(2,1)S(1)}, u32[]{:S(2)}, u32[]{:S(2)}) collective-permute-start(bf16[160,128]{1,0:T(8,128)(2,1)S(1)} %get-tuple-element.20), channel_id=1, source_target_pairs={{0,16},{1,9},{2,10},{3,19},{4,20},{5,13},{6,14},{7,23},{8,24},{9,1... | collective-permute-start | bytes 122888 | tf_op jit(solution)/shard_map/ppermute | solution.py:43
  46.4 25.9 %collective-permute-start.4 = (bf16[64,2048]{1,0:T(8,128)(2,1)S(1)}, bf16[64,2048]{1,0:T(8,128)(2,1)S(1)}, u32[]{:S(2)}, u32[]{:S(2)}) collective-permute-start(bf16[64,2048]{1,0:T(8,128)(2,1)S(1)} %get-tuple-element.25), channel_id=1, source_target_pairs={{1,0},{3,1},{0,2},{2,3},{5,4},{7,5},{4,6},{6,7},{9,8},{11,9},{8,10... | collective-permute-start | bytes 786440 | tf_op jit(solution)/shard_map/ppermute | solution.py:33
  48.4 12.3 %collective-permute-start.12 = (bf16[160,128]{1,0:T(8,128)(2,1)S(1)}, bf16[160,128]{1,0:T(8,128)(2,1)S(1)}, u32[]{:S(2)}, u32[]{:S(2)}) collective-permute-start(bf16[160,128]{1,0:T(8,128)(2,1)S(1)} %fusion), channel_id=1, source_target_pairs={{0,3},{1,2},{2,1},{3,0},{4,7},{5,6},{6,5},{7,4},{8,11},{9,10},{10,... | collective-permute-start | bytes 122888 | tf_op jit(solution)/shard_map/ppermute | solution.py:43
  48.5 12.2 %collective-permute-start.11 = (bf16[160,128]{1,0:T(8,128)(2,1)S(1)}, bf16[160,128]{1,0:T(8,128)(2,1)S(1)}, u32[]{:S(2)}, u32[]{:S(2)}) collective-permute-start(bf16[160,128]{1,0:T(8,128)(2,1)S(1)} %fusion), channel_id=1, source_target_pairs={{0,4},{1,5},{2,6},{3,7},{4,0},{5,1},{6,2},{7,3},{8,12},{9,13},{10,... | collective-permute-start | bytes 122888 | tf_op jit(solution)/shard_map/ppermute | solution.py:43
  51.6 11.6 %collective-permute-start.10 = (bf16[160,128]{1,0:T(8,128)(2,1)S(1)}, bf16[160,128]{1,0:T(8,128)(2,1)S(1)}, u32[]{:S(2)}, u32[]{:S(2)}) collective-permute-start(bf16[160,128]{1,0:T(8,128)(2,1)S(1)} %fusion), channel_id=1, source_target_pairs={{0,7},{1,6},{2,5},{3,4},{4,3},{5,2},{6,1},{7,0},{8,15},{9,14},{10,... | collective-permute-start | bytes 122888 | tf_op jit(solution)/shard_map/ppermute | solution.py:43
  60.7 11.7 %collective-permute-start.5 = (bf16[128,2048]{1,0:T(8,128)(2,1)S(1)}, bf16[128,2048]{1,0:T(8,128)(2,1)S(1)}, u32[]{:S(2)}, u32[]{:S(2)}) collective-permute-start(bf16[128,2048]{1,0:T(8,128)(2,1)S(1)} %slice_bitcast_fusion.1), channel_id=1, source_target_pairs={{1,0},{3,1},{0,2},{2,3},{5,4},{7,5},{4,6},{6,7},{9,8},{11,9},{8,10... | collective-permute-start | bytes 1572872 | tf_op jit(solution)/shard_map/ppermute | solution.py:33
  60.7 13.9 %collective-permute-start.6 = (bf16[64,2048]{1,0:T(8,128)(2,1)S(1)}, bf16[64,2048]{1,0:T(8,128)(2,1)S(1)}, u32[]{:S(2)}, u32[]{:S(2)}) collective-permute-start(bf16[64,2048]{1,0:T(8,128)(2,1)S(1)} %get-tuple-element.24), channel_id=1, source_target_pairs={{1,0},{3,1},{0,2},{2,3},{5,4},{7,5},{4,6},{6,7},{9,8},{11,9},{8,10... | collective-permute-start | bytes 786440 | tf_op jit(solution)/shard_map/ppermute | solution.py:33
  63.3 4.4 %collective-permute-start.13 = (bf16[160,128]{1,0:T(8,128)(2,1)S(1)}, bf16[160,128]{1,0:T(8,128)(2,1)S(1)}, u32[]{:S(2)}, u32[]{:S(2)}) collective-permute-start(bf16[160,128]{1,0:T(8,128)(2,1)S(1)} %multiply_convert_fusion), channel_id=1, source_target_pairs={{0,16},{1,9},{2,10},{3,19},{4,20},{5,13},{6,14},{7,23},{8,24},{9,1... | collective-permute-start | bytes 122888 | tf_op jit(solution)/shard_map/ppermute | solution.py:43
  67.7 4.5 %collective-permute-start.14 = (bf16[320,128]{1,0:T(8,128)(2,1)S(1)}, bf16[320,128]{1,0:T(8,128)(2,1)S(1)}, u32[]{:S(2)}, u32[]{:S(2)}) collective-permute-start(bf16[320,128]{1,0:T(8,128)(2,1)S(1)} %pad_maximum_fusion.1), channel_id=1, source_target_pairs={{0,8},{1,17},{2,18},{3,11},{4,12},{5,21},{6,22},{7,15},{8,0},{9,25... | collective-permute-start | bytes 245768 | tf_op jit(solution)/shard_map/ppermute | solution.py:43
  72.3 5.3 %collective-permute-start.15 = (bf16[640,128]{1,0:T(8,128)(2,1)S(1)}, bf16[640,128]{1,0:T(8,128)(2,1)S(1)}, u32[]{:S(2)}, u32[]{:S(2)}) collective-permute-start(bf16[640,128]{1,0:T(8,128)(2,1)S(1)} %pad_maximum_fusion.mine_ref), channel_id=1, source_target_pairs={{0,1},{1,0},{2,3},{3,2},{4,5},{5,4},{6,7},{7,6},{8,9},{9,8},{10,11... | collective-permute-start | bytes 491528 | tf_op jit(solution)/shard_map/ppermute | solution.py:43

commit v6 on v5

--- a/solution.py
+++ b/solution.py
@@ -164,22 +164,19 @@
     return m_ref[...].T
 
 
-def next_gamma_kernel(cut, codes, counts, b_ref, over_ref, gamma_in, *refs):
-    parts, (gamma_ref, r_ref, mt_ref, m_ref) = refs[:-4], refs[-4:]
+def second_gamma_kernel(codes, counts, b_ref, over_ref, gamma_in, r_ref, gamma_ref, mt_ref, m_ref):
     own, far = weights(codes, counts, 3 - first_round(lax.axis_index("mem")))
-    if len(parts) == 1:
-        r_ref = parts[0]
-    else:
-        joined(parts, r_ref)
-    mt_ref[...] = flat_amp(slice(cut, cut + r_ref.shape[0]), b_ref, r_ref, over_ref, m_ref)
+    mt_ref[...] = flat_amp(slice(0, r_ref.shape[0]), b_ref, r_ref, over_ref, m_ref)
     aux = gamma_ref.shape[1]
     for p in range(STRIPS):
         at = pl.ds(p * (aux // STRIPS), aux // STRIPS)
         gamma_ref[:, at] = gamma_in[:, at] + (own + far) * nn(mt_ref[...], r_ref[:, at])
 
 
-def last_gamma_kernel(codes, counts, b_ref, over_ref, gamma_in, r_ref, out_ref, held, sems, mt_ref, m_ref):
+def last_gamma_kernel(codes, counts, b_ref, over_ref, gamma_in, *refs):
+    parts, (out_ref, held, sems, r_ref, mt_ref, m_ref) = refs[:-6], refs[-6:]
     own, far = weights(codes, counts, 3 - first_round(lax.axis_index("mem")))
+    joined(parts, r_ref)
     vir = b_ref.shape[0]
     mt_ref[...] = flat_amp(slice(vir - r_ref.shape[0], vir), b_ref, r_ref, over_ref, m_ref)
     strips_out(
@@ -278,27 +275,21 @@
         mine = jnp.concatenate([jnp.where(upper, got, mine), jnp.where(upper, mine, got)])
     other = swap(mine, [(0, 1), (0, 1)])
 
-    unit = vir // 32
-    cuts = (0, 16 * unit, 20 * unit, 28 * unit, vir)
+    unit = vir // 16
+    cuts = (0, 8 * unit, 11 * unit, vir)
     parts = [block[a:b] for a, b in zip(cuts, cuts[1:])]
     second = [turn(part, True) for part in parts]
     gamma = call(first_gamma_kernel, wide, (), (0, 1), 5, dot)(
         pair_code, pair_count, gamma, mt, first
     )
-
-    def bounce(rows):
-        return [pltpu.VMEM((vir, rows), BF16), pltpu.VMEM((rows, vir), BF16)]
-
-    for a, b in ((0, 1), (1, 3)):
-        rows = cuts[b] - cuts[a]
-        gamma = call(
-            functools.partial(next_gamma_kernel, cuts[a]), wide, [pltpu.VMEM((rows, aux), BF16), *bounce(rows)],
-            (0, 1), 5 + b - a, dot,
-        )(pair_code, pair_count, block, over_second, gamma, *second[a:b])
+    bounce = [pltpu.VMEM((vir, vir // 2), BF16), pltpu.VMEM((vir // 2, vir), BF16)]
+    gamma = call(second_gamma_kernel, wide, bounce, (0, 1), 6, dot)(
+        pair_code, pair_count, block, over_second, gamma, second[0]
+    )
     result = call(
-        last_gamma_kernel, shape((vir, aux), BF16), [*out_scratch, *bounce(vir - cuts[3])],
-        (0, 1), 6, dot, any_space,
-    )(pair_code, pair_count, block, over_second, gamma, second[3])
+        last_gamma_kernel, shape((vir, aux), BF16), [*out_scratch, pltpu.VMEM((vir // 2, aux), BF16), *bounce],
+        (0, 1), 7, dot, any_space,
+    )(pair_code, pair_count, block, over_second, gamma, *second[1:])
     lagrangian = call(
         apply_kernel, shape((vir, aux), BF16), [pltpu.VMEM((vir, vir), BF16), *out_scratch], (), 3, dot,
         any_space,

time: 80 us -> 80.3 us (level)
  waiting for transfers between devices: 41.2 us -> 44.3 us
  Pallas kernels: 17.1 us -> 14.8 us
    ppermute x9, waiting for transfers between devices: 18.5 us -> 21.5 us  [swap(): return lax.ppermute(value, ('grp', 'mem'), pairs)]
    pallas_call x7 -> x6, Pallas kernels: 17.1 us -> 14.8 us  [call(): kernel_call(kernel, outs, scratch, smem, count, flops, out_spec)(*args)]
    ppermute x7 -> x6, starting transfers between devices: 3.86 us -> 3.47 us  [turn(): return lax.ppermute(value, 'mem', pairs)]
    ppermute x7 -> x6, waiting for transfers between devices: 22.8 us -> 22.8 us  [turn(): return lax.ppermute(value, 'mem', pairs)]
  transfers between devices with their start and end apart: 16 -> 15, of which waited for: 8 -> 8; matrix products, arithmetic and copies ran while one was open for 1% -> 1% of each run, Pallas kernels for 16% -> 13%
where the time goes in v6:
time: 80.3 us; the launch traced here: 80.1 us
  waiting for transfers between devices  44.3 us (55%)
  Pallas kernels  14.8 us (18%)
  starting transfers between devices  14.1 us (18%)
  local copies, waits for them, and re-layouts  3.09 us (4%)
  between operations  2.82 us (4%)
  other arithmetic  0.97 us (1%)
    ppermute x6, waiting for transfers between devices, turn(): return lax.ppermute(value, 'mem', pairs)  22.8 us
    ppermute x9, waiting for transfers between devices, swap(): return lax.ppermute(value, ('grp', 'mem'), pairs)  21.5 us
    pallas_call x6, Pallas kernels, call(): kernel_call(kernel, outs, scratch, smem, count, flops, out_spec)(*args)  14.8 us
    ppermute x9, starting transfers between devices, swap(): return lax.ppermute(value, ('grp', 'mem'), pairs)  10.6 us
    ppermute x6, starting transfers between devices, turn(): return lax.ppermute(value, 'mem', pairs)  3.47 us
    unnamed x12, local copies, waits for them, and re-layouts  2.94 us
  transfers between devices with their start and end apart: 15, of which 8 were waited for; matrix products, arithmetic and copies ran while one was open for 1% of the time, Pallas kernels for 13%

profile of v6, /device:TPU:0, one launch (start us, length us, event | category | flops | bytes accessed | tf_op | source)
XLA Modules:
  0.0 80.1 jit_solution(7499557370181793628)
XLA Ops:
  0.6 0.6 collective-permute-start.2
  1.2 2.1 %collective-permute-start = (bf16[1]{0:T(256)(128)(2,1)}, bf16[1]{0:T(256)(128)(2,1)}, u32[]{:S(2)}, u32[]{:S(2)}) collective-permute-start(bf16[1]{0:T(256)(128)(2,1)} %param.6), channel_id=1, source_target_pairs={{0,1},{1,3},{2,0},{3,2},{4,5},{5,7},{6,4},{7,6},{8,9},{9,11},{10,8... | collective-permute-start | bytes 14 | tf_op jit(solution)/shard_map/ppermute | solution.py:33
  3.3 0.6 collective-permute-start.1
  4.6 0.7 reshape.14
  5.3 22.8 %collective-permute-done = bf16[1]{0:T(256)(128)(2,1)} collective-permute-done((bf16[1]{0:T(256)(128)(2,1)}, bf16[1]{0:T(256)(128)(2,1)}, u32[]{:S(2)}, u32[]{:S(2)}) %collective-permute-start) | collective-permute-done | bytes 34 | tf_op jit(solution)/shard_map/ppermute | solution.py:33
  28.7 0.0 collective-permute-done.1
  29.4 0.0 copy-start
  29.4 1.6 %copy-done = bf16[1,512,2048]{2,1,0:T(8,128)(2,1)S(1)} copy-done((bf16[1,512,2048]{2,1,0:T(8,128)(2,1)S(1)}, bf16[1,512,2048]{2,1,0:T(8,128)(2,1)}, u32[]{:S(2)}) %copy-start) | copy-done | bytes 2097176
  31.0 0.7 copy-done.2
  31.6 0.7 copy-done.4
  32.3 3.4 %shard_map.68 = (f32[512,512]{1,0:T(8,128)S(1)}, f32[512,512]{1,0:T(8,128)S(1)}, f32[512,512]{1,0:T(8,128)S(1)}, f32[512,2048]{1,0:T(8,128)S(1)}, f32[320,128]{1,0:T(8,128)S(1)}, /*index=5*/f32[160,128]{1,0:T(8,128)S(1)}) custom-call(bf16[512,2048]{1,0:T(8,128)(2,1)S(1)} %bitcast.12, f32[1,512]{1,0:T(1,128)S(1)} %bitcast.22, ...), custom_call_target="tpu_custom_call" | custom-call | flops 2147483648 | bytes 1048576 | tf_op jit(solution)/shard_map/pallas_call | solution.py:202
  35.7 0.0 collective-permute-done.2.r_ref
  35.7 2.5 %shard_map.69 = (bf16[512,512]{1,0:T(8,128)(2,1)S(1)}, f32[640,128]{1,0:T(8,128)S(1)}, bf16[640,128]{1,0:T(8,128)(2,1)S(1)}) custom-call(bf16[512,2048]{1,0:T(8,128)(2,1)S(1)} %bitcast.13, bf16[512,2048]{1,0:T(8,128)(2,1)S(1)} %collective-permute-done.2.r_ref, f32[512,512]{1,0:T(8,128)S(1)} %get-tuple-element.13.over_ref, s32[3,1,8]{2,1,0:T(1,128)S(1)} %bitcast.18, ...), custom_call_target="tpu_custom_call" | custom-call | flops 1073741824 | bytes 1048576 | tf_op jit(solution)/shard_map/pallas_call | solution.py:202
  38.2 0.0 copy-start.1
  38.2 0.1 collective-permute-start.6
  38.3 1.4 %collective-permute-done.6 = bf16[640,128]{1,0:T(8,128)(2,1)S(1)} collective-permute-done((bf16[640,128]{1,0:T(8,128)(2,1)S(1)}, bf16[640,128]{1,0:T(8,128)(2,1)S(1)}, u32[]{:S(2)}, u32[]{:S(2)}) %collective-permute-start.6) | collective-permute-done | bytes 163872 | tf_op jit(solution)/shard_map/ppermute | solution.py:43
  39.8 2.0 %collective-permute-start.7 = (bf16[320,128]{1,0:T(8,128)(2,1)S(1)}, bf16[320,128]{1,0:T(8,128)(2,1)S(1)}, u32[]{:S(2)}, u32[]{:S(2)}) collective-permute-start(bf16[320,128]{1,0:T(8,128)(2,1)S(1)} %get-tuple-element.22), channel_id=1, source_target_pairs={{0,8},{1,17},{2,18},{3,11},{4,12},{5,21},{6,22},{7,15},{8,0},{9,25... | collective-permute-start | bytes 245768 | tf_op jit(solution)/shard_map/ppermute | solution.py:43
  41.8 2.5 %collective-permute-done.7 = bf16[320,128]{1,0:T(8,128)(2,1)S(1)} collective-permute-done((bf16[320,128]{1,0:T(8,128)(2,1)S(1)}, bf16[320,128]{1,0:T(8,128)(2,1)S(1)}, u32[]{:S(2)}, u32[]{:S(2)}) %collective-permute-start.7) | collective-permute-done | bytes 81952 | tf_op jit(solution)/shard_map/ppermute | solution.py:43
  44.3 0.0 copy-start.3
  44.4 0.0 copy-start.5
  44.4 2.0 %collective-permute-start.8 = (bf16[160,128]{1,0:T(8,128)(2,1)S(1)}, bf16[160,128]{1,0:T(8,128)(2,1)S(1)}, u32[]{:S(2)}, u32[]{:S(2)}) collective-permute-start(bf16[160,128]{1,0:T(8,128)(2,1)S(1)} %get-tuple-element.20), channel_id=1, source_target_pairs={{0,16},{1,9},{2,10},{3,19},{4,20},{5,13},{6,14},{7,23},{8,24},{9,1... | collective-permute-start | bytes 122888 | tf_op jit(solution)/shard_map/ppermute | solution.py:43
  46.4 0.0 copy-done.1
  46.4 0.1 slice_bitcast_fusion
  46.5 0.1 collective-permute-start.3
  46.6 1.9 %collective-permute-done.8 = bf16[160,128]{1,0:T(8,128)(2,1)S(1)} collective-permute-done((bf16[160,128]{1,0:T(8,128)(2,1)S(1)}, bf16[160,128]{1,0:T(8,128)(2,1)S(1)}, u32[]{:S(2)}, u32[]{:S(2)}) %collective-permute-start.8) | collective-permute-done | bytes 40992 | tf_op jit(solution)/shard_map/ppermute | solution.py:43
  48.5 0.1 collective-permute-start.11
  48.5 3.1 %collective-permute-start.10 = (bf16[160,128]{1,0:T(8,128)(2,1)S(1)}, bf16[160,128]{1,0:T(8,128)(2,1)S(1)}, u32[]{:S(2)}, u32[]{:S(2)}) collective-permute-start(bf16[160,128]{1,0:T(8,128)(2,1)S(1)} %fusion), channel_id=1, source_target_pairs={{0,4},{1,5},{2,6},{3,7},{4,0},{5,1},{6,2},{7,3},{8,12},{9,13},{10,... | collective-permute-start | bytes 122888 | tf_op jit(solution)/shard_map/ppermute | solution.py:43
  51.6 1.1 %collective-permute-start.9 = (bf16[160,128]{1,0:T(8,128)(2,1)S(1)}, bf16[160,128]{1,0:T(8,128)(2,1)S(1)}, u32[]{:S(2)}, u32[]{:S(2)}) collective-permute-start(bf16[160,128]{1,0:T(8,128)(2,1)S(1)} %fusion), channel_id=1, source_target_pairs={{0,7},{1,6},{2,5},{3,4},{4,3},{5,2},{6,1},{7,0},{8,15},{9,14},{10,... | collective-permute-start | bytes 122888 | tf_op jit(solution)/shard_map/ppermute | solution.py:43
  52.8 0.1 collective-permute-start.4
  52.8 8.7 %collective-permute-done.11 = bf16[160,128]{1,0:T(8,128)(2,1)S(1)} collective-permute-done((bf16[160,128]{1,0:T(8,128)(2,1)S(1)}, bf16[160,128]{1,0:T(8,128)(2,1)S(1)}, u32[]{:S(2)}, u32[]{:S(2)}) %collective-permute-start.11) | collective-permute-done | bytes 40992 | tf_op jit(solution)/shard_map/ppermute | solution.py:43
  61.5 0.0 collective-permute-done.10
  61.5 2.6 %collective-permute-done.9 = bf16[160,128]{1,0:T(8,128)(2,1)S(1)} collective-permute-done((bf16[160,128]{1,0:T(8,128)(2,1)S(1)}, bf16[160,128]{1,0:T(8,128)(2,1)S(1)}, u32[]{:S(2)}, u32[]{:S(2)}) %collective-permute-start.9) | collective-permute-done | bytes 40992 | tf_op jit(solution)/shard_map/ppermute | solution.py:43
  64.2 1.6 %collective-permute-start.12 = (bf16[160,128]{1,0:T(8,128)(2,1)S(1)}, bf16[160,128]{1,0:T(8,128)(2,1)S(1)}, u32[]{:S(2)}, u32[]{:S(2)}) collective-permute-start(bf16[160,128]{1,0:T(8,128)(2,1)S(1)} %multiply_convert_fusion), channel_id=1, source_target_pairs={{0,16},{1,9},{2,10},{3,19},{4,20},{5,13},{6,14},{7,23},{8,24},{9,1... | collective-permute-start | bytes 122888 | tf_op jit(solution)/shard_map/ppermute | solution.py:43
  65.7 0.1 slice_bitcast_fusion.1
  65.8 0.1 collective-permute-start.5
  65.9 2.4 %collective-permute-done.12 = bf16[160,128]{1,0:T(8,128)(2,1)S(1)} collective-permute-done((bf16[160,128]{1,0:T(8,128)(2,1)S(1)}, bf16[160,128]{1,0:T(8,128)(2,1)S(1)}, u32[]{:S(2)}, u32[]{:S(2)}) %collective-permute-start.12) | collective-permute-done | bytes 40992 | tf_op jit(solution)/shard_map/ppermute | solution.py:43
  68.3 0.6 collective-permute-start.13
  68.8 0.0 copy-done.3
  68.9 1.8 %shard_map.70.gamma_in = f32[512,2048]{1,0:T(8,128)S(1)} custom-call(s32[3,1,8]{2,1,0:T(1,128)S(1)} %bitcast.19, s32[1,8]{1,0:T(1,128)S(1)} %copy-done.5, f32[512,2048]{1,0:T(8,128)S(1)} %get-tuple-element.12.gamma_in, bf16[512,512]{1,0:T(8,128)(2,1)S(1)} %get-tuple-element.15.mt_ref, bf16[512,2048]{1,0:T(8,128)(2,1)S(1)} %collective-permute-done.2.r_ref), custom_call_target="tpu_custom_call" | custom-call | flops 1073741824 | bytes 1048576 | tf_op jit(solution)/shard_map/pallas_call | solution.py:202
  70.7 2.1 %collective-permute-done.13 = bf16[320,128]{1,0:T(8,128)(2,1)S(1)} collective-permute-done((bf16[320,128]{1,0:T(8,128)(2,1)S(1)}, bf16[320,128]{1,0:T(8,128)(2,1)S(1)}, u32[]{:S(2)}, u32[]{:S(2)}) %collective-permute-start.13) | collective-permute-done | bytes 81952 | tf_op jit(solution)/shard_map/ppermute | solution.py:43
  72.8 0.1 collective-permute-start.14
  72.9 0.0 collective-permute-done.3.r_ref
  72.9 2.0 %shard_map.71.gamma_in = f32[512,2048]{1,0:T(8,128)S(1)} custom-call(s32[3,1,8]{2,1,0:T(1,128)S(1)} %bitcast.20, s32[1,8]{1,0:T(1,128)S(1)} %copy-done.5, bf16[512,2048]{1,0:T(8,128)(2,1)S(1)} %bitcast.14, f32[512,512]{1,0:T(8,128)S(1)} %get-tuple-element.11.over_ref, f32[512,2048]{1,0:T(8,128)S(1)} %shard_map.70.gamma_in, ...), custom_call_target="tpu_custom_call" | custom-call | flops 1073741824 | bytes 1048576 | tf_op jit(solution)/shard_map/pallas_call | solution.py:202
  75.0 0.0 collective-permute-done.4.refs_0_
  75.0 0.0 collective-permute-done.5.refs_1_
  75.0 3.0 %shard_map.72 = bf16[512,2048]{1,0:T(8,128)(2,1)} custom-call(s32[3,1,8]{2,1,0:T(1,128)S(1)} %bitcast.21, s32[1,8]{1,0:T(1,128)S(1)} %copy-done.5, bf16[512,2048]{1,0:T(8,128)(2,1)S(1)} %bitcast.15, f32[512,512]{1,0:T(8,128)S(1)} %get-tuple-element.11.over_ref, f32[512,2048]{1,0:T(8,128)S(1)} %shard_map.71.gamma_in, ...), custom_call_target="tpu_custom_call" | custom-call | flops 1073741824 | bytes 1048576 | tf_op jit(solution)/shard_map/pallas_call | solution.py:202
  78.0 0.0 collective-permute-done.14.other_ref
  78.0 2.1 %shard_map.73 = bf16[512,2048]{1,0:T(8,128)(2,1)} custom-call(bf16[640,128]{1,0:T(8,128)(2,1)S(1)} %pad_maximum_fusion.mine_ref, bf16[640,128]{1,0:T(8,128)(2,1)S(1)} %collective-permute-done.14.other_ref, bf16[512,2048]{1,0:T(8,128)(2,1)S(1)} %bitcast.16), custom_call_target="tpu_custom_call" | custom-call | flops 1073741824 | bytes 1048576 | tf_op jit(solution)/shard_map/pallas_call | solution.py:202
  (14 shorter events, 0.3 us)
Async XLA Ops:
  0.6 35.1 %collective-permute-start.2 = (bf16[512,2048]{1,0:T(8,128)(2,1)}, bf16[512,2048]{1,0:T(8,128)(2,1)S(1)}, u32[]{:S(2)}, u32[]{:S(2)}) collective-permute-start(bf16[512,2048]{1,0:T(8,128)(2,1)} %bitcast.11), channel_id=1, source_target_pairs={{0,1},{1,3},{2,0},{3,2},{4,5},{5,7},{6,4},{7,6},{8,9},{9,11},{10,8... | collective-permute-start | bytes 6291464 | tf_op jit(solution)/shard_map/ppermute | solution.py:33
  1.2 26.9 %collective-permute-start = (bf16[1]{0:T(256)(128)(2,1)}, bf16[1]{0:T(256)(128)(2,1)}, u32[]{:S(2)}, u32[]{:S(2)}) collective-permute-start(bf16[1]{0:T(256)(128)(2,1)} %param.6), channel_id=1, source_target_pairs={{0,1},{1,3},{2,0},{3,2},{4,5},{5,7},{6,4},{7,6},{8,9},{9,11},{10,8... | collective-permute-start | bytes 14 | tf_op jit(solution)/shard_map/ppermute | solution.py:33
  3.3 25.4 %collective-permute-start.1 = (bf16[1]{0:T(256)(128)(2,1)}, bf16[1]{0:T(256)(128)(2,1)}, u32[]{:S(2)}, u32[]{:S(2)}) collective-permute-start(bf16[1]{0:T(256)(128)(2,1)} %param.6), channel_id=1, source_target_pairs={{1,0},{3,1},{0,2},{2,3},{5,4},{7,5},{4,6},{6,7},{9,8},{11,9},{8,10... | collective-permute-start | bytes 14 | tf_op jit(solution)/shard_map/ppermute | solution.py:33
  29.4 1.6 %copy-start = (bf16[1,512,2048]{2,1,0:T(8,128)(2,1)S(1)}, bf16[1,512,2048]{2,1,0:T(8,128)(2,1)}, u32[]{:S(2)}) copy-start(bf16[1,512,2048]{2,1,0:T(8,128)(2,1)} %param.5) | copy-start | bytes 6291460
  30.9 0.7 copy-start.2
  31.6 0.7 copy-start.4
  38.2 8.2 %copy-start.1 = (bf16[1,512,2048]{2,1,0:T(8,128)(2,1)S(1)}, bf16[1,512,2048]{2,1,0:T(8,128)(2,1)}, u32[]{:S(2)}) copy-start(bf16[1,512,2048]{2,1,0:T(8,128)(2,1)} %param.5) | copy-start | bytes 6291460
  38.2 1.5 %collective-permute-start.6 = (bf16[640,128]{1,0:T(8,128)(2,1)S(1)}, bf16[640,128]{1,0:T(8,128)(2,1)S(1)}, u32[]{:S(2)}, u32[]{:S(2)}) collective-permute-start(bf16[640,128]{1,0:T(8,128)(2,1)S(1)} %get-tuple-element.19), channel_id=1, source_target_pairs={{0,1},{1,0},{2,3},{3,2},{4,5},{5,4},{6,7},{7,6},{8,9},{9,8},{10,11... | collective-permute-start | bytes 491528 | tf_op jit(solution)/shard_map/ppermute | solution.py:43
  39.8 4.5 %collective-permute-start.7 = (bf16[320,128]{1,0:T(8,128)(2,1)S(1)}, bf16[320,128]{1,0:T(8,128)(2,1)S(1)}, u32[]{:S(2)}, u32[]{:S(2)}) collective-permute-start(bf16[320,128]{1,0:T(8,128)(2,1)S(1)} %get-tuple-element.22), channel_id=1, source_target_pairs={{0,8},{1,17},{2,18},{3,11},{4,12},{5,21},{6,22},{7,15},{8,0},{9,25... | collective-permute-start | bytes 245768 | tf_op jit(solution)/shard_map/ppermute | solution.py:43
  44.3 24.5 %copy-start.3 = (s32[1,8,3]{1,0,2:T(1,128)S(1)}, s32[1,8,3]{1,0,2:T(1,128)}, u32[]{:S(2)}) copy-start(s32[1,8,3]{1,0,2:T(1,128)} %param.8) | copy-start | bytes 292
  44.4 24.5 %copy-start.5 = (s32[1,8]{1,0:T(1,128)S(1)}, s32[1,8]{1,0:T(1,128)}, u32[]{:S(2)}) copy-start(s32[1,8]{1,0:T(1,128)} %counts.9) | copy-start | bytes 100
  44.4 4.1 %collective-permute-start.8 = (bf16[160,128]{1,0:T(8,128)(2,1)S(1)}, bf16[160,128]{1,0:T(8,128)(2,1)S(1)}, u32[]{:S(2)}, u32[]{:S(2)}) collective-permute-start(bf16[160,128]{1,0:T(8,128)(2,1)S(1)} %get-tuple-element.20), channel_id=1, source_target_pairs={{0,16},{1,9},{2,10},{3,19},{4,20},{5,13},{6,14},{7,23},{8,24},{9,1... | collective-permute-start | bytes 122888 | tf_op jit(solution)/shard_map/ppermute | solution.py:43
  46.5 26.4 %collective-permute-start.3 = (bf16[256,2048]{1,0:T(8,128)(2,1)S(1)}, bf16[256,2048]{1,0:T(8,128)(2,1)S(1)}, u32[]{:S(2)}, u32[]{:S(2)}) collective-permute-start(bf16[256,2048]{1,0:T(8,128)(2,1)S(1)} %slice_bitcast_fusion), channel_id=1, source_target_pairs={{1,0},{3,1},{0,2},{2,3},{5,4},{7,5},{4,6},{6,7},{9,8},{11,9},{8,10... | collective-permute-start | bytes 3145736 | tf_op jit(solution)/shard_map/ppermute | solution.py:33
  48.5 13.1 %collective-permute-start.11 = (bf16[160,128]{1,0:T(8,128)(2,1)S(1)}, bf16[160,128]{1,0:T(8,128)(2,1)S(1)}, u32[]{:S(2)}, u32[]{:S(2)}) collective-permute-start(bf16[160,128]{1,0:T(8,128)(2,1)S(1)} %fusion), channel_id=1, source_target_pairs={{0,3},{1,2},{2,1},{3,0},{4,7},{5,6},{6,5},{7,4},{8,11},{9,10},{10,... | collective-permute-start | bytes 122888 | tf_op jit(solution)/shard_map/ppermute | solution.py:43
  48.5 13.0 %collective-permute-start.10 = (bf16[160,128]{1,0:T(8,128)(2,1)S(1)}, bf16[160,128]{1,0:T(8,128)(2,1)S(1)}, u32[]{:S(2)}, u32[]{:S(2)}) collective-permute-start(bf16[160,128]{1,0:T(8,128)(2,1)S(1)} %fusion), channel_id=1, source_target_pairs={{0,4},{1,5},{2,6},{3,7},{4,0},{5,1},{6,2},{7,3},{8,12},{9,13},{10,... | collective-permute-start | bytes 122888 | tf_op jit(solution)/shard_map/ppermute | solution.py:43
  51.6 12.5 %collective-permute-start.9 = (bf16[160,128]{1,0:T(8,128)(2,1)S(1)}, bf16[160,128]{1,0:T(8,128)(2,1)S(1)}, u32[]{:S(2)}, u32[]{:S(2)}) collective-permute-start(bf16[160,128]{1,0:T(8,128)(2,1)S(1)} %fusion), channel_id=1, source_target_pairs={{0,7},{1,6},{2,5},{3,4},{4,3},{5,2},{6,1},{7,0},{8,15},{9,14},{10,... | collective-permute-start | bytes 122888 | tf_op jit(solution)/shard_map/ppermute | solution.py:43
  52.8 22.2 %collective-permute-start.4 = (bf16[96,2048]{1,0:T(8,128)(2,1)S(1)}, bf16[96,2048]{1,0:T(8,128)(2,1)S(1)}, u32[]{:S(2)}, u32[]{:S(2)}) collective-permute-start(bf16[96,2048]{1,0:T(8,128)(2,1)S(1)} %slice_bitcast_fusion.2), channel_id=1, source_target_pairs={{1,0},{3,1},{0,2},{2,3},{5,4},{7,5},{4,6},{6,7},{9,8},{11,9},{8,10... | collective-permute-start | bytes 1179656 | tf_op jit(solution)/shard_map/ppermute | solution.py:33
  64.2 4.1 %collective-permute-start.12 = (bf16[160,128]{1,0:T(8,128)(2,1)S(1)}, bf16[160,128]{1,0:T(8,128)(2,1)S(1)}, u32[]{:S(2)}, u32[]{:S(2)}) collective-permute-start(bf16[160,128]{1,0:T(8,128)(2,1)S(1)} %multiply_convert_fusion), channel_id=1, source_target_pairs={{0,16},{1,9},{2,10},{3,19},{4,20},{5,13},{6,14},{7,23},{8,24},{9,1... | collective-permute-start | bytes 122888 | tf_op jit(solution)/shard_map/ppermute | solution.py:43
  65.8 9.2 %collective-permute-start.5 = (bf16[160,2048]{1,0:T(8,128)(2,1)S(1)}, bf16[160,2048]{1,0:T(8,128)(2,1)S(1)}, u32[]{:S(2)}, u32[]{:S(2)}) collective-permute-start(bf16[160,2048]{1,0:T(8,128)(2,1)S(1)} %slice_bitcast_fusion.1), channel_id=1, source_target_pairs={{1,0},{3,1},{0,2},{2,3},{5,4},{7,5},{4,6},{6,7},{9,8},{11,9},{8,10... | collective-permute-start | bytes 1966088 | tf_op jit(solution)/shard_map/ppermute | solution.py:33
  68.3 4.5 %collective-permute-start.13 = (bf16[320,128]{1,0:T(8,128)(2,1)S(1)}, bf16[320,128]{1,0:T(8,128)(2,1)S(1)}, u32[]{:S(2)}, u32[]{:S(2)}) collective-permute-start(bf16[320,128]{1,0:T(8,128)(2,1)S(1)} %pad_maximum_fusion.1), channel_id=1, source_target_pairs={{0,8},{1,17},{2,18},{3,11},{4,12},{5,21},{6,22},{7,15},{8,0},{9,25... | collective-permute-start | bytes 245768 | tf_op jit(solution)/shard_map/ppermute | solution.py:43
  72.8 5.1 %collective-permute-start.14 = (bf16[640,128]{1,0:T(8,128)(2,1)S(1)}, bf16[640,128]{1,0:T(8,128)(2,1)S(1)}, u32[]{:S(2)}, u32[]{:S(2)}) collective-permute-start(bf16[640,128]{1,0:T(8,128)(2,1)S(1)} %pad_maximum_fusion.mine_ref), channel_id=1, source_target_pairs={{0,1},{1,0},{2,3},{3,2},{4,5},{5,4},{6,7},{7,6},{8,9},{9,8},{10,11... | collective-permute-start | bytes 491528 | tf_op jit(solution)/shard_map/ppermute | solution.py:43

commit v7 on v6

--- a/solution.py
+++ b/solution.py
@@ -173,12 +173,15 @@
         gamma_ref[:, at] = gamma_in[:, at] + (own + far) * nn(mt_ref[...], r_ref[:, at])
 
 
-def last_gamma_kernel(codes, counts, b_ref, over_ref, gamma_in, *refs):
-    parts, (out_ref, held, sems, r_ref, mt_ref, m_ref) = refs[:-6], refs[-6:]
-    own, far = weights(codes, counts, 3 - first_round(lax.axis_index("mem")))
+def amp_kernel(b_ref, over_ref, *refs):
+    parts, (mt_ref, r_ref, m_ref) = refs[:-3], refs[-3:]
     joined(parts, r_ref)
     vir = b_ref.shape[0]
     mt_ref[...] = flat_amp(slice(vir - r_ref.shape[0], vir), b_ref, r_ref, over_ref, m_ref)
+
+
+def last_gamma_kernel(codes, counts, gamma_in, mt_ref, r_ref, out_ref, held, sems):
+    own, far = weights(codes, counts, 3 - first_round(lax.axis_index("mem")))
     strips_out(
         out_ref, held, sems, STRIPS, lambda at: gamma_in[:, at] + (own + far) * nn(mt_ref[...], r_ref[:, at])
     )
@@ -286,10 +289,12 @@
     gamma = call(second_gamma_kernel, wide, bounce, (0, 1), 6, dot)(
         pair_code, pair_count, block, over_second, gamma, second[0]
     )
-    result = call(
-        last_gamma_kernel, shape((vir, aux), BF16), [*out_scratch, pltpu.VMEM((vir // 2, aux), BF16), *bounce],
-        (0, 1), 7, dot, any_space,
-    )(pair_code, pair_count, block, over_second, gamma, *second[1:])
+    rest, rows = call(
+        amp_kernel, (shape((vir, vir // 2), BF16), shape((vir // 2, aux), BF16)), bounce[1:], (), 4, dot // 2
+    )(block, over_second, *second[1:])
+    result = call(last_gamma_kernel, shape((vir, aux), BF16), out_scratch, (0, 1), 5, dot // 2, any_space)(
+        pair_code, pair_count, gamma, rest, rows
+    )
     lagrangian = call(
         apply_kernel, shape((vir, aux), BF16), [pltpu.VMEM((vir, vir), BF16), *out_scratch], (), 3, dot,
         any_space,

time: 80.3 us -> 82.6 us (1.029)
  waiting for transfers between devices: 44.3 us -> 46 us
    ppermute x6, waiting for transfers between devices: 22.8 us -> 26.6 us  [turn(): return lax.ppermute(value, 'mem', pairs)]
    ppermute x9, waiting for transfers between devices: 21.5 us -> 19.4 us  [swap(): return lax.ppermute(value, ('grp', 'mem'), pairs)]
    pallas_call x6 -> x7, Pallas kernels: 14.8 us -> 14.9 us  [call(): kernel_call(kernel, outs, scratch, smem, count, flops, out_spec)(*args)]
where the time goes in v7:
time: 82.6 us; the launch traced here: 82.3 us
  waiting for transfers between devices  46 us (56%)
  Pallas kernels  14.9 us (18%)
  starting transfers between devices  14.4 us (17%)
  local copies, waits for them, and re-layouts  3.1 us (4%)
  between operations  2.92 us (4%)
  other arithmetic  0.99 us (1%)
    ppermute x6, waiting for transfers between devices, turn(): return lax.ppermute(value, 'mem', pairs)  26.6 us
    ppermute x9, waiting for transfers between devices, swap(): return lax.ppermute(value, ('grp', 'mem'), pairs)  19.4 us
    pallas_call x7, Pallas kernels, call(): kernel_call(kernel, outs, scratch, smem, count, flops, out_spec)(*args)  14.9 us
    ppermute x9, starting transfers between devices, swap(): return lax.ppermute(value, ('grp', 'mem'), pairs)  10.9 us
    ppermute x6, starting transfers between devices, turn(): return lax.ppermute(value, 'mem', pairs)  3.47 us
    unnamed x12, local copies, waits for them, and re-layouts  2.93 us
  transfers between devices with their start and end apart: 15, of which 8 were waited for; matrix products, arithmetic and copies ran while one was open for 1% of the time, Pallas kernels for 13%

profile of v7, /device:TPU:0, one launch (start us, length us, event | category | flops | bytes accessed | tf_op | source)
XLA Modules:
  0.0 82.3 jit_solution(6865073556392977974)
XLA Ops:
  0.6 0.6 collective-permute-start.2
  1.2 2.1 %collective-permute-start = (bf16[1]{0:T(256)(128)(2,1)}, bf16[1]{0:T(256)(128)(2,1)}, u32[]{:S(2)}, u32[]{:S(2)}) collective-permute-start(bf16[1]{0:T(256)(128)(2,1)} %param.6), channel_id=1, source_target_pairs={{0,1},{1,3},{2,0},{3,2},{4,5},{5,7},{6,4},{7,6},{8,9},{9,11},{10,8... | collective-permute-start | bytes 14 | tf_op jit(solution)/shard_map/ppermute | solution.py:33
  3.3 0.6 collective-permute-start.1
  4.6 0.7 reshape.14
  5.3 22.7 %collective-permute-done = bf16[1]{0:T(256)(128)(2,1)} collective-permute-done((bf16[1]{0:T(256)(128)(2,1)}, bf16[1]{0:T(256)(128)(2,1)}, u32[]{:S(2)}, u32[]{:S(2)}) %collective-permute-start) | collective-permute-done | bytes 34 | tf_op jit(solution)/shard_map/ppermute | solution.py:33
  28.7 0.0 collective-permute-done.1
  29.4 0.0 copy-start
  29.4 1.6 %copy-done = bf16[1,512,2048]{2,1,0:T(8,128)(2,1)S(1)} copy-done((bf16[1,512,2048]{2,1,0:T(8,128)(2,1)S(1)}, bf16[1,512,2048]{2,1,0:T(8,128)(2,1)}, u32[]{:S(2)}) %copy-start) | copy-done | bytes 2097176
  31.0 0.7 copy-done.2
  31.7 0.7 copy-done.4
  32.3 3.4 %shard_map.68 = (f32[512,512]{1,0:T(8,128)S(1)}, f32[512,512]{1,0:T(8,128)S(1)}, f32[512,512]{1,0:T(8,128)S(1)}, f32[512,2048]{1,0:T(8,128)S(1)}, f32[320,128]{1,0:T(8,128)S(1)}, /*index=5*/f32[160,128]{1,0:T(8,128)S(1)}) custom-call(bf16[512,2048]{1,0:T(8,128)(2,1)S(1)} %bitcast.12, f32[1,512]{1,0:T(1,128)S(1)} %bitcast.22, ...), custom_call_target="tpu_custom_call" | custom-call | flops 2147483648 | bytes 1048576 | tf_op jit(solution)/shard_map/pallas_call | solution.py:205
  35.8 0.0 collective-permute-done.2.r_ref
  35.8 2.5 %shard_map.69 = (bf16[512,512]{1,0:T(8,128)(2,1)S(1)}, f32[640,128]{1,0:T(8,128)S(1)}, bf16[640,128]{1,0:T(8,128)(2,1)S(1)}) custom-call(bf16[512,2048]{1,0:T(8,128)(2,1)S(1)} %bitcast.13, bf16[512,2048]{1,0:T(8,128)(2,1)S(1)} %collective-permute-done.2.r_ref, f32[512,512]{1,0:T(8,128)S(1)} %get-tuple-element.15.over_ref, s32[3,1,8]{2,1,0:T(1,128)S(1)} %bitcast.18, ...), custom_call_target="tpu_custom_call" | custom-call | flops 1073741824 | bytes 1048576 | tf_op jit(solution)/shard_map/pallas_call | solution.py:205
  38.2 0.0 copy-start.1
  38.3 0.1 collective-permute-start.6
  38.3 1.4 %collective-permute-done.6 = bf16[640,128]{1,0:T(8,128)(2,1)S(1)} collective-permute-done((bf16[640,128]{1,0:T(8,128)(2,1)S(1)}, bf16[640,128]{1,0:T(8,128)(2,1)S(1)}, u32[]{:S(2)}, u32[]{:S(2)}) %collective-permute-start.6) | collective-permute-done | bytes 163872 | tf_op jit(solution)/shard_map/ppermute | solution.py:43
  39.8 2.0 %collective-permute-start.7 = (bf16[320,128]{1,0:T(8,128)(2,1)S(1)}, bf16[320,128]{1,0:T(8,128)(2,1)S(1)}, u32[]{:S(2)}, u32[]{:S(2)}) collective-permute-start(bf16[320,128]{1,0:T(8,128)(2,1)S(1)} %get-tuple-element.26), channel_id=1, source_target_pairs={{0,8},{1,17},{2,18},{3,11},{4,12},{5,21},{6,22},{7,15},{8,0},{9,25... | collective-permute-start | bytes 245768 | tf_op jit(solution)/shard_map/ppermute | solution.py:43
  41.8 2.5 %collective-permute-done.7 = bf16[320,128]{1,0:T(8,128)(2,1)S(1)} collective-permute-done((bf16[320,128]{1,0:T(8,128)(2,1)S(1)}, bf16[320,128]{1,0:T(8,128)(2,1)S(1)}, u32[]{:S(2)}, u32[]{:S(2)}) %collective-permute-start.7) | collective-permute-done | bytes 81952 | tf_op jit(solution)/shard_map/ppermute | solution.py:43
  44.4 2.0 %collective-permute-start.8 = (bf16[160,128]{1,0:T(8,128)(2,1)S(1)}, bf16[160,128]{1,0:T(8,128)(2,1)S(1)}, u32[]{:S(2)}, u32[]{:S(2)}) collective-permute-start(bf16[160,128]{1,0:T(8,128)(2,1)S(1)} %get-tuple-element.24), channel_id=1, source_target_pairs={{0,16},{1,9},{2,10},{3,19},{4,20},{5,13},{6,14},{7,23},{8,24},{9,1... | collective-permute-start | bytes 122888 | tf_op jit(solution)/shard_map/ppermute | solution.py:43
  46.4 0.0 copy-done.1
  46.4 0.1 slice_bitcast_fusion
  46.5 0.1 collective-permute-start.3
  46.6 1.9 %collective-permute-done.8 = bf16[160,128]{1,0:T(8,128)(2,1)S(1)} collective-permute-done((bf16[160,128]{1,0:T(8,128)(2,1)S(1)}, bf16[160,128]{1,0:T(8,128)(2,1)S(1)}, u32[]{:S(2)}, u32[]{:S(2)}) %collective-permute-start.8) | collective-permute-done | bytes 40992 | tf_op jit(solution)/shard_map/ppermute | solution.py:43
  48.5 0.1 collective-permute-start.11
  48.6 3.1 %collective-permute-start.10 = (bf16[160,128]{1,0:T(8,128)(2,1)S(1)}, bf16[160,128]{1,0:T(8,128)(2,1)S(1)}, u32[]{:S(2)}, u32[]{:S(2)}) collective-permute-start(bf16[160,128]{1,0:T(8,128)(2,1)S(1)} %fusion), channel_id=1, source_target_pairs={{0,4},{1,5},{2,6},{3,7},{4,0},{5,1},{6,2},{7,3},{8,12},{9,13},{10,... | collective-permute-start | bytes 122888 | tf_op jit(solution)/shard_map/ppermute | solution.py:43
  51.7 1.1 %collective-permute-start.9 = (bf16[160,128]{1,0:T(8,128)(2,1)S(1)}, bf16[160,128]{1,0:T(8,128)(2,1)S(1)}, u32[]{:S(2)}, u32[]{:S(2)}) collective-permute-start(bf16[160,128]{1,0:T(8,128)(2,1)S(1)} %fusion), channel_id=1, source_target_pairs={{0,7},{1,6},{2,5},{3,4},{4,3},{5,2},{6,1},{7,0},{8,15},{9,14},{10,... | collective-permute-start | bytes 122888 | tf_op jit(solution)/shard_map/ppermute | solution.py:43
  52.8 0.1 collective-permute-start.5
  52.9 8.7 %collective-permute-done.11 = bf16[160,128]{1,0:T(8,128)(2,1)S(1)} collective-permute-done((bf16[160,128]{1,0:T(8,128)(2,1)S(1)}, bf16[160,128]{1,0:T(8,128)(2,1)S(1)}, u32[]{:S(2)}, u32[]{:S(2)}) %collective-permute-start.11) | collective-permute-done | bytes 40992 | tf_op jit(solution)/shard_map/ppermute | solution.py:43
  61.6 0.0 collective-permute-done.10
  61.6 2.6 %collective-permute-done.9 = bf16[160,128]{1,0:T(8,128)(2,1)S(1)} collective-permute-done((bf16[160,128]{1,0:T(8,128)(2,1)S(1)}, bf16[160,128]{1,0:T(8,128)(2,1)S(1)}, u32[]{:S(2)}, u32[]{:S(2)}) %collective-permute-start.9) | collective-permute-done | bytes 40992 | tf_op jit(solution)/shard_map/ppermute | solution.py:43
  64.2 1.6 %collective-permute-start.12 = (bf16[160,128]{1,0:T(8,128)(2,1)S(1)}, bf16[160,128]{1,0:T(8,128)(2,1)S(1)}, u32[]{:S(2)}, u32[]{:S(2)}) collective-permute-start(bf16[160,128]{1,0:T(8,128)(2,1)S(1)} %multiply_convert_fusion), channel_id=1, source_target_pairs={{0,16},{1,9},{2,10},{3,19},{4,20},{5,13},{6,14},{7,23},{8,24},{9,1... | collective-permute-start | bytes 122888 | tf_op jit(solution)/shard_map/ppermute | solution.py:43
  65.8 0.1 collective-permute-start.4
  65.9 2.4 %collective-permute-done.12 = bf16[160,128]{1,0:T(8,128)(2,1)S(1)} collective-permute-done((bf16[160,128]{1,0:T(8,128)(2,1)S(1)}, bf16[160,128]{1,0:T(8,128)(2,1)S(1)}, u32[]{:S(2)}, u32[]{:S(2)}) %collective-permute-start.12) | collective-permute-done | bytes 40992 | tf_op jit(solution)/shard_map/ppermute | solution.py:43
  68.3 0.6 collective-permute-start.13
  68.9 3.9 %collective-permute-done.4.refs_0_ = bf16[96,2048]{1,0:T(8,128)(2,1)S(1)} collective-permute-done((bf16[96,2048]{1,0:T(8,128)(2,1)S(1)}, bf16[96,2048]{1,0:T(8,128)(2,1)S(1)}, u32[]{:S(2)}, u32[]{:S(2)}) %collective-permute-start.4) | collective-permute-done | bytes 393248 | tf_op jit(solution)/shard_map/ppermute | solution.py:33
  72.8 0.0 collective-permute-done.5.refs_1_
  72.8 0.8 shard_map.72
  73.6 0.0 collective-permute-done.13
  73.6 0.1 fusion.2
  73.7 0.4 collective-permute-start.14
  74.1 0.0 copy-done.3
  74.1 1.8 %shard_map.70.gamma_in = f32[512,2048]{1,0:T(8,128)S(1)} custom-call(s32[3,1,8]{2,1,0:T(1,128)S(1)} %bitcast.19, s32[1,8]{1,0:T(1,128)S(1)} %copy-done.4, f32[512,2048]{1,0:T(8,128)S(1)} %get-tuple-element.14.gamma_in, bf16[512,512]{1,0:T(8,128)(2,1)S(1)} %get-tuple-element.17.mt_ref, bf16[512,2048]{1,0:T(8,128)(2,1)S(1)} %collective-permute-done.2.r_ref), custom_call_target="tpu_custom_call" | custom-call | flops 1073741824 | bytes 1048576 | tf_op jit(solution)/shard_map/pallas_call | solution.py:205
  75.9 0.0 collective-permute-done.3.r_ref
  75.9 0.0 copy-done.5
  75.9 2.0 %shard_map.71.gamma_in = f32[512,2048]{1,0:T(8,128)S(1)} custom-call(s32[3,1,8]{2,1,0:T(1,128)S(1)} %bitcast.20, s32[1,8]{1,0:T(1,128)S(1)} %copy-done.5, bf16[512,2048]{1,0:T(8,128)(2,1)S(1)} %bitcast.15, f32[512,512]{1,0:T(8,128)S(1)} %get-tuple-element.13.over_ref, f32[512,2048]{1,0:T(8,128)S(1)} %shard_map.70.gamma_in, ...), custom_call_target="tpu_custom_call" | custom-call | flops 1073741824 | bytes 1048576 | tf_op jit(solution)/shard_map/pallas_call | solution.py:205
  78.0 2.2 %shard_map.73 = bf16[512,2048]{1,0:T(8,128)(2,1)} custom-call(s32[3,1,8]{2,1,0:T(1,128)S(1)} %bitcast.21, s32[1,8]{1,0:T(1,128)S(1)} %copy-done.5, f32[512,2048]{1,0:T(8,128)S(1)} %shard_map.71.gamma_in, bf16[512,256]{1,0:T(8,128)(2,1)S(1)} %get-tuple-element.18.mt_ref, bf16[256,2048]{1,0:T(8,128)(2,1)S(1)} %get-tuple-element.19.r_ref), custom_call_target="tpu_custom_call" | custom-call | flops 536870912 | bytes 1048576 | tf_op jit(solution)/shard_map/pallas_call | solution.py:205
  80.2 0.0 collective-permute-done.14.other_ref
  80.2 2.1 %shard_map.74 = bf16[512,2048]{1,0:T(8,128)(2,1)} custom-call(bf16[640,128]{1,0:T(8,128)(2,1)S(1)} %pad_maximum_fusion.mine_ref, bf16[640,128]{1,0:T(8,128)(2,1)S(1)} %collective-permute-done.14.other_ref, bf16[512,2048]{1,0:T(8,128)(2,1)S(1)} %bitcast.16), custom_call_target="tpu_custom_call" | custom-call | flops 1073741824 | bytes 1048576 | tf_op jit(solution)/shard_map/pallas_call | solution.py:205
  (15 shorter events, 0.3 us)
Async XLA Ops:
  0.6 35.1 %collective-permute-start.2 = (bf16[512,2048]{1,0:T(8,128)(2,1)}, bf16[512,2048]{1,0:T(8,128)(2,1)S(1)}, u32[]{:S(2)}, u32[]{:S(2)}) collective-permute-start(bf16[512,2048]{1,0:T(8,128)(2,1)} %bitcast.11), channel_id=1, source_target_pairs={{0,1},{1,3},{2,0},{3,2},{4,5},{5,7},{6,4},{7,6},{8,9},{9,11},{10,8... | collective-permute-start | bytes 6291464 | tf_op jit(solution)/shard_map/ppermute | solution.py:33
  1.2 26.8 %collective-permute-start = (bf16[1]{0:T(256)(128)(2,1)}, bf16[1]{0:T(256)(128)(2,1)}, u32[]{:S(2)}, u32[]{:S(2)}) collective-permute-start(bf16[1]{0:T(256)(128)(2,1)} %param.6), channel_id=1, source_target_pairs={{0,1},{1,3},{2,0},{3,2},{4,5},{5,7},{6,4},{7,6},{8,9},{9,11},{10,8... | collective-permute-start | bytes 14 | tf_op jit(solution)/shard_map/ppermute | solution.py:33
  3.3 25.4 %collective-permute-start.1 = (bf16[1]{0:T(256)(128)(2,1)}, bf16[1]{0:T(256)(128)(2,1)}, u32[]{:S(2)}, u32[]{:S(2)}) collective-permute-start(bf16[1]{0:T(256)(128)(2,1)} %param.6), channel_id=1, source_target_pairs={{1,0},{3,1},{0,2},{2,3},{5,4},{7,5},{4,6},{6,7},{9,8},{11,9},{8,10... | collective-permute-start | bytes 14 | tf_op jit(solution)/shard_map/ppermute | solution.py:33
  29.4 1.6 %copy-start = (bf16[1,512,2048]{2,1,0:T(8,128)(2,1)S(1)}, bf16[1,512,2048]{2,1,0:T(8,128)(2,1)}, u32[]{:S(2)}) copy-start(bf16[1,512,2048]{2,1,0:T(8,128)(2,1)} %param.5) | copy-start | bytes 6291460
  31.0 0.7 copy-start.2
  31.7 0.7 copy-start.4
  38.2 8.2 %copy-start.1 = (bf16[1,512,2048]{2,1,0:T(8,128)(2,1)S(1)}, bf16[1,512,2048]{2,1,0:T(8,128)(2,1)}, u32[]{:S(2)}) copy-start(bf16[1,512,2048]{2,1,0:T(8,128)(2,1)} %param.5) | copy-start | bytes 6291460
  38.3 1.5 %collective-permute-start.6 = (bf16[640,128]{1,0:T(8,128)(2,1)S(1)}, bf16[640,128]{1,0:T(8,128)(2,1)S(1)}, u32[]{:S(2)}, u32[]{:S(2)}) collective-permute-start(bf16[640,128]{1,0:T(8,128)(2,1)S(1)} %get-tuple-element.23), channel_id=1, source_target_pairs={{0,1},{1,0},{2,3},{3,2},{4,5},{5,4},{6,7},{7,6},{8,9},{9,8},{10,11... | collective-permute-start | bytes 491528 | tf_op jit(solution)/shard_map/ppermute | solution.py:43
  39.8 4.5 %collective-permute-start.7 = (bf16[320,128]{1,0:T(8,128)(2,1)S(1)}, bf16[320,128]{1,0:T(8,128)(2,1)S(1)}, u32[]{:S(2)}, u32[]{:S(2)}) collective-permute-start(bf16[320,128]{1,0:T(8,128)(2,1)S(1)} %get-tuple-element.26), channel_id=1, source_target_pairs={{0,8},{1,17},{2,18},{3,11},{4,12},{5,21},{6,22},{7,15},{8,0},{9,25... | collective-permute-start | bytes 245768 | tf_op jit(solution)/shard_map/ppermute | solution.py:43
  44.4 4.1 %collective-permute-start.8 = (bf16[160,128]{1,0:T(8,128)(2,1)S(1)}, bf16[160,128]{1,0:T(8,128)(2,1)S(1)}, u32[]{:S(2)}, u32[]{:S(2)}) collective-permute-start(bf16[160,128]{1,0:T(8,128)(2,1)S(1)} %get-tuple-element.24), channel_id=1, source_target_pairs={{0,16},{1,9},{2,10},{3,19},{4,20},{5,13},{6,14},{7,23},{8,24},{9,1... | collective-permute-start | bytes 122888 | tf_op jit(solution)/shard_map/ppermute | solution.py:43
  46.5 29.4 %collective-permute-start.3 = (bf16[256,2048]{1,0:T(8,128)(2,1)S(1)}, bf16[256,2048]{1,0:T(8,128)(2,1)S(1)}, u32[]{:S(2)}, u32[]{:S(2)}) collective-permute-start(bf16[256,2048]{1,0:T(8,128)(2,1)S(1)} %slice_bitcast_fusion), channel_id=1, source_target_pairs={{1,0},{3,1},{0,2},{2,3},{5,4},{7,5},{4,6},{6,7},{9,8},{11,9},{8,10... | collective-permute-start | bytes 3145736 | tf_op jit(solution)/shard_map/ppermute | solution.py:33
  48.5 13.1 %collective-permute-start.11 = (bf16[160,128]{1,0:T(8,128)(2,1)S(1)}, bf16[160,128]{1,0:T(8,128)(2,1)S(1)}, u32[]{:S(2)}, u32[]{:S(2)}) collective-permute-start(bf16[160,128]{1,0:T(8,128)(2,1)S(1)} %fusion), channel_id=1, source_target_pairs={{0,3},{1,2},{2,1},{3,0},{4,7},{5,6},{6,5},{7,4},{8,11},{9,10},{10,... | collective-permute-start | bytes 122888 | tf_op jit(solution)/shard_map/ppermute | solution.py:43
  48.6 13.0 %collective-permute-start.10 = (bf16[160,128]{1,0:T(8,128)(2,1)S(1)}, bf16[160,128]{1,0:T(8,128)(2,1)S(1)}, u32[]{:S(2)}, u32[]{:S(2)}) collective-permute-start(bf16[160,128]{1,0:T(8,128)(2,1)S(1)} %fusion), channel_id=1, source_target_pairs={{0,4},{1,5},{2,6},{3,7},{4,0},{5,1},{6,2},{7,3},{8,12},{9,13},{10,... | collective-permute-start | bytes 122888 | tf_op jit(solution)/shard_map/ppermute | solution.py:43
  51.7 12.5 %collective-permute-start.9 = (bf16[160,128]{1,0:T(8,128)(2,1)S(1)}, bf16[160,128]{1,0:T(8,128)(2,1)S(1)}, u32[]{:S(2)}, u32[]{:S(2)}) collective-permute-start(bf16[160,128]{1,0:T(8,128)(2,1)S(1)} %fusion), channel_id=1, source_target_pairs={{0,7},{1,6},{2,5},{3,4},{4,3},{5,2},{6,1},{7,0},{8,15},{9,14},{10,... | collective-permute-start | bytes 122888 | tf_op jit(solution)/shard_map/ppermute | solution.py:43
  52.8 20.0 %collective-permute-start.5 = (bf16[160,2048]{1,0:T(8,128)(2,1)S(1)}, bf16[160,2048]{1,0:T(8,128)(2,1)S(1)}, u32[]{:S(2)}, u32[]{:S(2)}) collective-permute-start(bf16[160,2048]{1,0:T(8,128)(2,1)S(1)} %slice_bitcast_fusion.1), channel_id=1, source_target_pairs={{1,0},{3,1},{0,2},{2,3},{5,4},{7,5},{4,6},{6,7},{9,8},{11,9},{8,10... | collective-permute-start | bytes 1966088 | tf_op jit(solution)/shard_map/ppermute | solution.py:33
  64.2 4.1 %collective-permute-start.12 = (bf16[160,128]{1,0:T(8,128)(2,1)S(1)}, bf16[160,128]{1,0:T(8,128)(2,1)S(1)}, u32[]{:S(2)}, u32[]{:S(2)}) collective-permute-start(bf16[160,128]{1,0:T(8,128)(2,1)S(1)} %multiply_convert_fusion), channel_id=1, source_target_pairs={{0,16},{1,9},{2,10},{3,19},{4,20},{5,13},{6,14},{7,23},{8,24},{9,1... | collective-permute-start | bytes 122888 | tf_op jit(solution)/shard_map/ppermute | solution.py:43
  65.8 7.0 %collective-permute-start.4 = (bf16[96,2048]{1,0:T(8,128)(2,1)S(1)}, bf16[96,2048]{1,0:T(8,128)(2,1)S(1)}, u32[]{:S(2)}, u32[]{:S(2)}) collective-permute-start(bf16[96,2048]{1,0:T(8,128)(2,1)S(1)} %slice_bitcast_fusion.2), channel_id=1, source_target_pairs={{1,0},{3,1},{0,2},{2,3},{5,4},{7,5},{4,6},{6,7},{9,8},{11,9},{8,10... | collective-permute-start | bytes 1179656 | tf_op jit(solution)/shard_map/ppermute | solution.py:33
  68.3 5.3 %collective-permute-start.13 = (bf16[320,128]{1,0:T(8,128)(2,1)S(1)}, bf16[320,128]{1,0:T(8,128)(2,1)S(1)}, u32[]{:S(2)}, u32[]{:S(2)}) collective-permute-start(bf16[320,128]{1,0:T(8,128)(2,1)S(1)} %pad_maximum_fusion.1), channel_id=1, source_target_pairs={{0,8},{1,17},{2,18},{3,11},{4,12},{5,21},{6,22},{7,15},{8,0},{9,25... | collective-permute-start | bytes 245768 | tf_op jit(solution)/shard_map/ppermute | solution.py:43
  72.8 1.3 %copy-start.3 = (s32[1,8,3]{1,0,2:T(1,128)S(1)}, s32[1,8,3]{1,0,2:T(1,128)}, u32[]{:S(2)}) copy-start(s32[1,8,3]{1,0,2:T(1,128)} %param.8) | copy-start | bytes 292
  73.7 6.5 %collective-permute-start.14 = (bf16[640,128]{1,0:T(8,128)(2,1)S(1)}, bf16[640,128]{1,0:T(8,128)(2,1)S(1)}, u32[]{:S(2)}, u32[]{:S(2)}) collective-permute-start(bf16[640,128]{1,0:T(8,128)(2,1)S(1)} %pad_maximum_fusion.mine_ref), channel_id=1, source_target_pairs={{0,1},{1,0},{2,3},{3,2},{4,5},{5,4},{6,7},{7,6},{8,9},{9,8},{10,11... | collective-permute-start | bytes 491528 | tf_op jit(solution)/shard_map/ppermute | solution.py:43
  74.1 1.8 %copy-start.5 = (s32[1,8]{1,0:T(1,128)S(1)}, s32[1,8]{1,0:T(1,128)}, u32[]{:S(2)}) copy-start(s32[1,8]{1,0:T(1,128)} %counts.9) | copy-start | bytes 100

commit v8 on v7

--- a/solution.py
+++ b/solution.py
@@ -152,13 +152,6 @@
         copy.wait()
 
 
-def joined(parts, held):
-    start = 0
-    for part in parts:
-        held[start : start + part.shape[0], :] = part[...]
-        start += part.shape[0]
-
-
 def flat_amp(at, b_ref, r_ref, over_ref, m_ref):
     m_ref[...] = (nt(r_ref[...], b_ref[...]) * over_ref[at, :]).astype(BF16)
     return m_ref[...].T
@@ -166,18 +159,20 @@
 
 def second_gamma_kernel(codes, counts, b_ref, over_ref, gamma_in, r_ref, gamma_ref, mt_ref, m_ref):
     own, far = weights(codes, counts, 3 - first_round(lax.axis_index("mem")))
-    mt_ref[...] = flat_amp(slice(0, r_ref.shape[0]), b_ref, r_ref, over_ref, m_ref)
+    rows = slice(0, m_ref.shape[0])
+    mt_ref[...] = flat_amp(rows, b_ref, r_ref.at[rows, :], over_ref, m_ref)
     aux = gamma_ref.shape[1]
     for p in range(STRIPS):
         at = pl.ds(p * (aux // STRIPS), aux // STRIPS)
-        gamma_ref[:, at] = gamma_in[:, at] + (own + far) * nn(mt_ref[...], r_ref[:, at])
-
-
-def amp_kernel(b_ref, over_ref, *refs):
-    parts, (mt_ref, r_ref, m_ref) = refs[:-3], refs[-3:]
-    joined(parts, r_ref)
-    vir = b_ref.shape[0]
-    mt_ref[...] = flat_amp(slice(vir - r_ref.shape[0], vir), b_ref, r_ref, over_ref, m_ref)
+        gamma_ref[:, at] = gamma_in[:, at] + (own + far) * nn(mt_ref[...], r_ref[rows, at])
+
+
+def amp_kernel(b_ref, over_ref, first_ref, last_ref, mt_ref, r_ref, m_ref):
+    vir, rows = b_ref.shape[0], r_ref.shape[0]
+    left = first_ref.shape[0] - (vir - rows)
+    r_ref[:left, :] = first_ref[vir - rows :, :]
+    r_ref[left:, :] = last_ref[...]
+    mt_ref[...] = flat_amp(slice(vir - rows, vir), b_ref, r_ref, over_ref, m_ref)
 
 
 def last_gamma_kernel(codes, counts, gamma_in, mt_ref, r_ref, out_ref, held, sems):
@@ -279,7 +274,7 @@
     other = swap(mine, [(0, 1), (0, 1)])
 
     unit = vir // 16
-    cuts = (0, 8 * unit, 11 * unit, vir)
+    cuts = (0, 10 * unit, vir)
     parts = [block[a:b] for a, b in zip(cuts, cuts[1:])]
     second = [turn(part, True) for part in parts]
     gamma = call(first_gamma_kernel, wide, (), (0, 1), 5, dot)(
@@ -291,7 +286,7 @@
     )
     rest, rows = call(
         amp_kernel, (shape((vir, vir // 2), BF16), shape((vir // 2, aux), BF16)), bounce[1:], (), 4, dot // 2
-    )(block, over_second, *second[1:])
+    )(block, over_second, *second)
     result = call(last_gamma_kernel, shape((vir, aux), BF16), out_scratch, (0, 1), 5, dot // 2, any_space)(
         pair_code, pair_count, gamma, rest, rows
     )

time: 82.6 us -> 88.9 us (1.076)
  waiting for transfers between devices: 46 us -> 52.9 us
    ppermute x9, waiting for transfers between devices: 19.4 us -> 30.1 us  [swap(): return lax.ppermute(value, ('grp', 'mem'), pairs)]
    ppermute x6 -> x5, waiting for transfers between devices: 26.6 us -> 22.8 us  [turn(): return lax.ppermute(value, 'mem', pairs)]
    ppermute x6 -> x5, starting transfers between devices: 3.47 us -> 3.4 us  [turn(): return lax.ppermute(value, 'mem', pairs)]
  transfers between devices with their start and end apart: 15 -> 14, of which waited for: 8 -> 8; matrix products, arithmetic and copies ran while one was open for 1% -> 1% of each run, Pallas kernels for 13% -> 12%
where the time goes in v8:
time: 88.9 us; the launch traced here: 88.6 us
  waiting for transfers between devices  52.9 us (60%)
  Pallas kernels  14.9 us (17%)
  starting transfers between devices  13.9 us (16%)
  local copies, waits for them, and re-layouts  3.12 us (4%)
  between operations  2.8 us (3%)
  other arithmetic  0.98 us (1%)
    ppermute x9, waiting for transfers between devices, swap(): return lax.ppermute(value, ('grp', 'mem'), pairs)  30.1 us
    ppermute x5, waiting for transfers between devices, turn(): return lax.ppermute(value, 'mem', pairs)  22.8 us
    pallas_call x7, Pallas kernels, call(): kernel_call(kernel, outs, scratch, smem, count, flops, out_spec)(*args)  14.9 us
    ppermute x9, starting transfers between devices, swap(): return lax.ppermute(value, ('grp', 'mem'), pairs)  10.5 us
    ppermute x5, starting transfers between devices, turn(): return lax.ppermute(value, 'mem', pairs)  3.4 us
    unnamed x12, local copies, waits for them, and re-layouts  2.94 us
  transfers between devices with their start and end apart: 14, of which 8 were waited for; matrix products, arithmetic and copies ran while one was open for 1% of the time, Pallas kernels for 12%

profile of v8, /device:TPU:0, one launch (start us, length us, event | category | flops | bytes accessed | tf_op | source)
XLA Modules:
  0.0 88.6 jit_solution(8836827158891245311)
XLA Ops:
  0.6 0.6 collective-permute-start.2
  1.2 2.1 %collective-permute-start = (bf16[1]{0:T(256)(128)(2,1)}, bf16[1]{0:T(256)(128)(2,1)}, u32[]{:S(2)}, u32[]{:S(2)}) collective-permute-start(bf16[1]{0:T(256)(128)(2,1)} %param.6), channel_id=1, source_target_pairs={{0,1},{1,3},{2,0},{3,2},{4,5},{5,7},{6,4},{7,6},{8,9},{9,11},{10,8... | collective-permute-start | bytes 14 | tf_op jit(solution)/shard_map/ppermute | solution.py:33
  3.3 0.6 collective-permute-start.1
  4.6 0.7 reshape.13
  5.3 22.8 %collective-permute-done = bf16[1]{0:T(256)(128)(2,1)} collective-permute-done((bf16[1]{0:T(256)(128)(2,1)}, bf16[1]{0:T(256)(128)(2,1)}, u32[]{:S(2)}, u32[]{:S(2)}) %collective-permute-start) | collective-permute-done | bytes 34 | tf_op jit(solution)/shard_map/ppermute | solution.py:33
  28.7 0.0 collective-permute-done.1
  29.4 0.0 copy-start
  29.4 1.6 %copy-done = bf16[1,512,2048]{2,1,0:T(8,128)(2,1)S(1)} copy-done((bf16[1,512,2048]{2,1,0:T(8,128)(2,1)S(1)}, bf16[1,512,2048]{2,1,0:T(8,128)(2,1)}, u32[]{:S(2)}) %copy-start) | copy-done | bytes 2097176
  30.9 0.0 copy-start.2
  31.0 0.7 copy-done.2
  31.6 0.7 copy-done.4
  32.3 3.4 %shard_map.68 = (f32[512,512]{1,0:T(8,128)S(1)}, f32[512,512]{1,0:T(8,128)S(1)}, f32[512,512]{1,0:T(8,128)S(1)}, f32[512,2048]{1,0:T(8,128)S(1)}, f32[320,128]{1,0:T(8,128)S(1)}, /*index=5*/f32[160,128]{1,0:T(8,128)S(1)}) custom-call(bf16[512,2048]{1,0:T(8,128)(2,1)S(1)} %bitcast.10, f32[1,512]{1,0:T(1,128)S(1)} %bitcast.20, ...), custom_call_target="tpu_custom_call" | custom-call | flops 2147483648 | bytes 1048576 | tf_op jit(solution)/shard_map/pallas_call | solution.py:200
  35.7 0.0 collective-permute-done.2.r_ref
  35.7 0.0 copy-start.1
  35.8 2.5 %shard_map.69 = (bf16[512,512]{1,0:T(8,128)(2,1)S(1)}, f32[640,128]{1,0:T(8,128)S(1)}, bf16[640,128]{1,0:T(8,128)(2,1)S(1)}) custom-call(bf16[512,2048]{1,0:T(8,128)(2,1)S(1)} %bitcast.11, bf16[512,2048]{1,0:T(8,128)(2,1)S(1)} %collective-permute-done.2.r_ref, f32[512,512]{1,0:T(8,128)S(1)} %get-tuple-element.15.over_ref, s32[3,1,8]{2,1,0:T(1,128)S(1)} %bitcast.16, ...), custom_call_target="tpu_custom_call" | custom-call | flops 1073741824 | bytes 1048576 | tf_op jit(solution)/shard_map/pallas_call | solution.py:200
  38.2 0.1 collective-permute-start.5
  38.3 1.4 %collective-permute-done.5 = bf16[640,128]{1,0:T(8,128)(2,1)S(1)} collective-permute-done((bf16[640,128]{1,0:T(8,128)(2,1)S(1)}, bf16[640,128]{1,0:T(8,128)(2,1)S(1)}, u32[]{:S(2)}, u32[]{:S(2)}) %collective-permute-start.5) | collective-permute-done | bytes 163872 | tf_op jit(solution)/shard_map/ppermute | solution.py:43
  39.8 2.0 %collective-permute-start.6 = (bf16[320,128]{1,0:T(8,128)(2,1)S(1)}, bf16[320,128]{1,0:T(8,128)(2,1)S(1)}, u32[]{:S(2)}, u32[]{:S(2)}) collective-permute-start(bf16[320,128]{1,0:T(8,128)(2,1)S(1)} %get-tuple-element.26), channel_id=1, source_target_pairs={{0,8},{1,17},{2,18},{3,11},{4,12},{5,21},{6,22},{7,15},{8,0},{9,25... | collective-permute-start | bytes 245768 | tf_op jit(solution)/shard_map/ppermute | solution.py:43
  41.8 0.0 copy-done.1
  41.8 0.1 slice_bitcast_fusion
  41.9 0.1 collective-permute-start.3
  42.0 2.3 %collective-permute-done.6 = bf16[320,128]{1,0:T(8,128)(2,1)S(1)} collective-permute-done((bf16[320,128]{1,0:T(8,128)(2,1)S(1)}, bf16[320,128]{1,0:T(8,128)(2,1)S(1)}, u32[]{:S(2)}, u32[]{:S(2)}) %collective-permute-start.6) | collective-permute-done | bytes 81952 | tf_op jit(solution)/shard_map/ppermute | solution.py:43
  44.4 2.0 %collective-permute-start.7 = (bf16[160,128]{1,0:T(8,128)(2,1)S(1)}, bf16[160,128]{1,0:T(8,128)(2,1)S(1)}, u32[]{:S(2)}, u32[]{:S(2)}) collective-permute-start(bf16[160,128]{1,0:T(8,128)(2,1)S(1)} %get-tuple-element.24), channel_id=1, source_target_pairs={{0,16},{1,9},{2,10},{3,19},{4,20},{5,13},{6,14},{7,23},{8,24},{9,1... | collective-permute-start | bytes 122888 | tf_op jit(solution)/shard_map/ppermute | solution.py:43
  46.4 0.1 slice_bitcast_fusion.1
  46.4 0.1 collective-permute-start.4
  46.5 1.9 %collective-permute-done.7 = bf16[160,128]{1,0:T(8,128)(2,1)S(1)} collective-permute-done((bf16[160,128]{1,0:T(8,128)(2,1)S(1)}, bf16[160,128]{1,0:T(8,128)(2,1)S(1)}, u32[]{:S(2)}, u32[]{:S(2)}) %collective-permute-start.7) | collective-permute-done | bytes 40992 | tf_op jit(solution)/shard_map/ppermute | solution.py:43
  48.5 0.1 collective-permute-start.10
  48.5 3.1 %collective-permute-start.9 = (bf16[160,128]{1,0:T(8,128)(2,1)S(1)}, bf16[160,128]{1,0:T(8,128)(2,1)S(1)}, u32[]{:S(2)}, u32[]{:S(2)}) collective-permute-start(bf16[160,128]{1,0:T(8,128)(2,1)S(1)} %fusion), channel_id=1, source_target_pairs={{0,4},{1,5},{2,6},{3,7},{4,0},{5,1},{6,2},{7,3},{8,12},{9,13},{10,... | collective-permute-start | bytes 122888 | tf_op jit(solution)/shard_map/ppermute | solution.py:43
  51.6 1.1 %collective-permute-start.8 = (bf16[160,128]{1,0:T(8,128)(2,1)S(1)}, bf16[160,128]{1,0:T(8,128)(2,1)S(1)}, u32[]{:S(2)}, u32[]{:S(2)}) collective-permute-start(bf16[160,128]{1,0:T(8,128)(2,1)S(1)} %fusion), channel_id=1, source_target_pairs={{0,7},{1,6},{2,5},{3,4},{4,3},{5,2},{6,1},{7,0},{8,15},{9,14},{10,... | collective-permute-start | bytes 122888 | tf_op jit(solution)/shard_map/ppermute | solution.py:43
  52.7 16.4 %collective-permute-done.10 = bf16[160,128]{1,0:T(8,128)(2,1)S(1)} collective-permute-done((bf16[160,128]{1,0:T(8,128)(2,1)S(1)}, bf16[160,128]{1,0:T(8,128)(2,1)S(1)}, u32[]{:S(2)}, u32[]{:S(2)}) %collective-permute-start.10) | collective-permute-done | bytes 40992 | tf_op jit(solution)/shard_map/ppermute | solution.py:43
  69.1 0.0 collective-permute-done.9
  69.1 2.5 %collective-permute-done.8 = bf16[160,128]{1,0:T(8,128)(2,1)S(1)} collective-permute-done((bf16[160,128]{1,0:T(8,128)(2,1)S(1)}, bf16[160,128]{1,0:T(8,128)(2,1)S(1)}, u32[]{:S(2)}, u32[]{:S(2)}) %collective-permute-start.8) | collective-permute-done | bytes 40992 | tf_op jit(solution)/shard_map/ppermute | solution.py:43
  71.6 0.6 collective-permute-start.11
  72.2 3.5 %collective-permute-done.11 = bf16[160,128]{1,0:T(8,128)(2,1)S(1)} collective-permute-done((bf16[160,128]{1,0:T(8,128)(2,1)S(1)}, bf16[160,128]{1,0:T(8,128)(2,1)S(1)}, u32[]{:S(2)}, u32[]{:S(2)}) %collective-permute-start.11) | collective-permute-done | bytes 40992 | tf_op jit(solution)/shard_map/ppermute | solution.py:43
  75.7 1.6 %collective-permute-start.12 = (bf16[320,128]{1,0:T(8,128)(2,1)S(1)}, bf16[320,128]{1,0:T(8,128)(2,1)S(1)}, u32[]{:S(2)}, u32[]{:S(2)}) collective-permute-start(bf16[320,128]{1,0:T(8,128)(2,1)S(1)} %pad_maximum_fusion.1), channel_id=1, source_target_pairs={{0,8},{1,17},{2,18},{3,11},{4,12},{5,21},{6,22},{7,15},{8,0},{9,25... | collective-permute-start | bytes 245768 | tf_op jit(solution)/shard_map/ppermute | solution.py:43
  77.3 0.0 collective-permute-done.4.last_ref
  77.3 0.0 collective-permute-done.3.r_ref.first_ref
  77.3 0.8 shard_map.72
  78.1 2.1 %collective-permute-done.12 = bf16[320,128]{1,0:T(8,128)(2,1)S(1)} collective-permute-done((bf16[320,128]{1,0:T(8,128)(2,1)S(1)}, bf16[320,128]{1,0:T(8,128)(2,1)S(1)}, u32[]{:S(2)}, u32[]{:S(2)}) %collective-permute-start.12) | collective-permute-done | bytes 81952 | tf_op jit(solution)/shard_map/ppermute | solution.py:43
  80.3 0.1 collective-permute-start.13
  80.4 0.0 copy-done.3
  80.4 0.0 copy-start.5
  80.4 1.8 %shard_map.70.gamma_in = f32[512,2048]{1,0:T(8,128)S(1)} custom-call(s32[3,1,8]{2,1,0:T(1,128)S(1)} %bitcast.17, s32[1,8]{1,0:T(1,128)S(1)} %copy-done.4, f32[512,2048]{1,0:T(8,128)S(1)} %get-tuple-element.14.gamma_in, bf16[512,512]{1,0:T(8,128)(2,1)S(1)} %get-tuple-element.17.mt_ref, bf16[512,2048]{1,0:T(8,128)(2,1)S(1)} %collective-permute-done.2.r_ref), custom_call_target="tpu_custom_call" | custom-call | flops 1073741824 | bytes 1048576 | tf_op jit(solution)/shard_map/pallas_call | solution.py:200
  82.2 0.0 copy-done.5
  82.3 2.0 %shard_map.71.gamma_in = f32[512,2048]{1,0:T(8,128)S(1)} custom-call(s32[3,1,8]{2,1,0:T(1,128)S(1)} %bitcast.18, s32[1,8]{1,0:T(1,128)S(1)} %copy-done.5, bf16[512,2048]{1,0:T(8,128)(2,1)S(1)} %bitcast.13, f32[512,512]{1,0:T(8,128)S(1)} %get-tuple-element.13.over_ref, f32[512,2048]{1,0:T(8,128)S(1)} %shard_map.70.gamma_in, ...), custom_call_target="tpu_custom_call" | custom-call | flops 1073741824 | bytes 1048576 | tf_op jit(solution)/shard_map/pallas_call | solution.py:200
  84.3 2.2 %shard_map.73 = bf16[512,2048]{1,0:T(8,128)(2,1)} custom-call(s32[3,1,8]{2,1,0:T(1,128)S(1)} %bitcast.19, s32[1,8]{1,0:T(1,128)S(1)} %copy-done.5, f32[512,2048]{1,0:T(8,128)S(1)} %shard_map.71.gamma_in, bf16[512,256]{1,0:T(8,128)(2,1)S(1)} %get-tuple-element.18.mt_ref, bf16[256,2048]{1,0:T(8,128)(2,1)S(1)} %get-tuple-element.19.r_ref), custom_call_target="tpu_custom_call" | custom-call | flops 536870912 | bytes 1048576 | tf_op jit(solution)/shard_map/pallas_call | solution.py:200
  86.5 0.0 collective-permute-done.13.other_ref
  86.5 2.1 %shard_map.74 = bf16[512,2048]{1,0:T(8,128)(2,1)} custom-call(bf16[640,128]{1,0:T(8,128)(2,1)S(1)} %pad_maximum_fusion.mine_ref, bf16[640,128]{1,0:T(8,128)(2,1)S(1)} %collective-permute-done.13.other_ref, bf16[512,2048]{1,0:T(8,128)(2,1)S(1)} %bitcast.14), custom_call_target="tpu_custom_call" | custom-call | flops 1073741824 | bytes 1048576 | tf_op jit(solution)/shard_map/pallas_call | solution.py:200
  (12 shorter events, 0.3 us)
Async XLA Ops:
  0.6 35.1 %collective-permute-start.2 = (bf16[512,2048]{1,0:T(8,128)(2,1)}, bf16[512,2048]{1,0:T(8,128)(2,1)S(1)}, u32[]{:S(2)}, u32[]{:S(2)}) collective-permute-start(bf16[512,2048]{1,0:T(8,128)(2,1)} %bitcast.9), channel_id=1, source_target_pairs={{0,1},{1,3},{2,0},{3,2},{4,5},{5,7},{6,4},{7,6},{8,9},{9,11},{10,8... | collective-permute-start | bytes 6291464 | tf_op jit(solution)/shard_map/ppermute | solution.py:33
  1.2 26.9 %collective-permute-start = (bf16[1]{0:T(256)(128)(2,1)}, bf16[1]{0:T(256)(128)(2,1)}, u32[]{:S(2)}, u32[]{:S(2)}) collective-permute-start(bf16[1]{0:T(256)(128)(2,1)} %param.6), channel_id=1, source_target_pairs={{0,1},{1,3},{2,0},{3,2},{4,5},{5,7},{6,4},{7,6},{8,9},{9,11},{10,8... | collective-permute-start | bytes 14 | tf_op jit(solution)/shard_map/ppermute | solution.py:33
  3.3 25.4 %collective-permute-start.1 = (bf16[1]{0:T(256)(128)(2,1)}, bf16[1]{0:T(256)(128)(2,1)}, u32[]{:S(2)}, u32[]{:S(2)}) collective-permute-start(bf16[1]{0:T(256)(128)(2,1)} %param.6), channel_id=1, source_target_pairs={{1,0},{3,1},{0,2},{2,3},{5,4},{7,5},{4,6},{6,7},{9,8},{11,9},{8,10... | collective-permute-start | bytes 14 | tf_op jit(solution)/shard_map/ppermute | solution.py:33
  29.4 1.6 %copy-start = (bf16[1,512,2048]{2,1,0:T(8,128)(2,1)S(1)}, bf16[1,512,2048]{2,1,0:T(8,128)(2,1)}, u32[]{:S(2)}) copy-start(bf16[1,512,2048]{2,1,0:T(8,128)(2,1)} %param.5) | copy-start | bytes 6291460
  30.9 0.7 copy-start.2
  31.6 0.7 copy-start.4
  35.7 6.0 %copy-start.1 = (bf16[1,512,2048]{2,1,0:T(8,128)(2,1)S(1)}, bf16[1,512,2048]{2,1,0:T(8,128)(2,1)}, u32[]{:S(2)}) copy-start(bf16[1,512,2048]{2,1,0:T(8,128)(2,1)} %param.5) | copy-start | bytes 6291460
  38.2 1.5 %collective-permute-start.5 = (bf16[640,128]{1,0:T(8,128)(2,1)S(1)}, bf16[640,128]{1,0:T(8,128)(2,1)S(1)}, u32[]{:S(2)}, u32[]{:S(2)}) collective-permute-start(bf16[640,128]{1,0:T(8,128)(2,1)S(1)} %get-tuple-element.23), channel_id=1, source_target_pairs={{0,1},{1,0},{2,3},{3,2},{4,5},{5,4},{6,7},{7,6},{8,9},{9,8},{10,11... | collective-permute-start | bytes 491528 | tf_op jit(solution)/shard_map/ppermute | solution.py:43
  39.8 4.5 %collective-permute-start.6 = (bf16[320,128]{1,0:T(8,128)(2,1)S(1)}, bf16[320,128]{1,0:T(8,128)(2,1)S(1)}, u32[]{:S(2)}, u32[]{:S(2)}) collective-permute-start(bf16[320,128]{1,0:T(8,128)(2,1)S(1)} %get-tuple-element.26), channel_id=1, source_target_pairs={{0,8},{1,17},{2,18},{3,11},{4,12},{5,21},{6,22},{7,15},{8,0},{9,25... | collective-permute-start | bytes 245768 | tf_op jit(solution)/shard_map/ppermute | solution.py:43
  41.9 35.4 %collective-permute-start.3 = (bf16[320,2048]{1,0:T(8,128)(2,1)S(1)}, bf16[320,2048]{1,0:T(8,128)(2,1)S(1)}, u32[]{:S(2)}, u32[]{:S(2)}) collective-permute-start(bf16[320,2048]{1,0:T(8,128)(2,1)S(1)} %slice_bitcast_fusion), channel_id=1, source_target_pairs={{1,0},{3,1},{0,2},{2,3},{5,4},{7,5},{4,6},{6,7},{9,8},{11,9},{8,10... | collective-permute-start | bytes 3932168 | tf_op jit(solution)/shard_map/ppermute | solution.py:33
  44.4 4.1 %collective-permute-start.7 = (bf16[160,128]{1,0:T(8,128)(2,1)S(1)}, bf16[160,128]{1,0:T(8,128)(2,1)S(1)}, u32[]{:S(2)}, u32[]{:S(2)}) collective-permute-start(bf16[160,128]{1,0:T(8,128)(2,1)S(1)} %get-tuple-element.24), channel_id=1, source_target_pairs={{0,16},{1,9},{2,10},{3,19},{4,20},{5,13},{6,14},{7,23},{8,24},{9,1... | collective-permute-start | bytes 122888 | tf_op jit(solution)/shard_map/ppermute | solution.py:43
  46.4 30.9 %collective-permute-start.4 = (bf16[192,2048]{1,0:T(8,128)(2,1)S(1)}, bf16[192,2048]{1,0:T(8,128)(2,1)S(1)}, u32[]{:S(2)}, u32[]{:S(2)}) collective-permute-start(bf16[192,2048]{1,0:T(8,128)(2,1)S(1)} %slice_bitcast_fusion.1), channel_id=1, source_target_pairs={{1,0},{3,1},{0,2},{2,3},{5,4},{7,5},{4,6},{6,7},{9,8},{11,9},{8,10... | collective-permute-start | bytes 2359304 | tf_op jit(solution)/shard_map/ppermute | solution.py:33
  48.5 20.7 %collective-permute-start.10 = (bf16[160,128]{1,0:T(8,128)(2,1)S(1)}, bf16[160,128]{1,0:T(8,128)(2,1)S(1)}, u32[]{:S(2)}, u32[]{:S(2)}) collective-permute-start(bf16[160,128]{1,0:T(8,128)(2,1)S(1)} %fusion), channel_id=1, source_target_pairs={{0,3},{1,2},{2,1},{3,0},{4,7},{5,6},{6,5},{7,4},{8,11},{9,10},{10,... | collective-permute-start | bytes 122888 | tf_op jit(solution)/shard_map/ppermute | solution.py:43
  48.5 20.6 %collective-permute-start.9 = (bf16[160,128]{1,0:T(8,128)(2,1)S(1)}, bf16[160,128]{1,0:T(8,128)(2,1)S(1)}, u32[]{:S(2)}, u32[]{:S(2)}) collective-permute-start(bf16[160,128]{1,0:T(8,128)(2,1)S(1)} %fusion), channel_id=1, source_target_pairs={{0,4},{1,5},{2,6},{3,7},{4,0},{5,1},{6,2},{7,3},{8,12},{9,13},{10,... | collective-permute-start | bytes 122888 | tf_op jit(solution)/shard_map/ppermute | solution.py:43
  51.6 20.0 %collective-permute-start.8 = (bf16[160,128]{1,0:T(8,128)(2,1)S(1)}, bf16[160,128]{1,0:T(8,128)(2,1)S(1)}, u32[]{:S(2)}, u32[]{:S(2)}) collective-permute-start(bf16[160,128]{1,0:T(8,128)(2,1)S(1)} %fusion), channel_id=1, source_target_pairs={{0,7},{1,6},{2,5},{3,4},{4,3},{5,2},{6,1},{7,0},{8,15},{9,14},{10,... | collective-permute-start | bytes 122888 | tf_op jit(solution)/shard_map/ppermute | solution.py:43
  71.6 4.1 %collective-permute-start.11 = (bf16[160,128]{1,0:T(8,128)(2,1)S(1)}, bf16[160,128]{1,0:T(8,128)(2,1)S(1)}, u32[]{:S(2)}, u32[]{:S(2)}) collective-permute-start(bf16[160,128]{1,0:T(8,128)(2,1)S(1)} %multiply_convert_fusion), channel_id=1, source_target_pairs={{0,16},{1,9},{2,10},{3,19},{4,20},{5,13},{6,14},{7,23},{8,24},{9,1... | collective-permute-start | bytes 122888 | tf_op jit(solution)/shard_map/ppermute | solution.py:43
  75.7 4.5 %collective-permute-start.12 = (bf16[320,128]{1,0:T(8,128)(2,1)S(1)}, bf16[320,128]{1,0:T(8,128)(2,1)S(1)}, u32[]{:S(2)}, u32[]{:S(2)}) collective-permute-start(bf16[320,128]{1,0:T(8,128)(2,1)S(1)} %pad_maximum_fusion.1), channel_id=1, source_target_pairs={{0,8},{1,17},{2,18},{3,11},{4,12},{5,21},{6,22},{7,15},{8,0},{9,25... | collective-permute-start | bytes 245768 | tf_op jit(solution)/shard_map/ppermute | solution.py:43
  77.3 3.1 %copy-start.3 = (s32[1,8,3]{1,0,2:T(1,128)S(1)}, s32[1,8,3]{1,0,2:T(1,128)}, u32[]{:S(2)}) copy-start(s32[1,8,3]{1,0,2:T(1,128)} %param.8) | copy-start | bytes 292
  80.3 6.2 %collective-permute-start.13 = (bf16[640,128]{1,0:T(8,128)(2,1)S(1)}, bf16[640,128]{1,0:T(8,128)(2,1)S(1)}, u32[]{:S(2)}, u32[]{:S(2)}) collective-permute-start(bf16[640,128]{1,0:T(8,128)(2,1)S(1)} %pad_maximum_fusion.mine_ref), channel_id=1, source_target_pairs={{0,1},{1,0},{2,3},{3,2},{4,5},{5,4},{6,7},{7,6},{8,9},{9,8},{10,11... | collective-permute-start | bytes 491528 | tf_op jit(solution)/shard_map/ppermute | solution.py:43
  80.4 1.8 %copy-start.5 = (s32[1,8]{1,0:T(1,128)S(1)}, s32[1,8]{1,0:T(1,128)}, u32[]{:S(2)}) copy-start(s32[1,8]{1,0:T(1,128)} %counts.9) | copy-start | bytes 100

commit v9 on v8

--- a/solution.py
+++ b/solution.py
@@ -175,11 +175,20 @@
     mt_ref[...] = flat_amp(slice(vir - rows, vir), b_ref, r_ref, over_ref, m_ref)
 
 
-def last_gamma_kernel(codes, counts, gamma_in, mt_ref, r_ref, out_ref, held, sems):
+def half_gamma_kernel(start, codes, counts, gamma_in, mt_ref, r_ref, *refs):
+    out_ref, held, sems = refs[-3:]
     own, far = weights(codes, counts, 3 - first_round(lax.axis_index("mem")))
-    strips_out(
-        out_ref, held, sems, STRIPS, lambda at: gamma_in[:, at] + (own + far) * nn(mt_ref[...], r_ref[:, at])
-    )
+    strips = sems.shape[0]
+    width = held.shape[1] // strips
+    copies = []
+    for p in range(strips):
+        here, at = pl.ds(p * width, width), pl.ds(start + p * width, width)
+        total = gamma_in[:, at] + (own + far) * nn(mt_ref[...], r_ref[:, at])
+        held[:, here] = total.astype(held.dtype)
+        copies.append(pltpu.make_async_copy(held.at[:, here], out_ref.at[:, at], sems.at[p]))
+        copies[-1].start()
+    for copy in copies:
+        copy.wait()
 
 
 def apply_kernel(mine_ref, other_ref, b_ref, out_ref, tile, held, sems):
@@ -274,7 +283,7 @@
     other = swap(mine, [(0, 1), (0, 1)])
 
     unit = vir // 16
-    cuts = (0, 10 * unit, vir)
+    cuts = (0, 11 * unit, vir)
     parts = [block[a:b] for a, b in zip(cuts, cuts[1:])]
     second = [turn(part, True) for part in parts]
     gamma = call(first_gamma_kernel, wide, (), (0, 1), 5, dot)(
@@ -287,9 +296,21 @@
     rest, rows = call(
         amp_kernel, (shape((vir, vir // 2), BF16), shape((vir // 2, aux), BF16)), bounce[1:], (), 4, dot // 2
     )(block, over_second, *second)
-    result = call(last_gamma_kernel, shape((vir, aux), BF16), out_scratch, (0, 1), 5, dot // 2, any_space)(
-        pair_code, pair_count, gamma, rest, rows
-    )
+    result = ()
+    for part in range(2):
+        result = (
+            pl.pallas_call(
+                functools.partial(half_gamma_kernel, part * (aux // 2)),
+                out_shape=shape((vir, aux), BF16),
+                in_specs=[SMEM, SMEM, VMEM, VMEM, VMEM] + [any_space] * part,
+                out_specs=any_space,
+                scratch_shapes=[pltpu.VMEM((vir, aux // 2), BF16), pltpu.SemaphoreType.DMA((2,))],
+                input_output_aliases={5: 0} if part else {},
+                compiler_params=pltpu.CompilerParams(vmem_limit_bytes=12 << 20),
+                cost_estimate=pl.CostEstimate(flops=dot // 4, bytes_accessed=1 << 20, transcendentals=0),
+            )(pair_code, pair_count, gamma, rest, rows, *result),
+        )
+    result = result[0]
     lagrangian = call(
         apply_kernel, shape((vir, aux), BF16), [pltpu.VMEM((vir, vir), BF16), *out_scratch], (), 3, dot,
         any_space,

time: 88.9 us -> 83.5 us (0.939)
  waiting for transfers between devices: 52.9 us -> 46 us
  Pallas kernels: 14.9 us -> 16.4 us
    ppermute x9, waiting for transfers between devices: 30.1 us -> 23.1 us  [swap(): return lax.ppermute(value, ('grp', 'mem'), pairs)]
    pallas_call x0 -> x2, Pallas kernels: none -> 3.7 us  [body(): pl.pallas_call(functools.partial(half_gamma_kernel, part * (aux // 2)), o...]
    pallas_call x7 -> x6, Pallas kernels: 14.9 us -> 12.7 us  [call(): kernel_call(kernel, outs, scratch, smem, count, flops, out_spec)(*args)]
  transfers between devices with their start and end apart: 14 -> 14, of which waited for: 8 -> 8; matrix products, arithmetic and copies ran while one was open for 1% -> 1% of each run, Pallas kernels for 12% -> 14%
where the time goes in v9:
time: 83.5 us; the launch traced here: 83.2 us
  waiting for transfers between devices  46 us (55%)
  Pallas kernels  16.4 us (20%)
  starting transfers between devices  14 us (17%)
  local copies, waits for them, and re-layouts  3.13 us (4%)
  between operations  2.81 us (3%)
  other arithmetic  0.97 us (1%)
    ppermute x9, waiting for transfers between devices, swap(): return lax.ppermute(value, ('grp', 'mem'), pairs)  23.1 us
    ppermute x5, waiting for transfers between devices, turn(): return lax.ppermute(value, 'mem', pairs)  22.8 us
    pallas_call x6, Pallas kernels, call(): kernel_call(kernel, outs, scratch, smem, count, flops, out_spec)(*args)  12.7 us
    ppermute x9, starting transfers between devices, swap(): return lax.ppermute(value, ('grp', 'mem'), pairs)  10.6 us
    pallas_call x2, Pallas kernels, body(): pl.pallas_call(functools.partial(half_gamma_kernel, part * (aux // 2)), o...  3.7 us
    ppermute x5, starting transfers between devices, turn(): return lax.ppermute(value, 'mem', pairs)  3.4 us
    unnamed x12, local copies, waits for them, and re-layouts  2.94 us
  transfers between devices with their start and end apart: 14, of which 8 were waited for; matrix products, arithmetic and copies ran while one was open for 1% of the time, Pallas kernels for 14%

profile of v9, /device:TPU:0, one launch (start us, length us, event | category | flops | bytes accessed | tf_op | source)
XLA Modules:
  0.0 83.2 jit_solution(1330009086700105619)
XLA Ops:
  0.6 0.6 collective-permute-start.2
  1.2 2.1 %collective-permute-start = (bf16[1]{0:T(256)(128)(2,1)}, bf16[1]{0:T(256)(128)(2,1)}, u32[]{:S(2)}, u32[]{:S(2)}) collective-permute-start(bf16[1]{0:T(256)(128)(2,1)} %param.6), channel_id=1, source_target_pairs={{0,1},{1,3},{2,0},{3,2},{4,5},{5,7},{6,4},{7,6},{8,9},{9,11},{10,8... | collective-permute-start | bytes 14 | tf_op jit(solution)/shard_map/ppermute | solution.py:33
  3.3 0.6 collective-permute-start.1
  4.6 0.7 reshape.13
  5.3 22.8 %collective-permute-done = bf16[1]{0:T(256)(128)(2,1)} collective-permute-done((bf16[1]{0:T(256)(128)(2,1)}, bf16[1]{0:T(256)(128)(2,1)}, u32[]{:S(2)}, u32[]{:S(2)}) %collective-permute-start) | collective-permute-done | bytes 34 | tf_op jit(solution)/shard_map/ppermute | solution.py:33
  28.7 0.0 collective-permute-done.1
  29.4 0.0 copy-start
  29.4 1.6 %copy-done = bf16[1,512,2048]{2,1,0:T(8,128)(2,1)S(1)} copy-done((bf16[1,512,2048]{2,1,0:T(8,128)(2,1)S(1)}, bf16[1,512,2048]{2,1,0:T(8,128)(2,1)}, u32[]{:S(2)}) %copy-start) | copy-done | bytes 2097176
  30.9 0.0 copy-start.2
  31.0 0.7 copy-done.2
  31.6 0.7 copy-done.4
  32.3 3.4 %shard_map.68 = (f32[512,512]{1,0:T(8,128)S(1)}, f32[512,512]{1,0:T(8,128)S(1)}, f32[512,512]{1,0:T(8,128)S(1)}, f32[512,2048]{1,0:T(8,128)S(1)}, f32[320,128]{1,0:T(8,128)S(1)}, /*index=5*/f32[160,128]{1,0:T(8,128)S(1)}) custom-call(bf16[512,2048]{1,0:T(8,128)(2,1)S(1)} %bitcast.10, f32[1,512]{1,0:T(1,128)S(1)} %bitcast.21, ...), custom_call_target="tpu_custom_call" | custom-call | flops 2147483648 | bytes 1048576 | tf_op jit(solution)/shard_map/pallas_call | solution.py:209
  35.7 0.0 collective-permute-done.2.r_ref
  35.7 0.0 copy-done.3
  35.7 0.0 copy-start.1
  35.8 2.5 %shard_map.69 = (bf16[512,512]{1,0:T(8,128)(2,1)S(1)}, f32[640,128]{1,0:T(8,128)S(1)}, bf16[640,128]{1,0:T(8,128)(2,1)S(1)}) custom-call(bf16[512,2048]{1,0:T(8,128)(2,1)S(1)} %bitcast.11, bf16[512,2048]{1,0:T(8,128)(2,1)S(1)} %collective-permute-done.2.r_ref, f32[512,512]{1,0:T(8,128)S(1)} %get-tuple-element.15.over_ref, s32[3,1,8]{2,1,0:T(1,128)S(1)} %bitcast.16, ...), custom_call_target="tpu_custom_call" | custom-call | flops 1073741824 | bytes 1048576 | tf_op jit(solution)/shard_map/pallas_call | solution.py:209
  38.2 0.1 collective-permute-start.5
  38.3 1.4 %collective-permute-done.5 = bf16[640,128]{1,0:T(8,128)(2,1)S(1)} collective-permute-done((bf16[640,128]{1,0:T(8,128)(2,1)S(1)}, bf16[640,128]{1,0:T(8,128)(2,1)S(1)}, u32[]{:S(2)}, u32[]{:S(2)}) %collective-permute-start.5) | collective-permute-done | bytes 163872 | tf_op jit(solution)/shard_map/ppermute | solution.py:43
  39.8 2.0 %collective-permute-start.6 = (bf16[320,128]{1,0:T(8,128)(2,1)S(1)}, bf16[320,128]{1,0:T(8,128)(2,1)S(1)}, u32[]{:S(2)}, u32[]{:S(2)}) collective-permute-start(bf16[320,128]{1,0:T(8,128)(2,1)S(1)} %get-tuple-element.26), channel_id=1, source_target_pairs={{0,8},{1,17},{2,18},{3,11},{4,12},{5,21},{6,22},{7,15},{8,0},{9,25... | collective-permute-start | bytes 245768 | tf_op jit(solution)/shard_map/ppermute | solution.py:43
  41.8 0.0 copy-done.1
  41.8 0.1 slice_bitcast_fusion
  41.9 0.1 collective-permute-start.3
  42.0 2.3 %collective-permute-done.6 = bf16[320,128]{1,0:T(8,128)(2,1)S(1)} collective-permute-done((bf16[320,128]{1,0:T(8,128)(2,1)S(1)}, bf16[320,128]{1,0:T(8,128)(2,1)S(1)}, u32[]{:S(2)}, u32[]{:S(2)}) %collective-permute-start.6) | collective-permute-done | bytes 81952 | tf_op jit(solution)/shard_map/ppermute | solution.py:43
  44.4 2.0 %collective-permute-start.7 = (bf16[160,128]{1,0:T(8,128)(2,1)S(1)}, bf16[160,128]{1,0:T(8,128)(2,1)S(1)}, u32[]{:S(2)}, u32[]{:S(2)}) collective-permute-start(bf16[160,128]{1,0:T(8,128)(2,1)S(1)} %get-tuple-element.24), channel_id=1, source_target_pairs={{0,16},{1,9},{2,10},{3,19},{4,20},{5,13},{6,14},{7,23},{8,24},{9,1... | collective-permute-start | bytes 122888 | tf_op jit(solution)/shard_map/ppermute | solution.py:43
  46.4 2.0 %collective-permute-done.7 = bf16[160,128]{1,0:T(8,128)(2,1)S(1)} collective-permute-done((bf16[160,128]{1,0:T(8,128)(2,1)S(1)}, bf16[160,128]{1,0:T(8,128)(2,1)S(1)}, u32[]{:S(2)}, u32[]{:S(2)}) %collective-permute-start.7) | collective-permute-done | bytes 40992 | tf_op jit(solution)/shard_map/ppermute | solution.py:43
  48.4 0.1 collective-permute-start.10
  48.5 3.1 %collective-permute-start.9 = (bf16[160,128]{1,0:T(8,128)(2,1)S(1)}, bf16[160,128]{1,0:T(8,128)(2,1)S(1)}, u32[]{:S(2)}, u32[]{:S(2)}) collective-permute-start(bf16[160,128]{1,0:T(8,128)(2,1)S(1)} %fusion), channel_id=1, source_target_pairs={{0,4},{1,5},{2,6},{3,7},{4,0},{5,1},{6,2},{7,3},{8,12},{9,13},{10,... | collective-permute-start | bytes 122888 | tf_op jit(solution)/shard_map/ppermute | solution.py:43
  51.6 1.1 %collective-permute-start.8 = (bf16[160,128]{1,0:T(8,128)(2,1)S(1)}, bf16[160,128]{1,0:T(8,128)(2,1)S(1)}, u32[]{:S(2)}, u32[]{:S(2)}) collective-permute-start(bf16[160,128]{1,0:T(8,128)(2,1)S(1)} %fusion), channel_id=1, source_target_pairs={{0,7},{1,6},{2,5},{3,4},{4,3},{5,2},{6,1},{7,0},{8,15},{9,14},{10,... | collective-permute-start | bytes 122888 | tf_op jit(solution)/shard_map/ppermute | solution.py:43
  52.8 0.1 collective-permute-start.4
  52.9 9.3 %collective-permute-done.10 = bf16[160,128]{1,0:T(8,128)(2,1)S(1)} collective-permute-done((bf16[160,128]{1,0:T(8,128)(2,1)S(1)}, bf16[160,128]{1,0:T(8,128)(2,1)S(1)}, u32[]{:S(2)}, u32[]{:S(2)}) %collective-permute-start.10) | collective-permute-done | bytes 40992 | tf_op jit(solution)/shard_map/ppermute | solution.py:43
  62.1 0.0 collective-permute-done.9
  62.1 2.6 %collective-permute-done.8 = bf16[160,128]{1,0:T(8,128)(2,1)S(1)} collective-permute-done((bf16[160,128]{1,0:T(8,128)(2,1)S(1)}, bf16[160,128]{1,0:T(8,128)(2,1)S(1)}, u32[]{:S(2)}, u32[]{:S(2)}) %collective-permute-start.8) | collective-permute-done | bytes 40992 | tf_op jit(solution)/shard_map/ppermute | solution.py:43
  64.7 0.6 collective-permute-start.11
  65.3 3.5 %collective-permute-done.11 = bf16[160,128]{1,0:T(8,128)(2,1)S(1)} collective-permute-done((bf16[160,128]{1,0:T(8,128)(2,1)S(1)}, bf16[160,128]{1,0:T(8,128)(2,1)S(1)}, u32[]{:S(2)}, u32[]{:S(2)}) %collective-permute-start.11) | collective-permute-done | bytes 40992 | tf_op jit(solution)/shard_map/ppermute | solution.py:43
  68.8 1.6 %collective-permute-start.12 = (bf16[320,128]{1,0:T(8,128)(2,1)S(1)}, bf16[320,128]{1,0:T(8,128)(2,1)S(1)}, u32[]{:S(2)}, u32[]{:S(2)}) collective-permute-start(bf16[320,128]{1,0:T(8,128)(2,1)S(1)} %pad_maximum_fusion.1), channel_id=1, source_target_pairs={{0,8},{1,17},{2,18},{3,11},{4,12},{5,21},{6,22},{7,15},{8,0},{9,25... | collective-permute-start | bytes 245768 | tf_op jit(solution)/shard_map/ppermute | solution.py:43
  70.4 0.0 collective-permute-done.4.last_ref
  70.4 0.0 collective-permute-done.3.r_ref.first_ref
  70.4 0.8 shard_map.72
  71.2 2.1 %collective-permute-done.12 = bf16[320,128]{1,0:T(8,128)(2,1)S(1)} collective-permute-done((bf16[320,128]{1,0:T(8,128)(2,1)S(1)}, bf16[320,128]{1,0:T(8,128)(2,1)S(1)}, u32[]{:S(2)}, u32[]{:S(2)}) %collective-permute-start.12) | collective-permute-done | bytes 81952 | tf_op jit(solution)/shard_map/ppermute | solution.py:43
  73.4 0.1 collective-permute-start.13
  73.5 0.0 copy-start.5
  73.5 1.8 %shard_map.70.gamma_in = f32[512,2048]{1,0:T(8,128)S(1)} custom-call(s32[3,1,8]{2,1,0:T(1,128)S(1)} %bitcast.17, s32[1,8]{1,0:T(1,128)S(1)} %copy-done.4, f32[512,2048]{1,0:T(8,128)S(1)} %get-tuple-element.14.gamma_in, bf16[512,512]{1,0:T(8,128)(2,1)S(1)} %get-tuple-element.17.mt_ref, bf16[512,2048]{1,0:T(8,128)(2,1)S(1)} %collective-permute-done.2.r_ref), custom_call_target="tpu_custom_call" | custom-call | flops 1073741824 | bytes 1048576 | tf_op jit(solution)/shard_map/pallas_call | solution.py:209
  75.3 0.0 copy-done.5
  75.3 2.0 %shard_map.71.gamma_in = f32[512,2048]{1,0:T(8,128)S(1)} custom-call(s32[3,1,8]{2,1,0:T(1,128)S(1)} %bitcast.18, s32[1,8]{1,0:T(1,128)S(1)} %copy-done.5, bf16[512,2048]{1,0:T(8,128)(2,1)S(1)} %bitcast.13, f32[512,512]{1,0:T(8,128)S(1)} %get-tuple-element.13.over_ref, f32[512,2048]{1,0:T(8,128)S(1)} %shard_map.70.gamma_in, ...), custom_call_target="tpu_custom_call" | custom-call | flops 1073741824 | bytes 1048576 | tf_op jit(solution)/shard_map/pallas_call | solution.py:209
  77.4 1.8 %shard_map.73.refs_0_ = bf16[512,2048]{1,0:T(8,128)(2,1)} custom-call(s32[3,1,8]{2,1,0:T(1,128)S(1)} %bitcast.19, s32[1,8]{1,0:T(1,128)S(1)} %copy-done.5, f32[512,2048]{1,0:T(8,128)S(1)} %shard_map.71.gamma_in, bf16[512,256]{1,0:T(8,128)(2,1)S(1)} %get-tuple-element.18.mt_ref, bf16[256,2048]{1,0:T(8,128)(2,1)S(1)} %get-tuple-element.19.r_ref), custom_call_target="tpu_custom_call" | custom-call | flops 268435456 | bytes 1048576 | tf_op jit(solution)/shard_map/pallas_call | solution.py:302
  79.2 1.9 %shard_map.74 = bf16[512,2048]{1,0:T(8,128)(2,1)} custom-call(s32[3,1,8]{2,1,0:T(1,128)S(1)} %bitcast.20, s32[1,8]{1,0:T(1,128)S(1)} %copy-done.5, f32[512,2048]{1,0:T(8,128)S(1)} %shard_map.71.gamma_in, bf16[512,256]{1,0:T(8,128)(2,1)S(1)} %get-tuple-element.18.mt_ref, ...), custom_call_target="tpu_custom_call", output_to_operand_aliasing={{}: (5, {})} | custom-call | flops 268435456 | bytes 1048576 | tf_op jit(solution)/shard_map/pallas_call | solution.py:302
  81.1 0.0 collective-permute-done.13.other_ref
  81.1 2.1 %shard_map.75 = bf16[512,2048]{1,0:T(8,128)(2,1)} custom-call(bf16[640,128]{1,0:T(8,128)(2,1)S(1)} %pad_maximum_fusion.mine_ref, bf16[640,128]{1,0:T(8,128)(2,1)S(1)} %collective-permute-done.13.other_ref, bf16[512,2048]{1,0:T(8,128)(2,1)S(1)} %bitcast.14), custom_call_target="tpu_custom_call" | custom-call | flops 1073741824 | bytes 1048576 | tf_op jit(solution)/shard_map/pallas_call | solution.py:209
  (13 shorter events, 0.3 us)
Async XLA Ops:
  0.6 35.1 %collective-permute-start.2 = (bf16[512,2048]{1,0:T(8,128)(2,1)}, bf16[512,2048]{1,0:T(8,128)(2,1)S(1)}, u32[]{:S(2)}, u32[]{:S(2)}) collective-permute-start(bf16[512,2048]{1,0:T(8,128)(2,1)} %bitcast.9), channel_id=1, source_target_pairs={{0,1},{1,3},{2,0},{3,2},{4,5},{5,7},{6,4},{7,6},{8,9},{9,11},{10,8... | collective-permute-start | bytes 6291464 | tf_op jit(solution)/shard_map/ppermute | solution.py:33
  1.2 26.9 %collective-permute-start = (bf16[1]{0:T(256)(128)(2,1)}, bf16[1]{0:T(256)(128)(2,1)}, u32[]{:S(2)}, u32[]{:S(2)}) collective-permute-start(bf16[1]{0:T(256)(128)(2,1)} %param.6), channel_id=1, source_target_pairs={{0,1},{1,3},{2,0},{3,2},{4,5},{5,7},{6,4},{7,6},{8,9},{9,11},{10,8... | collective-permute-start | bytes 14 | tf_op jit(solution)/shard_map/ppermute | solution.py:33
  3.3 25.4 %collective-permute-start.1 = (bf16[1]{0:T(256)(128)(2,1)}, bf16[1]{0:T(256)(128)(2,1)}, u32[]{:S(2)}, u32[]{:S(2)}) collective-permute-start(bf16[1]{0:T(256)(128)(2,1)} %param.6), channel_id=1, source_target_pairs={{1,0},{3,1},{0,2},{2,3},{5,4},{7,5},{4,6},{6,7},{9,8},{11,9},{8,10... | collective-permute-start | bytes 14 | tf_op jit(solution)/shard_map/ppermute | solution.py:33
  29.4 1.6 %copy-start = (bf16[1,512,2048]{2,1,0:T(8,128)(2,1)S(1)}, bf16[1,512,2048]{2,1,0:T(8,128)(2,1)}, u32[]{:S(2)}) copy-start(bf16[1,512,2048]{2,1,0:T(8,128)(2,1)} %param.5) | copy-start | bytes 6291460
  30.9 0.7 copy-start.2
  31.6 0.7 copy-start.4
  32.3 3.5 %copy-start.3 = (s32[1,8,3]{1,0,2:T(1,128)S(1)}, s32[1,8,3]{1,0,2:T(1,128)}, u32[]{:S(2)}) copy-start(s32[1,8,3]{1,0,2:T(1,128)} %param.8) | copy-start | bytes 292
  35.7 6.0 %copy-start.1 = (bf16[1,512,2048]{2,1,0:T(8,128)(2,1)S(1)}, bf16[1,512,2048]{2,1,0:T(8,128)(2,1)}, u32[]{:S(2)}) copy-start(bf16[1,512,2048]{2,1,0:T(8,128)(2,1)} %param.5) | copy-start | bytes 6291460
  38.2 1.5 %collective-permute-start.5 = (bf16[640,128]{1,0:T(8,128)(2,1)S(1)}, bf16[640,128]{1,0:T(8,128)(2,1)S(1)}, u32[]{:S(2)}, u32[]{:S(2)}) collective-permute-start(bf16[640,128]{1,0:T(8,128)(2,1)S(1)} %get-tuple-element.23), channel_id=1, source_target_pairs={{0,1},{1,0},{2,3},{3,2},{4,5},{5,4},{6,7},{7,6},{8,9},{9,8},{10,11... | collective-permute-start | bytes 491528 | tf_op jit(solution)/shard_map/ppermute | solution.py:43
  39.8 4.5 %collective-permute-start.6 = (bf16[320,128]{1,0:T(8,128)(2,1)S(1)}, bf16[320,128]{1,0:T(8,128)(2,1)S(1)}, u32[]{:S(2)}, u32[]{:S(2)}) collective-permute-start(bf16[320,128]{1,0:T(8,128)(2,1)S(1)} %get-tuple-element.26), channel_id=1, source_target_pairs={{0,8},{1,17},{2,18},{3,11},{4,12},{5,21},{6,22},{7,15},{8,0},{9,25... | collective-permute-start | bytes 245768 | tf_op jit(solution)/shard_map/ppermute | solution.py:43
  41.9 28.5 %collective-permute-start.3 = (bf16[352,2048]{1,0:T(8,128)(2,1)S(1)}, bf16[352,2048]{1,0:T(8,128)(2,1)S(1)}, u32[]{:S(2)}, u32[]{:S(2)}) collective-permute-start(bf16[352,2048]{1,0:T(8,128)(2,1)S(1)} %slice_bitcast_fusion), channel_id=1, source_target_pairs={{1,0},{3,1},{0,2},{2,3},{5,4},{7,5},{4,6},{6,7},{9,8},{11,9},{8,10... | collective-permute-start | bytes 4325384 | tf_op jit(solution)/shard_map/ppermute | solution.py:33
  44.4 4.1 %collective-permute-start.7 = (bf16[160,128]{1,0:T(8,128)(2,1)S(1)}, bf16[160,128]{1,0:T(8,128)(2,1)S(1)}, u32[]{:S(2)}, u32[]{:S(2)}) collective-permute-start(bf16[160,128]{1,0:T(8,128)(2,1)S(1)} %get-tuple-element.24), channel_id=1, source_target_pairs={{0,16},{1,9},{2,10},{3,19},{4,20},{5,13},{6,14},{7,23},{8,24},{9,1... | collective-permute-start | bytes 122888 | tf_op jit(solution)/shard_map/ppermute | solution.py:43
  48.4 13.7 %collective-permute-start.10 = (bf16[160,128]{1,0:T(8,128)(2,1)S(1)}, bf16[160,128]{1,0:T(8,128)(2,1)S(1)}, u32[]{:S(2)}, u32[]{:S(2)}) collective-permute-start(bf16[160,128]{1,0:T(8,128)(2,1)S(1)} %fusion), channel_id=1, source_target_pairs={{0,3},{1,2},{2,1},{3,0},{4,7},{5,6},{6,5},{7,4},{8,11},{9,10},{10,... | collective-permute-start | bytes 122888 | tf_op jit(solution)/shard_map/ppermute | solution.py:43
  48.5 13.6 %collective-permute-start.9 = (bf16[160,128]{1,0:T(8,128)(2,1)S(1)}, bf16[160,128]{1,0:T(8,128)(2,1)S(1)}, u32[]{:S(2)}, u32[]{:S(2)}) collective-permute-start(bf16[160,128]{1,0:T(8,128)(2,1)S(1)} %fusion), channel_id=1, source_target_pairs={{0,4},{1,5},{2,6},{3,7},{4,0},{5,1},{6,2},{7,3},{8,12},{9,13},{10,... | collective-permute-start | bytes 122888 | tf_op jit(solution)/shard_map/ppermute | solution.py:43
  51.6 13.1 %collective-permute-start.8 = (bf16[160,128]{1,0:T(8,128)(2,1)S(1)}, bf16[160,128]{1,0:T(8,128)(2,1)S(1)}, u32[]{:S(2)}, u32[]{:S(2)}) collective-permute-start(bf16[160,128]{1,0:T(8,128)(2,1)S(1)} %fusion), channel_id=1, source_target_pairs={{0,7},{1,6},{2,5},{3,4},{4,3},{5,2},{6,1},{7,0},{8,15},{9,14},{10,... | collective-permute-start | bytes 122888 | tf_op jit(solution)/shard_map/ppermute | solution.py:43
  52.8 17.6 %collective-permute-start.4 = (bf16[160,2048]{1,0:T(8,128)(2,1)S(1)}, bf16[160,2048]{1,0:T(8,128)(2,1)S(1)}, u32[]{:S(2)}, u32[]{:S(2)}) collective-permute-start(bf16[160,2048]{1,0:T(8,128)(2,1)S(1)} %slice_bitcast_fusion.1), channel_id=1, source_target_pairs={{1,0},{3,1},{0,2},{2,3},{5,4},{7,5},{4,6},{6,7},{9,8},{11,9},{8,10... | collective-permute-start | bytes 1966088 | tf_op jit(solution)/shard_map/ppermute | solution.py:33
  64.7 4.1 %collective-permute-start.11 = (bf16[160,128]{1,0:T(8,128)(2,1)S(1)}, bf16[160,128]{1,0:T(8,128)(2,1)S(1)}, u32[]{:S(2)}, u32[]{:S(2)}) collective-permute-start(bf16[160,128]{1,0:T(8,128)(2,1)S(1)} %multiply_convert_fusion), channel_id=1, source_target_pairs={{0,16},{1,9},{2,10},{3,19},{4,20},{5,13},{6,14},{7,23},{8,24},{9,1... | collective-permute-start | bytes 122888 | tf_op jit(solution)/shard_map/ppermute | solution.py:43
  68.8 4.5 %collective-permute-start.12 = (bf16[320,128]{1,0:T(8,128)(2,1)S(1)}, bf16[320,128]{1,0:T(8,128)(2,1)S(1)}, u32[]{:S(2)}, u32[]{:S(2)}) collective-permute-start(bf16[320,128]{1,0:T(8,128)(2,1)S(1)} %pad_maximum_fusion.1), channel_id=1, source_target_pairs={{0,8},{1,17},{2,18},{3,11},{4,12},{5,21},{6,22},{7,15},{8,0},{9,25... | collective-permute-start | bytes 245768 | tf_op jit(solution)/shard_map/ppermute | solution.py:43
  73.4 7.7 %collective-permute-start.13 = (bf16[640,128]{1,0:T(8,128)(2,1)S(1)}, bf16[640,128]{1,0:T(8,128)(2,1)S(1)}, u32[]{:S(2)}, u32[]{:S(2)}) collective-permute-start(bf16[640,128]{1,0:T(8,128)(2,1)S(1)} %pad_maximum_fusion.mine_ref), channel_id=1, source_target_pairs={{0,1},{1,0},{2,3},{3,2},{4,5},{5,4},{6,7},{7,6},{8,9},{9,8},{10,11... | collective-permute-start | bytes 491528 | tf_op jit(solution)/shard_map/ppermute | solution.py:43
  73.5 1.8 %copy-start.5 = (s32[1,8]{1,0:T(1,128)S(1)}, s32[1,8]{1,0:T(1,128)}, u32[]{:S(2)}) copy-start(s32[1,8]{1,0:T(1,128)} %counts.11) | copy-start | bytes 100

commit v10 on v9

--- a/solution.py
+++ b/solution.py
@@ -297,14 +297,15 @@
         amp_kernel, (shape((vir, vir // 2), BF16), shape((vir // 2, aux), BF16)), bounce[1:], (), 4, dot // 2
     )(block, over_second, *second)
     result = ()
-    for part in range(2):
+    quarter = aux // STRIPS
+    for part, strips in enumerate((1, STRIPS - 1)):
         result = (
             pl.pallas_call(
-                functools.partial(half_gamma_kernel, part * (aux // 2)),
+                functools.partial(half_gamma_kernel, part * quarter),
                 out_shape=shape((vir, aux), BF16),
                 in_specs=[SMEM, SMEM, VMEM, VMEM, VMEM] + [any_space] * part,
                 out_specs=any_space,
-                scratch_shapes=[pltpu.VMEM((vir, aux // 2), BF16), pltpu.SemaphoreType.DMA((2,))],
+                scratch_shapes=[pltpu.VMEM((vir, strips * quarter), BF16), pltpu.SemaphoreType.DMA((strips,))],
                 input_output_aliases={5: 0} if part else {},
                 compiler_params=pltpu.CompilerParams(vmem_limit_bytes=12 << 20),
                 cost_estimate=pl.CostEstimate(flops=dot // 4, bytes_accessed=1 << 20, transcendentals=0),

time: 83.5 us -> 83.4 us (level)
  no operation moved by 1% of the time
where the time goes in v10:
time: 83.4 us; the launch traced here: 83.2 us
  waiting for transfers between devices  46 us (55%)
  Pallas kernels  16.4 us (20%)
  starting transfers between devices  14 us (17%)
  local copies, waits for them, and re-layouts  3.13 us (4%)
  between operations  2.81 us (3%)
  other arithmetic  0.97 us (1%)
    ppermute x9, waiting for transfers between devices, swap(): return lax.ppermute(value, ('grp', 'mem'), pairs)  23.1 us
    ppermute x5, waiting for transfers between devices, turn(): return lax.ppermute(value, 'mem', pairs)  22.8 us
    pallas_call x6, Pallas kernels, call(): kernel_call(kernel, outs, scratch, smem, count, flops, out_spec)(*args)  12.7 us
    ppermute x9, starting transfers between devices, swap(): return lax.ppermute(value, ('grp', 'mem'), pairs)  10.6 us
    pallas_call x2, Pallas kernels, body(): pl.pallas_call(functools.partial(half_gamma_kernel, part * quarter), out_...  3.69 us
    ppermute x5, starting transfers between devices, turn(): return lax.ppermute(value, 'mem', pairs)  3.4 us
    unnamed x12, local copies, waits for them, and re-layouts  2.94 us
  transfers between devices with their start and end apart: 14, of which 8 were waited for; matrix products, arithmetic and copies ran while one was open for 1% of the time, Pallas kernels for 14%

profile of v10, /device:TPU:0, one launch (start us, length us, event | category | flops | bytes accessed | tf_op | source)
XLA Modules:
  0.0 83.2 jit_solution(2586744302605687772)
XLA Ops:
  0.6 0.6 collective-permute-start.2
  1.2 2.1 %collective-permute-start = (bf16[1]{0:T(256)(128)(2,1)}, bf16[1]{0:T(256)(128)(2,1)}, u32[]{:S(2)}, u32[]{:S(2)}) collective-permute-start(bf16[1]{0:T(256)(128)(2,1)} %param.6), channel_id=1, source_target_pairs={{0,1},{1,3},{2,0},{3,2},{4,5},{5,7},{6,4},{7,6},{8,9},{9,11},{10,8... | collective-permute-start | bytes 14 | tf_op jit(solution)/shard_map/ppermute | solution.py:33
  3.3 0.6 collective-permute-start.1
  4.6 0.7 reshape.13
  5.3 22.8 %collective-permute-done = bf16[1]{0:T(256)(128)(2,1)} collective-permute-done((bf16[1]{0:T(256)(128)(2,1)}, bf16[1]{0:T(256)(128)(2,1)}, u32[]{:S(2)}, u32[]{:S(2)}) %collective-permute-start) | collective-permute-done | bytes 34 | tf_op jit(solution)/shard_map/ppermute | solution.py:33
  28.7 0.0 collective-permute-done.1
  29.4 0.0 copy-start
  29.4 1.6 %copy-done = bf16[1,512,2048]{2,1,0:T(8,128)(2,1)S(1)} copy-done((bf16[1,512,2048]{2,1,0:T(8,128)(2,1)S(1)}, bf16[1,512,2048]{2,1,0:T(8,128)(2,1)}, u32[]{:S(2)}) %copy-start) | copy-done | bytes 2097176
  30.9 0.0 copy-start.2
  31.0 0.7 copy-done.2
  31.6 0.7 copy-done.4
  32.3 3.4 %shard_map.68 = (f32[512,512]{1,0:T(8,128)S(1)}, f32[512,512]{1,0:T(8,128)S(1)}, f32[512,512]{1,0:T(8,128)S(1)}, f32[512,2048]{1,0:T(8,128)S(1)}, f32[320,128]{1,0:T(8,128)S(1)}, /*index=5*/f32[160,128]{1,0:T(8,128)S(1)}) custom-call(bf16[512,2048]{1,0:T(8,128)(2,1)S(1)} %bitcast.10, f32[1,512]{1,0:T(1,128)S(1)} %bitcast.21, ...), custom_call_target="tpu_custom_call" | custom-call | flops 2147483648 | bytes 1048576 | tf_op jit(solution)/shard_map/pallas_call | solution.py:209
  35.7 0.0 collective-permute-done.2.r_ref
  35.7 0.0 copy-done.3
  35.7 0.0 copy-start.1
  35.8 2.5 %shard_map.69 = (bf16[512,512]{1,0:T(8,128)(2,1)S(1)}, f32[640,128]{1,0:T(8,128)S(1)}, bf16[640,128]{1,0:T(8,128)(2,1)S(1)}) custom-call(bf16[512,2048]{1,0:T(8,128)(2,1)S(1)} %bitcast.11, bf16[512,2048]{1,0:T(8,128)(2,1)S(1)} %collective-permute-done.2.r_ref, f32[512,512]{1,0:T(8,128)S(1)} %get-tuple-element.15.over_ref, s32[3,1,8]{2,1,0:T(1,128)S(1)} %bitcast.16, ...), custom_call_target="tpu_custom_call" | custom-call | flops 1073741824 | bytes 1048576 | tf_op jit(solution)/shard_map/pallas_call | solution.py:209
  38.2 0.1 collective-permute-start.5
  38.3 1.4 %collective-permute-done.5 = bf16[640,128]{1,0:T(8,128)(2,1)S(1)} collective-permute-done((bf16[640,128]{1,0:T(8,128)(2,1)S(1)}, bf16[640,128]{1,0:T(8,128)(2,1)S(1)}, u32[]{:S(2)}, u32[]{:S(2)}) %collective-permute-start.5) | collective-permute-done | bytes 163872 | tf_op jit(solution)/shard_map/ppermute | solution.py:43
  39.8 2.0 %collective-permute-start.6 = (bf16[320,128]{1,0:T(8,128)(2,1)S(1)}, bf16[320,128]{1,0:T(8,128)(2,1)S(1)}, u32[]{:S(2)}, u32[]{:S(2)}) collective-permute-start(bf16[320,128]{1,0:T(8,128)(2,1)S(1)} %get-tuple-element.26), channel_id=1, source_target_pairs={{0,8},{1,17},{2,18},{3,11},{4,12},{5,21},{6,22},{7,15},{8,0},{9,25... | collective-permute-start | bytes 245768 | tf_op jit(solution)/shard_map/ppermute | solution.py:43
  41.8 0.0 copy-done.1
  41.8 0.1 slice_bitcast_fusion
  41.9 0.1 collective-permute-start.3
  42.0 2.3 %collective-permute-done.6 = bf16[320,128]{1,0:T(8,128)(2,1)S(1)} collective-permute-done((bf16[320,128]{1,0:T(8,128)(2,1)S(1)}, bf16[320,128]{1,0:T(8,128)(2,1)S(1)}, u32[]{:S(2)}, u32[]{:S(2)}) %collective-permute-start.6) | collective-permute-done | bytes 81952 | tf_op jit(solution)/shard_map/ppermute | solution.py:43
  44.4 2.0 %collective-permute-start.7 = (bf16[160,128]{1,0:T(8,128)(2,1)S(1)}, bf16[160,128]{1,0:T(8,128)(2,1)S(1)}, u32[]{:S(2)}, u32[]{:S(2)}) collective-permute-start(bf16[160,128]{1,0:T(8,128)(2,1)S(1)} %get-tuple-element.24), channel_id=1, source_target_pairs={{0,16},{1,9},{2,10},{3,19},{4,20},{5,13},{6,14},{7,23},{8,24},{9,1... | collective-permute-start | bytes 122888 | tf_op jit(solution)/shard_map/ppermute | solution.py:43
  46.4 2.0 %collective-permute-done.7 = bf16[160,128]{1,0:T(8,128)(2,1)S(1)} collective-permute-done((bf16[160,128]{1,0:T(8,128)(2,1)S(1)}, bf16[160,128]{1,0:T(8,128)(2,1)S(1)}, u32[]{:S(2)}, u32[]{:S(2)}) %collective-permute-start.7) | collective-permute-done | bytes 40992 | tf_op jit(solution)/shard_map/ppermute | solution.py:43
  48.4 0.1 collective-permute-start.10
  48.5 3.1 %collective-permute-start.9 = (bf16[160,128]{1,0:T(8,128)(2,1)S(1)}, bf16[160,128]{1,0:T(8,128)(2,1)S(1)}, u32[]{:S(2)}, u32[]{:S(2)}) collective-permute-start(bf16[160,128]{1,0:T(8,128)(2,1)S(1)} %fusion), channel_id=1, source_target_pairs={{0,4},{1,5},{2,6},{3,7},{4,0},{5,1},{6,2},{7,3},{8,12},{9,13},{10,... | collective-permute-start | bytes 122888 | tf_op jit(solution)/shard_map/ppermute | solution.py:43
  51.6 1.1 %collective-permute-start.8 = (bf16[160,128]{1,0:T(8,128)(2,1)S(1)}, bf16[160,128]{1,0:T(8,128)(2,1)S(1)}, u32[]{:S(2)}, u32[]{:S(2)}) collective-permute-start(bf16[160,128]{1,0:T(8,128)(2,1)S(1)} %fusion), channel_id=1, source_target_pairs={{0,7},{1,6},{2,5},{3,4},{4,3},{5,2},{6,1},{7,0},{8,15},{9,14},{10,... | collective-permute-start | bytes 122888 | tf_op jit(solution)/shard_map/ppermute | solution.py:43
  52.8 0.1 collective-permute-start.4
  52.9 9.3 %collective-permute-done.10 = bf16[160,128]{1,0:T(8,128)(2,1)S(1)} collective-permute-done((bf16[160,128]{1,0:T(8,128)(2,1)S(1)}, bf16[160,128]{1,0:T(8,128)(2,1)S(1)}, u32[]{:S(2)}, u32[]{:S(2)}) %collective-permute-start.10) | collective-permute-done | bytes 40992 | tf_op jit(solution)/shard_map/ppermute | solution.py:43
  62.1 0.0 collective-permute-done.9
  62.1 2.6 %collective-permute-done.8 = bf16[160,128]{1,0:T(8,128)(2,1)S(1)} collective-permute-done((bf16[160,128]{1,0:T(8,128)(2,1)S(1)}, bf16[160,128]{1,0:T(8,128)(2,1)S(1)}, u32[]{:S(2)}, u32[]{:S(2)}) %collective-permute-start.8) | collective-permute-done | bytes 40992 | tf_op jit(solution)/shard_map/ppermute | solution.py:43
  64.7 0.6 collective-permute-start.11
  65.3 3.5 %collective-permute-done.11 = bf16[160,128]{1,0:T(8,128)(2,1)S(1)} collective-permute-done((bf16[160,128]{1,0:T(8,128)(2,1)S(1)}, bf16[160,128]{1,0:T(8,128)(2,1)S(1)}, u32[]{:S(2)}, u32[]{:S(2)}) %collective-permute-start.11) | collective-permute-done | bytes 40992 | tf_op jit(solution)/shard_map/ppermute | solution.py:43
  68.8 1.6 %collective-permute-start.12 = (bf16[320,128]{1,0:T(8,128)(2,1)S(1)}, bf16[320,128]{1,0:T(8,128)(2,1)S(1)}, u32[]{:S(2)}, u32[]{:S(2)}) collective-permute-start(bf16[320,128]{1,0:T(8,128)(2,1)S(1)} %pad_maximum_fusion.1), channel_id=1, source_target_pairs={{0,8},{1,17},{2,18},{3,11},{4,12},{5,21},{6,22},{7,15},{8,0},{9,25... | collective-permute-start | bytes 245768 | tf_op jit(solution)/shard_map/ppermute | solution.py:43
  70.4 0.0 collective-permute-done.4.last_ref
  70.4 0.0 collective-permute-done.3.r_ref.first_ref
  70.4 0.8 shard_map.72
  71.2 2.1 %collective-permute-done.12 = bf16[320,128]{1,0:T(8,128)(2,1)S(1)} collective-permute-done((bf16[320,128]{1,0:T(8,128)(2,1)S(1)}, bf16[320,128]{1,0:T(8,128)(2,1)S(1)}, u32[]{:S(2)}, u32[]{:S(2)}) %collective-permute-start.12) | collective-permute-done | bytes 81952 | tf_op jit(solution)/shard_map/ppermute | solution.py:43
  73.4 0.1 collective-permute-start.13
  73.5 0.0 copy-start.5
  73.5 1.8 %shard_map.70.gamma_in = f32[512,2048]{1,0:T(8,128)S(1)} custom-call(s32[3,1,8]{2,1,0:T(1,128)S(1)} %bitcast.17, s32[1,8]{1,0:T(1,128)S(1)} %copy-done.4, f32[512,2048]{1,0:T(8,128)S(1)} %get-tuple-element.14.gamma_in, bf16[512,512]{1,0:T(8,128)(2,1)S(1)} %get-tuple-element.17.mt_ref, bf16[512,2048]{1,0:T(8,128)(2,1)S(1)} %collective-permute-done.2.r_ref), custom_call_target="tpu_custom_call" | custom-call | flops 1073741824 | bytes 1048576 | tf_op jit(solution)/shard_map/pallas_call | solution.py:209
  75.3 0.0 copy-done.5
  75.3 2.0 %shard_map.71.gamma_in = f32[512,2048]{1,0:T(8,128)S(1)} custom-call(s32[3,1,8]{2,1,0:T(1,128)S(1)} %bitcast.18, s32[1,8]{1,0:T(1,128)S(1)} %copy-done.5, bf16[512,2048]{1,0:T(8,128)(2,1)S(1)} %bitcast.13, f32[512,512]{1,0:T(8,128)S(1)} %get-tuple-element.13.over_ref, f32[512,2048]{1,0:T(8,128)S(1)} %shard_map.70.gamma_in, ...), custom_call_target="tpu_custom_call" | custom-call | flops 1073741824 | bytes 1048576 | tf_op jit(solution)/shard_map/pallas_call | solution.py:209
  77.4 1.7 %shard_map.73.refs_0_ = bf16[512,2048]{1,0:T(8,128)(2,1)} custom-call(s32[3,1,8]{2,1,0:T(1,128)S(1)} %bitcast.19, s32[1,8]{1,0:T(1,128)S(1)} %copy-done.5, f32[512,2048]{1,0:T(8,128)S(1)} %shard_map.71.gamma_in, bf16[512,256]{1,0:T(8,128)(2,1)S(1)} %get-tuple-element.18.mt_ref, bf16[256,2048]{1,0:T(8,128)(2,1)S(1)} %get-tuple-element.19.r_ref), custom_call_target="tpu_custom_call" | custom-call | flops 268435456 | bytes 1048576 | tf_op jit(solution)/shard_map/pallas_call | solution.py:303
  79.0 2.0 %shard_map.74 = bf16[512,2048]{1,0:T(8,128)(2,1)} custom-call(s32[3,1,8]{2,1,0:T(1,128)S(1)} %bitcast.20, s32[1,8]{1,0:T(1,128)S(1)} %copy-done.5, f32[512,2048]{1,0:T(8,128)S(1)} %shard_map.71.gamma_in, bf16[512,256]{1,0:T(8,128)(2,1)S(1)} %get-tuple-element.18.mt_ref, ...), custom_call_target="tpu_custom_call", output_to_operand_aliasing={{}: (5, {})} | custom-call | flops 268435456 | bytes 1048576 | tf_op jit(solution)/shard_map/pallas_call | solution.py:303
  81.1 0.0 collective-permute-done.13.other_ref
  81.1 2.1 %shard_map.75 = bf16[512,2048]{1,0:T(8,128)(2,1)} custom-call(bf16[640,128]{1,0:T(8,128)(2,1)S(1)} %pad_maximum_fusion.mine_ref, bf16[640,128]{1,0:T(8,128)(2,1)S(1)} %collective-permute-done.13.other_ref, bf16[512,2048]{1,0:T(8,128)(2,1)S(1)} %bitcast.14), custom_call_target="tpu_custom_call" | custom-call | flops 1073741824 | bytes 1048576 | tf_op jit(solution)/shard_map/pallas_call | solution.py:209
  (13 shorter events, 0.3 us)
Async XLA Ops:
  0.6 35.1 %collective-permute-start.2 = (bf16[512,2048]{1,0:T(8,128)(2,1)}, bf16[512,2048]{1,0:T(8,128)(2,1)S(1)}, u32[]{:S(2)}, u32[]{:S(2)}) collective-permute-start(bf16[512,2048]{1,0:T(8,128)(2,1)} %bitcast.9), channel_id=1, source_target_pairs={{0,1},{1,3},{2,0},{3,2},{4,5},{5,7},{6,4},{7,6},{8,9},{9,11},{10,8... | collective-permute-start | bytes 6291464 | tf_op jit(solution)/shard_map/ppermute | solution.py:33
  1.2 26.9 %collective-permute-start = (bf16[1]{0:T(256)(128)(2,1)}, bf16[1]{0:T(256)(128)(2,1)}, u32[]{:S(2)}, u32[]{:S(2)}) collective-permute-start(bf16[1]{0:T(256)(128)(2,1)} %param.6), channel_id=1, source_target_pairs={{0,1},{1,3},{2,0},{3,2},{4,5},{5,7},{6,4},{7,6},{8,9},{9,11},{10,8... | collective-permute-start | bytes 14 | tf_op jit(solution)/shard_map/ppermute | solution.py:33
  3.3 25.4 %collective-permute-start.1 = (bf16[1]{0:T(256)(128)(2,1)}, bf16[1]{0:T(256)(128)(2,1)}, u32[]{:S(2)}, u32[]{:S(2)}) collective-permute-start(bf16[1]{0:T(256)(128)(2,1)} %param.6), channel_id=1, source_target_pairs={{1,0},{3,1},{0,2},{2,3},{5,4},{7,5},{4,6},{6,7},{9,8},{11,9},{8,10... | collective-permute-start | bytes 14 | tf_op jit(solution)/shard_map/ppermute | solution.py:33
  29.4 1.6 %copy-start = (bf16[1,512,2048]{2,1,0:T(8,128)(2,1)S(1)}, bf16[1,512,2048]{2,1,0:T(8,128)(2,1)}, u32[]{:S(2)}) copy-start(bf16[1,512,2048]{2,1,0:T(8,128)(2,1)} %param.5) | copy-start | bytes 6291460
  30.9 0.7 copy-start.2
  31.6 0.7 copy-start.4
  32.3 3.5 %copy-start.3 = (s32[1,8,3]{1,0,2:T(1,128)S(1)}, s32[1,8,3]{1,0,2:T(1,128)}, u32[]{:S(2)}) copy-start(s32[1,8,3]{1,0,2:T(1,128)} %param.8) | copy-start | bytes 292
  35.7 6.0 %copy-start.1 = (bf16[1,512,2048]{2,1,0:T(8,128)(2,1)S(1)}, bf16[1,512,2048]{2,1,0:T(8,128)(2,1)}, u32[]{:S(2)}) copy-start(bf16[1,512,2048]{2,1,0:T(8,128)(2,1)} %param.5) | copy-start | bytes 6291460
  38.2 1.5 %collective-permute-start.5 = (bf16[640,128]{1,0:T(8,128)(2,1)S(1)}, bf16[640,128]{1,0:T(8,128)(2,1)S(1)}, u32[]{:S(2)}, u32[]{:S(2)}) collective-permute-start(bf16[640,128]{1,0:T(8,128)(2,1)S(1)} %get-tuple-element.23), channel_id=1, source_target_pairs={{0,1},{1,0},{2,3},{3,2},{4,5},{5,4},{6,7},{7,6},{8,9},{9,8},{10,11... | collective-permute-start | bytes 491528 | tf_op jit(solution)/shard_map/ppermute | solution.py:43
  39.8 4.5 %collective-permute-start.6 = (bf16[320,128]{1,0:T(8,128)(2,1)S(1)}, bf16[320,128]{1,0:T(8,128)(2,1)S(1)}, u32[]{:S(2)}, u32[]{:S(2)}) collective-permute-start(bf16[320,128]{1,0:T(8,128)(2,1)S(1)} %get-tuple-element.26), channel_id=1, source_target_pairs={{0,8},{1,17},{2,18},{3,11},{4,12},{5,21},{6,22},{7,15},{8,0},{9,25... | collective-permute-start | bytes 245768 | tf_op jit(solution)/shard_map/ppermute | solution.py:43
  41.9 28.5 %collective-permute-start.3 = (bf16[352,2048]{1,0:T(8,128)(2,1)S(1)}, bf16[352,2048]{1,0:T(8,128)(2,1)S(1)}, u32[]{:S(2)}, u32[]{:S(2)}) collective-permute-start(bf16[352,2048]{1,0:T(8,128)(2,1)S(1)} %slice_bitcast_fusion), channel_id=1, source_target_pairs={{1,0},{3,1},{0,2},{2,3},{5,4},{7,5},{4,6},{6,7},{9,8},{11,9},{8,10... | collective-permute-start | bytes 4325384 | tf_op jit(solution)/shard_map/ppermute | solution.py:33
  44.4 4.1 %collective-permute-start.7 = (bf16[160,128]{1,0:T(8,128)(2,1)S(1)}, bf16[160,128]{1,0:T(8,128)(2,1)S(1)}, u32[]{:S(2)}, u32[]{:S(2)}) collective-permute-start(bf16[160,128]{1,0:T(8,128)(2,1)S(1)} %get-tuple-element.24), channel_id=1, source_target_pairs={{0,16},{1,9},{2,10},{3,19},{4,20},{5,13},{6,14},{7,23},{8,24},{9,1... | collective-permute-start | bytes 122888 | tf_op jit(solution)/shard_map/ppermute | solution.py:43
  48.4 13.7 %collective-permute-start.10 = (bf16[160,128]{1,0:T(8,128)(2,1)S(1)}, bf16[160,128]{1,0:T(8,128)(2,1)S(1)}, u32[]{:S(2)}, u32[]{:S(2)}) collective-permute-start(bf16[160,128]{1,0:T(8,128)(2,1)S(1)} %fusion), channel_id=1, source_target_pairs={{0,3},{1,2},{2,1},{3,0},{4,7},{5,6},{6,5},{7,4},{8,11},{9,10},{10,... | collective-permute-start | bytes 122888 | tf_op jit(solution)/shard_map/ppermute | solution.py:43
  48.5 13.6 %collective-permute-start.9 = (bf16[160,128]{1,0:T(8,128)(2,1)S(1)}, bf16[160,128]{1,0:T(8,128)(2,1)S(1)}, u32[]{:S(2)}, u32[]{:S(2)}) collective-permute-start(bf16[160,128]{1,0:T(8,128)(2,1)S(1)} %fusion), channel_id=1, source_target_pairs={{0,4},{1,5},{2,6},{3,7},{4,0},{5,1},{6,2},{7,3},{8,12},{9,13},{10,... | collective-permute-start | bytes 122888 | tf_op jit(solution)/shard_map/ppermute | solution.py:43
  51.6 13.1 %collective-permute-start.8 = (bf16[160,128]{1,0:T(8,128)(2,1)S(1)}, bf16[160,128]{1,0:T(8,128)(2,1)S(1)}, u32[]{:S(2)}, u32[]{:S(2)}) collective-permute-start(bf16[160,128]{1,0:T(8,128)(2,1)S(1)} %fusion), channel_id=1, source_target_pairs={{0,7},{1,6},{2,5},{3,4},{4,3},{5,2},{6,1},{7,0},{8,15},{9,14},{10,... | collective-permute-start | bytes 122888 | tf_op jit(solution)/shard_map/ppermute | solution.py:43
  52.8 17.6 %collective-permute-start.4 = (bf16[160,2048]{1,0:T(8,128)(2,1)S(1)}, bf16[160,2048]{1,0:T(8,128)(2,1)S(1)}, u32[]{:S(2)}, u32[]{:S(2)}) collective-permute-start(bf16[160,2048]{1,0:T(8,128)(2,1)S(1)} %slice_bitcast_fusion.1), channel_id=1, source_target_pairs={{1,0},{3,1},{0,2},{2,3},{5,4},{7,5},{4,6},{6,7},{9,8},{11,9},{8,10... | collective-permute-start | bytes 1966088 | tf_op jit(solution)/shard_map/ppermute | solution.py:33
  64.7 4.1 %collective-permute-start.11 = (bf16[160,128]{1,0:T(8,128)(2,1)S(1)}, bf16[160,128]{1,0:T(8,128)(2,1)S(1)}, u32[]{:S(2)}, u32[]{:S(2)}) collective-permute-start(bf16[160,128]{1,0:T(8,128)(2,1)S(1)} %multiply_convert_fusion), channel_id=1, source_target_pairs={{0,16},{1,9},{2,10},{3,19},{4,20},{5,13},{6,14},{7,23},{8,24},{9,1... | collective-permute-start | bytes 122888 | tf_op jit(solution)/shard_map/ppermute | solution.py:43
  68.8 4.5 %collective-permute-start.12 = (bf16[320,128]{1,0:T(8,128)(2,1)S(1)}, bf16[320,128]{1,0:T(8,128)(2,1)S(1)}, u32[]{:S(2)}, u32[]{:S(2)}) collective-permute-start(bf16[320,128]{1,0:T(8,128)(2,1)S(1)} %pad_maximum_fusion.1), channel_id=1, source_target_pairs={{0,8},{1,17},{2,18},{3,11},{4,12},{5,21},{6,22},{7,15},{8,0},{9,25... | collective-permute-start | bytes 245768 | tf_op jit(solution)/shard_map/ppermute | solution.py:43
  73.4 7.7 %collective-permute-start.13 = (bf16[640,128]{1,0:T(8,128)(2,1)S(1)}, bf16[640,128]{1,0:T(8,128)(2,1)S(1)}, u32[]{:S(2)}, u32[]{:S(2)}) collective-permute-start(bf16[640,128]{1,0:T(8,128)(2,1)S(1)} %pad_maximum_fusion.mine_ref), channel_id=1, source_target_pairs={{0,1},{1,0},{2,3},{3,2},{4,5},{5,4},{6,7},{7,6},{8,9},{9,8},{10,11... | collective-permute-start | bytes 491528 | tf_op jit(solution)/shard_map/ppermute | solution.py:43
  73.5 1.8 %copy-start.5 = (s32[1,8]{1,0:T(1,128)S(1)}, s32[1,8]{1,0:T(1,128)}, u32[]{:S(2)}) copy-start(s32[1,8]{1,0:T(1,128)} %counts.11) | copy-start | bytes 100
